TPU v7x, 32 devices: a whole 2x2x4 slice. The times are simulated.
32 devices in a mesh: fsdp: 4 (over z), ctx: 2 (over y), tp: 4 (over x, core).
Axes of the slice: x: 2, y: 2, z: 4, core: 2. Of those that a mesh axis runs over, the one named last changes fastest.
Arguments:
- tokens: bfloat16 [4, 768, 1024], P('fsdp', 'ctx'), may hold values from -16 to 16
- cotangent: bfloat16 [4, 768, 1024], P('fsdp', 'ctx'), may hold values from -6 to 6
- positions: int32 [4, 768], P('fsdp', 'ctx'), may hold values from 0 to 767, as said below
- routes: int32 [4, 768, 8], P('fsdp', 'ctx'), may hold values from 0 to 31, all different within a row; in each aligned block of 384 rows (0 to 383, 384 to 767, ..., all dimensions but the last counted through in order) at most 192 rows name the same one
- attn_gain: bfloat16 [1024], P('fsdp'), may hold values from 0.5 to 1.5
- w_query: bfloat16 [1024, 1024], P('fsdp', 'tp'), may hold values from -0.1875 to 0.1875
- key_value_projection: bfloat16 [1024, 8, 2, 64], P('fsdp', 'tp'), may hold values from -0.1875 to 0.1875
- output_projection_weight: bfloat16 [1024, 1024], P('tp', 'fsdp'), may hold values from -0.75 to 0.75
- ffn_gain: bfloat16 [1024], P('fsdp'), may hold values from 0.5 to 1.5
- w_router: bfloat16 [1024, 32], P('fsdp'), may hold values from -0.1875 to 0.1875
- w_gate: bfloat16 [32, 1024, 512], P('tp', 'fsdp'), may hold values from -0.1875 to 0.1875
- w_up: bfloat16 [32, 1024, 512], P('tp', 'fsdp'), may hold values from -0.1875 to 0.1875
- w_down: bfloat16 [32, 1024, 512], P('tp', 'fsdp'), may hold values from -0.75 to 0.75
Outputs:
- out: bfloat16 [4, 768, 1024], P('fsdp', 'ctx')
- d_tokens: float32 [4, 768, 1024], P('fsdp', 'ctx')
- d_attn_gain: float32 [1024], P('fsdp')
- d_query: float32 [1024, 1024], P('fsdp', 'tp')
- d_keyval: float32 [1024, 8, 2, 64], P('fsdp', 'tp')
- d_out: float32 [1024, 1024], P('tp', 'fsdp')
- d_ffn_gain: float32 [1024], P('fsdp')
- d_router: float32 [1024, 32], P('fsdp')
- d_gate: float32 [32, 1024, 512], P('tp', 'fsdp')
- d_up: float32 [32, 1024, 512], P('tp', 'fsdp')
- d_down: float32 [32, 1024, 512], P('tp', 'fsdp')
Inputs may be any that keep to these rules, and one draw needn't show every extreme that they name: positions[s, i] is 0 at the first token of a document and one more than positions[s, i - 1] otherwise; every sequence begins a document at its first token; the first sequence is one whole document. `routes`: each row names 8 different experts; in the rows of one device (aligned blocks of 384 rows) no expert is named by more than 192 rows, a bound that some block reaches.
All inputs are finite; a program needn't handle non-finite values.
Results may differ from a plain program's by a relative error of at most 0.02.
Values may be sent and summed in bfloat16 or wider, within the bound.
No kernel may reach another device: no remote copies, remote signals or barrier semaphores. Data moves between devices by JAX's collectives and lax.ppermute only.
A program may use at most 192 MiB of HBM per device.

v0:
```python
import math

import jax
import jax.numpy as jnp
from jax import lax
from jax.sharding import PartitionSpec as P

QUERY_HEADS = 16
KEY_VALUE_HEADS = 8
HEAD_SIZE = 64


EPS = 1e-06
THETA = 10000.0


def shifted(block, axis, distance):
    devices = range(lax.axis_size(axis))
    route = [(i - distance, i) for i in devices if i - distance in devices]
    return lax.ppermute(block, axis, route)


def rope_tables(place_rows, head_width):
    half_width = head_width // 2
    inverse = THETA ** (-2.0 * jnp.arange(half_width, dtype=jnp.float32) / head_width)
    angle = place_rows.astype(jnp.float32)[:, None] * inverse[None, :]
    return (jnp.cos(angle)[:, None, :], jnp.sin(angle)[:, None, :])


def apply_rotary(vector, cosine_lookup, sine_lookup, direction):
    half_width = vector.shape[-1] // 2
    first_half = vector[..., :half_width]
    second_half = vector[..., half_width:]
    return jnp.concatenate(
        [
            first_half * cosine_lookup - direction * second_half * sine_lookup,
            direction * first_half * sine_lookup + second_half * cosine_lookup,
        ],
        axis=-1,
    )


def rms_forward(wide_rows, gain_vector):
    factor = lax.rsqrt(jnp.mean(wide_rows * wide_rows, axis=-1, keepdims=True) + EPS)
    normed = wide_rows * factor
    return (normed, factor, (normed * gain_vector.astype(jnp.float32)).astype(jnp.bfloat16))


def rms_backward(gradient, normed, factor, gain_vector):
    gain_grad = jnp.sum(gradient * normed, axis=0)
    inner_term = gradient * gain_vector.astype(jnp.float32)
    back_term = factor * (
        inner_term - normed * jnp.mean(inner_term * normed, axis=-1, keepdims=True)
    )
    return (back_term, gain_grad)


def attend_mask(query_ids, query_starts, key_ids):
    return (key_ids[None, :] <= query_ids[:, None]) & (key_ids[None, :] >= query_starts[:, None])


def router_gates(logits, picks):
    selected = jnp.sum(jnp.where(picks, logits[:, None, :], 0.0), axis=-1)
    exp_sel = jnp.exp(selected)
    return exp_sel / jnp.sum(exp_sel, axis=-1, keepdims=True)


def slot_tables(route_rows, gate_weights, first_expert, expert_count, capacity):
    token_count = route_rows.shape[0]
    owners = first_expert + jnp.arange(expert_count, dtype=jnp.int32)
    hit_mask = route_rows[:, :, None] == owners[None, None, :]
    member = jnp.sum(hit_mask.astype(jnp.int32), axis=1)
    weight_rows = jnp.sum(jnp.where(hit_mask, gate_weights[:, :, None], 0.0), axis=1)
    places = jnp.cumsum(member, axis=0) - 1
    expert_ids = jnp.arange(expert_count, dtype=jnp.int32)
    slot_ids = jnp.where(
        member > 0, expert_ids[None, :] * capacity + places, expert_count * capacity
    )
    flat_slots = slot_ids.reshape(-1)
    token_ids = jnp.broadcast_to(
        jnp.arange(token_count, dtype=jnp.int32)[:, None], (token_count, expert_count)
    ).reshape(-1)
    source = jnp.zeros((expert_count * capacity + 1,), jnp.int32).at[flat_slots].set(token_ids)[:-1]
    scaled = (
        jnp.zeros((expert_count * capacity + 1,), jnp.float32)
        .at[flat_slots]
        .set(weight_rows.reshape(-1))[:-1]
    )
    return (hit_mask, slot_ids, source, scaled)


def expert_forward(hidden, source, w_gate, w_up, w_down, expert_count, capacity):
    picked = hidden[source].reshape(expert_count, capacity, hidden.shape[1])
    gate_pre = jnp.einsum("ecd,edf->ecf", picked, w_gate, preferred_element_type=jnp.float32)
    up_pre = jnp.einsum("ecd,edf->ecf", picked, w_up, preferred_element_type=jnp.float32)
    activation = (jax.nn.silu(gate_pre) * up_pre).astype(jnp.bfloat16)
    result = jnp.einsum("ecf,edf->ecd", activation, w_down, preferred_element_type=jnp.float32)
    return (picked, gate_pre, up_pre, activation, result)


def combine(result, source, scaled, token_count):
    model_width = result.shape[-1]
    flat_result = result.reshape(-1, model_width)
    return (
        jnp.zeros((token_count, model_width), jnp.float32)
        .at[source]
        .add(flat_result * scaled[:, None])
    )


def expert_backward(
    grad_rows,
    hit_mask,
    slot_ids,
    source,
    scaled,
    saved,
    w_gate,
    w_up,
    w_down,
    expert_count,
    capacity,
    token_count,
):
    picked, gate_pre, up_pre, activation, result = saved
    model_width = grad_rows.shape[1]
    slot_grad = jnp.sum(grad_rows * result.reshape(expert_count * capacity, model_width), axis=1)
    padded = jnp.concatenate([slot_grad, jnp.zeros((1,), jnp.float32)])
    per_expert = padded[slot_ids]
    gate_grad = jnp.sum(jnp.where(hit_mask, per_expert[:, None, :], 0.0), axis=2)
    out_grad = (
        (grad_rows * scaled[:, None])
        .astype(jnp.bfloat16)
        .reshape(expert_count, capacity, model_width)
    )
    grad_down = jnp.einsum("ecd,ecf->edf", out_grad, activation, preferred_element_type=jnp.float32)
    act_grad = jnp.einsum("ecd,edf->ecf", out_grad, w_down, preferred_element_type=jnp.float32)
    sigmoid_gate = jax.nn.sigmoid(gate_pre)
    gate_pre_grad = (
        act_grad * up_pre * sigmoid_gate * (1.0 + gate_pre * (1.0 - sigmoid_gate))
    ).astype(jnp.bfloat16)
    up_pre_grad = (act_grad * gate_pre * sigmoid_gate).astype(jnp.bfloat16)
    grad_gate = jnp.einsum(
        "ecd,ecf->edf", picked, gate_pre_grad, preferred_element_type=jnp.float32
    )
    grad_up = jnp.einsum("ecd,ecf->edf", picked, up_pre_grad, preferred_element_type=jnp.float32)
    picked_grad = jnp.einsum(
        "ecf,edf->ecd", gate_pre_grad, w_gate, preferred_element_type=jnp.float32
    ) + jnp.einsum("ecf,edf->ecd", up_pre_grad, w_up, preferred_element_type=jnp.float32)
    hidden_grad = (
        jnp.zeros((token_count, model_width), jnp.float32)
        .at[source]
        .add(picked_grad.reshape(-1, model_width))
    )
    return (gate_grad, hidden_grad, grad_gate, grad_up, grad_down)


def local(
    tokens,
    cotangent,
    positions,
    routes,
    attn_gain,
    w_query,
    key_value_projection,
    output_projection_weight,
    ffn_gain,
    w_router,
    w_gate,
    w_up,
    w_down,
):
    gain_one, gain_two, query_full, keyval_full, out_full, router_full = (
        lax.all_gather(attn_gain, "fsdp", axis=0, tiled=True),
        lax.all_gather(ffn_gain, "fsdp", axis=0, tiled=True),
        lax.all_gather(w_query, "fsdp", axis=0, tiled=True),
        lax.all_gather(key_value_projection, "fsdp", axis=0, tiled=True),
        lax.all_gather(output_projection_weight, "fsdp", axis=1, tiled=True),
        lax.all_gather(w_router, "fsdp", axis=0, tiled=True),
    )
    expert_full = (
        lax.all_gather(w_gate, "fsdp", axis=1, tiled=True),
        lax.all_gather(w_up, "fsdp", axis=1, tiled=True),
        lax.all_gather(w_down, "fsdp", axis=1, tiled=True),
    )
    input_rows = tokens[0]
    local_len = input_rows.shape[0]
    model_width = input_rows.shape[1]
    query_group_count = QUERY_HEADS // KEY_VALUE_HEADS
    local_heads = w_query.shape[1] // HEAD_SIZE
    local_kv = local_heads // query_group_count
    expert_count = w_gate.shape[0]
    capacity = local_len // 2
    ctx_count = lax.axis_size("ctx")
    ctx_rank = lax.axis_index("ctx")
    factor = 1.0 / math.sqrt(HEAD_SIZE)
    key_value_weight = keyval_full.reshape(model_width, local_kv * 2 * HEAD_SIZE)
    wide_input = input_rows.astype(jnp.float32)
    normed_one, factor_one, first_hidden_state = rms_forward(wide_input, gain_one)
    query_matrix = jnp.dot(
        first_hidden_state, query_full, preferred_element_type=jnp.float32
    ).reshape(local_len, local_heads, HEAD_SIZE)
    key_value_rows = jnp.dot(
        first_hidden_state, key_value_weight, preferred_element_type=jnp.float32
    ).reshape(local_len, local_kv, 2, HEAD_SIZE)
    place_rows = positions[0]
    cosine_lookup, sine_lookup = rope_tables(place_rows, HEAD_SIZE)
    rotated_query = (
        apply_rotary(query_matrix, cosine_lookup, sine_lookup, 1.0)
        .astype(jnp.bfloat16)
        .reshape(local_len, local_kv, query_group_count, HEAD_SIZE)
    )
    k_rot = apply_rotary(key_value_rows[:, :, 0], cosine_lookup, sine_lookup, 1.0).astype(
        jnp.bfloat16
    )
    v_rows = key_value_rows[:, :, 1].astype(jnp.bfloat16)
    local_ids = jnp.arange(local_len, dtype=jnp.int32)
    query_ids = ctx_rank * local_len + local_ids
    query_starts = query_ids - place_rows
    kv_pack = jnp.concatenate([k_rot, v_rows], axis=-1)
    kv_blocks = [kv_pack]
    key_ids = [query_ids]
    travelling = kv_pack
    cycle_step = 1
    travelling = shifted(travelling, "ctx", 1)
    kv_blocks.append(travelling)
    key_ids.append((ctx_rank - cycle_step) * local_len + local_ids)
    row_total = jnp.zeros((local_kv, query_group_count, local_len), jnp.float32)
    weighted = jnp.zeros((local_kv, query_group_count, local_len, HEAD_SIZE), jnp.float32)
    masks = []
    for block_index in range(ctx_count):
        allowed = attend_mask(query_ids, query_starts, key_ids[block_index])
        masks.append(allowed)
        key_rows = kv_blocks[block_index][..., :HEAD_SIZE]
        value_rows = kv_blocks[block_index][..., HEAD_SIZE:]
        scores = (
            jnp.einsum(
                "tkgd,skd->kgts", rotated_query, key_rows, preferred_element_type=jnp.float32
            )
            * factor
        )
        exp_scores = jnp.where(allowed[None, None], jnp.exp(scores), 0.0)
        row_total = row_total + jnp.sum(exp_scores, axis=-1)
        weighted = weighted + jnp.einsum(
            "kgts,skd->kgtd",
            exp_scores.astype(jnp.bfloat16),
            value_rows,
            preferred_element_type=jnp.float32,
        )
    head_out = (weighted / row_total[..., None]).astype(jnp.bfloat16)
    flat_heads = head_out.transpose(2, 0, 1, 3).reshape(local_len, local_heads * HEAD_SIZE)
    attn_part = jnp.dot(flat_heads, out_full, preferred_element_type=jnp.float32)
    residual = wide_input + lax.psum(attn_part, "tp")
    normed_two, factor_two, hidden_two = rms_forward(residual, gain_two)
    logits = jnp.dot(hidden_two, router_full, preferred_element_type=jnp.float32)
    route_rows = routes[0]
    picks = (
        route_rows[:, :, None] == jnp.arange(router_full.shape[1], dtype=jnp.int32)[None, None, :]
    )
    gate_weights = router_gates(logits, picks)
    first_expert = lax.axis_index("tp") * expert_count
    hit_mask, slot_ids, source, scaled = slot_tables(
        route_rows, gate_weights, first_expert, expert_count, capacity
    )
    saved = expert_forward(
        hidden_two, source, expert_full[0], expert_full[1], expert_full[2], expert_count, capacity
    )
    mixture_part = combine(saved[4], source, scaled, local_len)
    mixture = lax.psum(mixture_part.astype(jnp.bfloat16), "tp").astype(jnp.float32)
    out_rows = (residual + mixture).astype(jnp.bfloat16)
    grad_wide = cotangent[0].astype(jnp.float32)
    back_weights = (
        lax.all_gather(w_gate, "fsdp", axis=1, tiled=True),
        lax.all_gather(w_up, "fsdp", axis=1, tiled=True),
        lax.all_gather(w_down, "fsdp", axis=1, tiled=True),
    )
    grad_rows = grad_wide[source]
    gate_grad_part, hidden_grad_part, grad_gate, grad_up, grad_down = expert_backward(
        grad_rows,
        hit_mask,
        slot_ids,
        source,
        scaled,
        saved,
        back_weights[0],
        back_weights[1],
        back_weights[2],
        expert_count,
        capacity,
        local_len,
    )
    hidden_grad_sum, gate_grad = lax.psum((hidden_grad_part, gate_grad_part), "tp")
    sel_grad = gate_weights * (
        gate_grad - jnp.sum(gate_weights * gate_grad, axis=-1, keepdims=True)
    )
    logit_grad = jnp.sum(jnp.where(picks, sel_grad[:, :, None], 0.0), axis=1).astype(jnp.bfloat16)
    grad_router = jnp.einsum(
        "td,te->de", hidden_two, logit_grad, preferred_element_type=jnp.float32
    )
    hidden_grad = hidden_grad_sum + jnp.einsum(
        "te,de->td", logit_grad, router_full, preferred_element_type=jnp.float32
    )
    back_two, grad_ffn_gain = rms_backward(hidden_grad, normed_two, factor_two, gain_two)
    residual_grad = grad_wide + back_two
    residual_gradient_second = residual_grad.astype(jnp.bfloat16)
    grad_out_proj = jnp.einsum(
        "ti,td->id", flat_heads, residual_gradient_second, preferred_element_type=jnp.float32
    )
    per_head_gradient = jnp.einsum(
        "td,id->ti", residual_gradient_second, out_full, preferred_element_type=jnp.float32
    ).astype(jnp.bfloat16)
    per_head_gradient = per_head_gradient.reshape(
        local_len, local_kv, query_group_count, HEAD_SIZE
    ).transpose(1, 2, 0, 3)
    row_delta = jnp.sum(
        per_head_gradient.astype(jnp.float32) * head_out.astype(jnp.float32), axis=-1
    )
    log_total = jnp.log(row_total)
    query_grad = jnp.zeros((local_len, local_kv, query_group_count, HEAD_SIZE), jnp.float32)
    kv_grads = []
    for block_index in range(ctx_count):
        key_rows = kv_blocks[block_index][..., :HEAD_SIZE]
        value_rows = kv_blocks[block_index][..., HEAD_SIZE:]
        scores = (
            jnp.einsum(
                "tkgd,skd->kgts", rotated_query, key_rows, preferred_element_type=jnp.float32
            )
            * factor
        )
        probability = jnp.where(
            masks[block_index][None, None], jnp.exp(scores - log_total[..., None]), 0.0
        )
        prob_grad = jnp.einsum(
            "kgtd,skd->kgts", per_head_gradient, value_rows, preferred_element_type=jnp.float32
        )
        score_grad = (probability * (prob_grad - row_delta[..., None]) * factor).astype(
            jnp.bfloat16
        )
        query_grad = query_grad + jnp.einsum(
            "kgts,skd->tkgd", score_grad, key_rows, preferred_element_type=jnp.float32
        )
        key_grad = jnp.einsum(
            "kgts,tkgd->skd", score_grad, rotated_query, preferred_element_type=jnp.float32
        )
        value_gradient = jnp.einsum(
            "kgts,kgtd->skd",
            probability.astype(jnp.bfloat16),
            per_head_gradient,
            preferred_element_type=jnp.float32,
        )
        kv_grads.append(jnp.concatenate([key_grad, value_gradient], axis=-1))
    cycle_step = 1
    returning = shifted(kv_grads[cycle_step].astype(jnp.bfloat16), "ctx", -1).astype(jnp.float32)
    kv_grad_total = kv_grads[0] + returning
    key_backward_rows = apply_rotary(
        kv_grad_total[..., :HEAD_SIZE], cosine_lookup, sine_lookup, -1.0
    )
    key_value_backward = (
        jnp.stack([key_backward_rows, kv_grad_total[..., HEAD_SIZE:]], axis=2)
        .astype(jnp.bfloat16)
        .reshape(local_len, local_kv * 2 * HEAD_SIZE)
    )
    query_back = (
        apply_rotary(
            query_grad.reshape(local_len, local_heads, HEAD_SIZE), cosine_lookup, sine_lookup, -1.0
        )
        .astype(jnp.bfloat16)
        .reshape(local_len, local_heads * HEAD_SIZE)
    )
    grad_query = jnp.einsum(
        "td,tf->df", first_hidden_state, query_back, preferred_element_type=jnp.float32
    )
    key_value_gradient = jnp.einsum(
        "td,tf->df", first_hidden_state, key_value_backward, preferred_element_type=jnp.float32
    ).reshape(model_width, local_kv, 2, HEAD_SIZE)
    hidden_one_part = jnp.einsum(
        "tf,df->td", query_back, query_full, preferred_element_type=jnp.float32
    ) + jnp.einsum(
        "tf,df->td", key_value_backward, key_value_weight, preferred_element_type=jnp.float32
    )
    hidden_one_grad = lax.psum(hidden_one_part.astype(jnp.bfloat16), "tp").astype(jnp.float32)
    back_one, grad_attn_gain = rms_backward(hidden_one_grad, normed_one, factor_one, gain_one)
    input_grad = residual_grad + back_one
    shards = (
        lax.psum_scatter(
            grad_attn_gain.astype(jnp.bfloat16), "fsdp", scatter_dimension=0, tiled=True
        ).astype(jnp.float32),
        lax.psum_scatter(
            grad_ffn_gain.astype(jnp.bfloat16), "fsdp", scatter_dimension=0, tiled=True
        ).astype(jnp.float32),
        lax.psum_scatter(
            grad_query.astype(jnp.bfloat16), "fsdp", scatter_dimension=0, tiled=True
        ).astype(jnp.float32),
        lax.psum_scatter(
            key_value_gradient.astype(jnp.bfloat16), "fsdp", scatter_dimension=0, tiled=True
        ).astype(jnp.float32),
        lax.psum_scatter(
            grad_out_proj.astype(jnp.bfloat16), "fsdp", scatter_dimension=1, tiled=True
        ).astype(jnp.float32),
        lax.psum_scatter(
            grad_router.astype(jnp.bfloat16), "fsdp", scatter_dimension=0, tiled=True
        ).astype(jnp.float32),
    )
    piece_gate, piece_up, piece_down = (
        lax.psum_scatter(
            grad_gate.astype(jnp.bfloat16), ("fsdp", "ctx"), scatter_dimension=1, tiled=True
        ).astype(jnp.float32),
        lax.psum_scatter(
            grad_up.astype(jnp.bfloat16), ("fsdp", "ctx"), scatter_dimension=1, tiled=True
        ).astype(jnp.float32),
        lax.psum_scatter(
            grad_down.astype(jnp.bfloat16), ("fsdp", "ctx"), scatter_dimension=1, tiled=True
        ).astype(jnp.float32),
    )
    expert_totals = (
        lax.all_gather(piece_gate.astype(jnp.bfloat16), "ctx", axis=1, tiled=True).astype(
            piece_gate.dtype
        ),
        lax.all_gather(piece_up.astype(jnp.bfloat16), "ctx", axis=1, tiled=True).astype(
            piece_up.dtype
        ),
        lax.all_gather(piece_down.astype(jnp.bfloat16), "ctx", axis=1, tiled=True).astype(
            piece_down.dtype
        ),
    )
    small_totals = (
        lax.psum(shards[0].astype(jnp.bfloat16), "ctx").astype(jnp.float32),
        lax.psum(shards[1].astype(jnp.bfloat16), "ctx").astype(jnp.float32),
        lax.psum(shards[2].astype(jnp.bfloat16), "ctx").astype(jnp.float32),
        lax.psum(shards[3].astype(jnp.bfloat16), "ctx").astype(jnp.float32),
        lax.psum(shards[4].astype(jnp.bfloat16), "ctx").astype(jnp.float32),
        lax.psum(shards[5].astype(jnp.bfloat16), "ctx").astype(jnp.float32),
    )
    return (
        out_rows[None],
        input_grad[None],
        small_totals[0],
        small_totals[2],
        small_totals[3],
        small_totals[4],
        small_totals[1],
        small_totals[5],
        expert_totals[0],
        expert_totals[1],
        expert_totals[2],
    )


def solution(mesh):
    return jax.shard_map(
        local,
        mesh=mesh,
        in_specs=(
            P("fsdp", "ctx", None),
            P("fsdp", "ctx", None),
            P("fsdp", "ctx"),
            P("fsdp", "ctx", None),
            P("fsdp"),
            P("fsdp", "tp"),
            P("fsdp", "tp", None, None),
            P("tp", "fsdp"),
            P("fsdp"),
            P("fsdp", None),
            P("tp", "fsdp", None),
            P("tp", "fsdp", None),
            P("tp", "fsdp", None),
        ),
        out_specs=(
            P("fsdp", "ctx", None),
            P("fsdp", "ctx", None),
            P("fsdp"),
            P("fsdp", "tp"),
            P("fsdp", "tp", None, None),
            P("tp", "fsdp"),
            P("fsdp"),
            P("fsdp", None),
            P("tp", "fsdp", None),
            P("tp", "fsdp", None),
            P("tp", "fsdp", None),
        ),
        check_vma=False,
    )
```

profile of v0, /device:TPU:0, one launch (start us, length us, event | category | flops | bytes accessed | tf_op | source)
XLA Modules:
  0.0 1283.9 jit_solution(13563191291546895260)
XLA Ops:
  10.1 12.8 all-gather
  22.9 15.0 %all_gather.40 = bf16[1024,2,2,64]{0,3,2,1:T(8,128)(2,1)S(1)} all-gather(bf16[256,2,2,64]{0,3,2,1:T(8,128)(2,1)} %param.19), channel_id=1, replica_groups=mesh['fsdp'=4,'ctx'=2,'tp'=4] {'fsdp'}, dimensions={0}, use_global_device_ids=true | all-gather | bytes 655360 | tf_op jit(solution)/shard_map/all_gather | solution.py:177
  45.6 15.6 %all_gather.41 = bf16[1024,256]{1,0:T(8,128)(2,1)S(1)} all-gather(bf16[256,256]{1,0:T(8,128)(2,1)S(1)} %copy-done.46), channel_id=1, replica_groups=mesh['fsdp'=4,'ctx'=2,'tp'=4] {'fsdp'}, dimensions={0}, use_global_device_ids=true | all-gather | bytes 655360 | tf_op jit(solution)/shard_map/all_gather | solution.py:176
  64.2 14.6 %all_gather.42 = bf16[256,1024]{1,0:T(8,128)(2,1)S(1)} all-gather(bf16[256,256]{1,0:T(8,128)(2,1)S(1)} %copy-done.47), channel_id=1, replica_groups=mesh['fsdp'=4,'ctx'=2,'tp'=4] {'fsdp'}, dimensions={1}, use_global_device_ids=true | all-gather | bytes 655360 | tf_op jit(solution)/shard_map/all_gather | solution.py:178
  98.1 11.8 scatter_custom_fusion
  115.9 20.6 %all_gather.47 = bf16[1024,32]{0,1:T(8,128)(2,1)S(1)} all-gather(bf16[256,32]{0,1:T(8,128)(2,1)S(1)} %copy-done.51), channel_id=1, replica_groups=mesh['fsdp'=4,'ctx'=2,'tp'=4] {'fsdp'}, dimensions={0}, use_global_device_ids=true | all-gather | bytes 81920 | tf_op jit(solution)/shard_map/all_gather | solution.py:179
  144.7 91.1 %all-gather.9.cloned.1.call-done = bf16[8,1024,512]{2,1,0:T(8,128)(2,1)} async-done(((bf16[8,256,512]{2,1,0:T(8,128)(2,1)}), bf16[8,1024,512]{2,1,0:T(8,128)(2,1)}) %all-gather.9.cloned.1.call-update) | async-done | bytes 8388624 | tf_op jit(solution)/shard_map/all_gather | solution.py:182
  243.6 141.4 %all-gather.11.cloned.1.call-done = bf16[8,1024,512]{2,1,0:T(8,128)(2,1)} async-done(((bf16[8,256,512]{2,1,0:T(8,128)(2,1)}), bf16[8,1024,512]{2,1,0:T(8,128)(2,1)}) %all-gather.11.cloned.1.call-update) | async-done | bytes 8388624 | tf_op jit(solution)/shard_map/all_gather | solution.py:183
  385.0 9.4 multiply_convert_fusion.3
  394.4 139.7 %all-gather.13.cloned.1.call-done = bf16[8,1024,512]{2,1,0:T(8,128)(2,1)} async-done(((bf16[8,256,512]{2,1,0:T(8,128)(2,1)}), bf16[8,1024,512]{2,1,0:T(8,128)(2,1)}) %all-gather.13.cloned.1.call-update) | async-done | bytes 8388624 | tf_op jit(solution)/shard_map/all_gather | solution.py:184
  534.1 11.2 multiply_reduce_fusion
  545.4 17.4 %gather_fusion.2 = f32[3072]{0:T(1024)S(1)} fusion(f32[1537]{0:T(1024)S(1)} %pad_maximum_fusion.3, s32[3072]{0:T(1024)S(1)} %broadcast_clamp_fusion), kind=kCustom, calls=%fused_computation.2 | custom fusion | bytes 36864 | tf_op jit(solution)/shard_map/gather | solution.py:129
  566.6 12.2 scatter_custom_fusion.1
  578.9 9.6 multiply_convert_fusion.1
  604.9 15.8 %scatter_custom_fusion.3 = f32[384,1024]{1,0:T(8,128)} fusion(s32[1536]{0:T(1024)S(1)} %compare_select_fusion.4, f32[1536,1024]{1,0:T(8,128)} %bitcast.272, f32[]{:T(128)} %constant.22.clone.1), kind=kCustom, calls=%fused_computation.98 | custom fusion | flops 1572864 | bytes 1573376 | tf_op jit(solution)/shard_map/scatter-add | solution.py:153
  620.8 12.8 psum.80
  633.8 28.3 %all-reduce.13.cloned.1.call-done = f32[384,1024]{1,0:T(8,128)} async-done(((f32[384,1024]{1,0:T(8,128)}), f32[384,1024]{1,0:T(8,128)}) %all-reduce.13.cloned.1.call-update) | async-done | bytes 1572880 | tf_op jit(solution)/shard_map/psum | solution.py:292
  688.0 9.0 convolution_convert_fusion
  719.6 15.9 %scatter_custom_fusion.2 = f32[384,1024]{1,0:T(8,128)} fusion(s32[1536]{0:T(1024)} %copy-done.50, f32[1536,1024]{1,0:T(8,128)} %bitcast_multiply_fusion, f32[]{:T(128)} %constant.22.clone.1), kind=kCustom, calls=%fused_computation.100 | custom fusion | flops 1572864 | bytes 1573376 | tf_op jit(solution)/shard_map/scatter-add | solution.py:107
  746.5 149.2 %reduce-scatter.20.cloned.1.call-done = bf16[8,128,512]{2,1,0:T(8,128)(2,1)} async-done(((bf16[8,1024,512]{2,1,0:T(8,128)(2,1)}), bf16[8,128,512]{2,1,0:T(8,128)(2,1)}) %reduce-scatter.20.cloned.1.call-update) | async-done | bytes 1048592 | tf_op jit(solution)/shard_map/reduce_scatter | solution.py:411
  895.8 163.3 %reduce-scatter.18.cloned.1.call-done = bf16[8,128,512]{2,1,0:T(8,128)(2,1)} async-done(((bf16[8,1024,512]{2,1,0:T(8,128)(2,1)}), bf16[8,128,512]{2,1,0:T(8,128)(2,1)}) %reduce-scatter.18.cloned.1.call-update) | async-done | bytes 1048592 | tf_op jit(solution)/shard_map/reduce_scatter | solution.py:408
  1059.1 163.3 %reduce-scatter.16.cloned.1.call-done = bf16[8,128,512]{2,1,0:T(8,128)(2,1)} async-done(((bf16[8,1024,512]{2,1,0:T(8,128)(2,1)}), bf16[8,128,512]{2,1,0:T(8,128)(2,1)}) %reduce-scatter.16.cloned.1.call-update) | async-done | bytes 1048592 | tf_op jit(solution)/shard_map/reduce_scatter | solution.py:405
  1225.9 10.1 all-reduce.3
  1243.6 9.6 all-reduce.4
  (283 shorter events, 166.5 us)
Async XLA Ops:
  8.0 128.5 %all-reduce.11.cloned.1.call-start = ((), (), s32[]{:S(2)}) async-start(), calls=%async_computation.7 | async-start | bytes 3145728 | tf_op jit(solution)/shard_map/psum | solution.py:253
  41.5 37.4 %collective-permute-start = (bf16[384,2,128]{0,2,1:T(8,128)(2,1)}, bf16[384,2,128]{0,2,1:T(8,128)(2,1)}, u32[]{:S(2)}, u32[]{:S(2)}) collective-permute-start(bf16[384,2,128]{0,2,1:T(8,128)(2,1)} %pad_maximum_fusion.1), channel_id=1, source_target_pairs={{0,4},{1,5},{2,6},{3,7},{8,12},{9,13},{10,14},{11,15},{16,20},{17,... | collective-permute-start | bytes 589832 | tf_op jit(solution)/shard_map/ppermute | solution.py:20
  62.0 612.8 %copy-start.21 = (bf16[384,4,32]{0,2,1:T(8,128)(2,1)}, bf16[384,4,32]{0,2,1:T(8,128)(2,1)S(1)}, u32[]{:S(2)}) copy-start(bf16[384,4,32]{0,2,1:T(8,128)(2,1)S(1)} %get-tuple-element.39) | copy-start | bytes 294916
  62.1 612.8 %copy-start.23 = (bf16[384,4,32]{0,2,1:T(8,128)(2,1)}, bf16[384,4,32]{0,2,1:T(8,128)(2,1)S(1)}, u32[]{:S(2)}) copy-start(bf16[384,4,32]{0,2,1:T(8,128)(2,1)S(1)} %get-tuple-element.40) | copy-start | bytes 294916
  85.1 150.6 %all-gather.9.cloned.1.call-start = ((), (), s32[]{:S(2)}) async-start(), calls=%async_computation.8 | async-start | bytes 10485760 | tf_op jit(solution)/shard_map/all_gather | solution.py:182
  85.7 299.2 %all-gather.11.cloned.1.call-start = ((), (), s32[]{:S(2)}) async-start(), calls=%async_computation.9 | async-start | bytes 10485760 | tf_op jit(solution)/shard_map/all_gather | solution.py:183
  86.3 447.8 %all-gather.13.cloned.1.call-start = ((), (), s32[]{:S(2)}) async-start(), calls=%async_computation.10 | async-start | bytes 10485760 | tf_op jit(solution)/shard_map/all_gather | solution.py:184
  86.9 575.2 %all-reduce.13.cloned.1.call-start = ((), (), s32[]{:S(2)}) async-start(), calls=%async_computation.11 | async-start | bytes 3145728 | tf_op jit(solution)/shard_map/psum | solution.py:292
  109.9 495.1 %copy-start.50 = (s32[1536]{0:T(1024)}, s32[1536]{0:T(1024)S(1)}, u32[]{:S(2)}) copy-start(s32[1536]{0:T(1024)S(1)} %compare_select_fusion.4) | copy-start | bytes 18436
  620.8 119.9 %reduce-scatter.12.cloned.1.call-start = ((), (), s32[]{:S(2)}) async-start(), calls=%async_computation.14 | async-start | bytes 655360 | tf_op jit(solution)/shard_map/reduce_scatter | solution.py:397
  676.6 8.7 collective-permute-start.1
  677.9 62.9 %reduce-scatter.8.cloned.1.call-start = ((), (), s32[]{:S(2)}) async-start(), calls=%async_computation.12 | async-start | bytes 655360 | tf_op jit(solution)/shard_map/reduce_scatter | solution.py:391
  683.5 62.9 %reduce-scatter.10.cloned.1.call-start = ((), (), s32[]{:S(2)}) async-start(), calls=%async_computation.13 | async-start | bytes 655360 | tf_op jit(solution)/shard_map/reduce_scatter | solution.py:394
  687.9 207.8 %reduce-scatter.20.cloned.1.call-start = ((), (), s32[]{:S(2)}) async-start(), calls=%async_computation.20 | async-start | bytes 9437184 | tf_op jit(solution)/shard_map/reduce_scatter | solution.py:411
  697.0 362.0 %reduce-scatter.18.cloned.1.call-start = ((), (), s32[]{:S(2)}) async-start(), calls=%async_computation.18 | async-start | bytes 9437184 | tf_op jit(solution)/shard_map/reduce_scatter | solution.py:408
  705.3 517.1 %reduce-scatter.16.cloned.1.call-start = ((), (), s32[]{:S(2)}) async-start(), calls=%async_computation.16 | async-start | bytes 9437184 | tf_op jit(solution)/shard_map/reduce_scatter | solution.py:405
  713.5 510.3 %all-reduce.15.cloned.1.call-start = ((), (), s32[]{:S(2)}) async-start(), calls=%async_computation.22 | async-start | bytes 3145728 | tf_op jit(solution)/shard_map/psum | solution.py:269
  739.7 482.8 %copy-start.58 = (u32[32]{0:T(128)S(1)}, u32[32]{0:T(128)}, u32[]{:S(2)}) copy-start(u32[32]{0:T(128)} %constant.72) | copy-start | bytes 388
  739.7 503.9 %reduce-scatter.14.cloned.1.call-start = ((), (), s32[]{:S(2)}) async-start(), calls=%async_computation.15 | async-start | bytes 81920 | tf_op jit(solution)/shard_map/reduce_scatter | solution.py:400
  740.7 518.2 %all-reduce.17.cloned.1.call-start = ((), (), s32[]{:S(2)}) async-start(), calls=%async_computation.23 | async-start | bytes 786432 | tf_op jit(solution)/shard_map/psum | solution.py:429
  746.5 517.3 %all-gather.19.cloned.1.call-start = ((), (), s32[]{:S(2)}) async-start(), calls=%async_computation.21 | async-start | bytes 3145728 | tf_op jit(solution)/shard_map/all_gather | solution.py:422
  895.7 330.2 %copy-start.53 = (bf16[1024]{0:T(1024)(128)(2,1)S(1)}, bf16[1024]{0:T(1024)(128)(2,1)}, u32[]{:S(2)}) copy-start(bf16[1024]{0:T(1024)(128)(2,1)} %get-tuple-element.11) | copy-start | bytes 6148
  895.7 372.2 %all-gather.17.cloned.1.call-start = ((), (), s32[]{:S(2)}) async-start(), calls=%async_computation.19 | async-start | bytes 3145728 | tf_op jit(solution)/shard_map/all_gather | solution.py:419
  1059.1 213.1 %all-gather.15.cloned.1.call-start = ((), (), s32[]{:S(2)}) async-start(), calls=%async_computation.17 | async-start | bytes 3145728 | tf_op jit(solution)/shard_map/all_gather | solution.py:416
  (56 other events, 511.6 us)
Sparse Core Ops, SparseCore 0:
  85.2 40.9 all-reduce.10
  620.9 41.1 all-reduce.12
  739.8 44.9 all-reduce.14
  787.0 28.0 all-reduce.16
  895.8 32.5 all-gather.18
  1059.2 32.5 all-gather.16
  1222.6 32.7 all-gather.14
Sparse Core Ops, SparseCore 1:
  87.2 148.5 all-gather.8
  237.2 147.7 all-gather.10
  386.4 147.6 all-gather.12
  678.0 23.7 reduce-scatter.11
  704.0 20.1 reduce-scatter.7
  726.5 19.9 reduce-scatter.9
  749.9 145.7 reduce-scatter.19
  899.2 159.8 reduce-scatter.17
  1062.6 159.8 reduce-scatter.15
  1225.3 18.3 reduce-scatter.13
where the time goes:
time: 1290 us; the launch traced here: 1280 us
  waiting for transfers between devices  891 us (69%)
  blocking collectives  120 us (9%)
  matrix products  110 us (9%)
  other arithmetic  76.1 us (6%)
  local copies, waits for them, and re-layouts  62.6 us (5%)
  between operations  17.6 us (1%)
    reduce_scatter x1, waiting for transfers between devices, local(): lax.psum_scatter(grad_gate.astype(jnp.bfloat16), ('fsdp', 'ctx'), scatter...  163 us
    reduce_scatter x1, waiting for transfers between devices, local(): lax.psum_scatter(grad_up.astype(jnp.bfloat16), ('fsdp', 'ctx'), scatter_d...  163 us
    reduce_scatter x1, waiting for transfers between devices, local(): lax.psum_scatter(grad_down.astype(jnp.bfloat16), ('fsdp', 'ctx'), scatter...  149 us
    all_gather x1, waiting for transfers between devices, local(): lax.all_gather(w_up, 'fsdp', axis=1, tiled=True)  141 us
    all_gather x1, waiting for transfers between devices, local(): lax.all_gather(w_down, 'fsdp', axis=1, tiled=True)  140 us
    all_gather x1, waiting for transfers between devices, local(): lax.all_gather(w_gate, 'fsdp', axis=1, tiled=True)  91.1 us
    psum x1, waiting for transfers between devices, local(): lax.psum((hidden_grad_part, gate_grad_part), 'tp')  28.3 us
  transfers between devices with their start and end apart: 19, of which 9 were waited for; matrix products, arithmetic and copies ran while one was open for 10% of the time, Pallas kernels for 0%

commit v1 on v0

--- a/solution.py
+++ b/solution.py
@@ -446,9 +446,413 @@
     )
 
 
+def rotated(block, axis, distance):
+    count = lax.axis_size(axis)
+    return lax.ppermute(block, axis, [(i, (i + distance) % count) for i in range(count)])
+
+
+def pick_block(stacked, index):
+    return lax.dynamic_index_in_dim(stacked, index, 0, keepdims=False)
+
+
+def sum_over_tp(part):
+    count = lax.axis_size("tp")
+    pieces = part.astype(jnp.bfloat16).reshape(count, part.shape[0] // count, part.shape[1])
+    pieces = lax.all_to_all(pieces, "tp", 0, 0, tiled=True)
+    return jnp.sum(pieces.astype(jnp.float32), axis=0)
+
+
+def scatter_over_fsdp(stacked):
+    count = lax.axis_size("fsdp")
+    rank = lax.axis_index("fsdp")
+    total = pick_block(stacked, rank).astype(jnp.float32)
+    for step in range(1, count):
+        leaving = pick_block(stacked, (rank + step) % count)
+        total = total + rotated(leaving, "fsdp", step).astype(jnp.float32)
+    return total
+
+
+def sum_over_ctx(total):
+    sent = total.astype(jnp.bfloat16)
+    result = total
+    for step in range(1, lax.axis_size("ctx")):
+        result = result + rotated(sent, "ctx", step).astype(jnp.float32)
+    return result
+
+
+def local_spread(
+    tokens,
+    cotangent,
+    positions,
+    routes,
+    attn_gain,
+    w_query,
+    key_value_projection,
+    output_projection_weight,
+    ffn_gain,
+    w_router,
+    w_gate,
+    w_up,
+    w_down,
+):
+    everywhere = ("fsdp", "ctx", "tp")
+    fsdp_count, ctx_count, tp_count = (lax.axis_size(name) for name in everywhere)
+    fsdp_rank, ctx_rank, tp_rank = (lax.axis_index(name) for name in everywhere)
+    input_rows = tokens[0]
+    local_len, model_width = input_rows.shape
+    slice_width = w_query.shape[0]
+    own_len = local_len // tp_count
+    block_count = fsdp_count * ctx_count
+    expert_total = w_router.shape[1]
+    ff_width = w_gate.shape[2]
+    query_group_count = QUERY_HEADS // KEY_VALUE_HEADS
+    head_width = w_query.shape[1]
+    local_heads = head_width // HEAD_SIZE
+    local_kv = local_heads // query_group_count
+    capacity = local_len // 2
+    factor = 1.0 / math.sqrt(HEAD_SIZE)
+    own_start = tp_rank * own_len
+
+    def own_rows(rows):
+        return lax.dynamic_slice_in_dim(rows, own_start, own_len, 0)
+
+    kv_width = key_value_projection.shape[1] * 2 * HEAD_SIZE
+    side = jnp.concatenate([w_router, attn_gain[:, None], ffn_gain[:, None]], axis=1)
+    side = jnp.pad(side, ((0, 0), (0, -side.shape[1] % 128)))
+    packed = jnp.concatenate(
+        [w_query, key_value_projection.reshape(slice_width, kv_width), side], axis=1
+    )
+    packed = lax.all_gather(packed, "fsdp", axis=0, tiled=True)
+    out_full = lax.all_gather(output_projection_weight, "fsdp", axis=1, tiled=True)
+    query_full = packed[:, :head_width]
+    key_value_weight = packed[:, head_width : head_width + kv_width]
+    side_full = packed[:, head_width + kv_width :]
+    router_full = side_full[:, :expert_total]
+    gain_one = side_full[:, expert_total]
+    gain_two = side_full[:, expert_total + 1]
+
+    def leaving_weights(step):
+        index = ((fsdp_rank + step) % fsdp_count) * ctx_count + ctx_rank
+        return jnp.stack([pick_block(w, index) for w in (w_gate, w_up, w_down)])
+
+    weight_parts = [leaving_weights(0)]
+    for step in range(1, fsdp_count):
+        weight_parts.append(rotated(leaving_weights(step), "fsdp", step))
+    expert_weights = []
+    for kind in range(3):
+        whole = jnp.zeros((fsdp_count, slice_width, ff_width), jnp.bfloat16)
+        for step in range(fsdp_count):
+            whole = lax.dynamic_update_index_in_dim(
+                whole, weight_parts[step][kind], (fsdp_rank - step) % fsdp_count, 0
+            )
+        expert_weights.append(whole.reshape(fsdp_count * slice_width, ff_width))
+    gate_weight, up_weight, down_weight = expert_weights
+
+    route_rows = own_rows(routes[0])
+    route_tail = jnp.pad(
+        route_rows.astype(jnp.bfloat16), ((0, 0), (0, -route_rows.shape[1] % 128))
+    )
+    carried = jnp.concatenate([own_rows(cotangent[0]), route_tail], axis=1)
+    carried = lax.all_gather(carried, everywhere, axis=0, tiled=True)
+    grad_all = carried[:, :model_width].reshape(block_count, local_len, model_width)
+    routes_all = carried[:, model_width : model_width + route_rows.shape[1]].astype(jnp.int32)
+    expert_ids = jnp.arange(expert_total, dtype=jnp.int32)
+    chosen_all = jnp.any(routes_all[:, :, None] == expert_ids[None, None, :], axis=1)
+    own_expert = tp_rank * block_count + fsdp_rank * ctx_count + ctx_rank
+    member = jnp.any(routes_all == own_expert, axis=1).reshape(block_count, local_len)
+    places = jnp.cumsum(member.astype(jnp.int32), axis=1) - 1
+    slots = jnp.where(member, places, capacity)
+    slot_ids = jnp.arange(capacity, dtype=jnp.int32)
+    hot = slots[:, None, :] == slot_ids[None, :, None]
+    hot_b = hot.astype(jnp.bfloat16)
+
+    def take_rows(rows):
+        return (
+            jnp.einsum("bst,btd->bsd", hot_b, rows, preferred_element_type=jnp.float32)
+            .astype(jnp.bfloat16)
+            .reshape(block_count * capacity, model_width)
+        )
+
+    def put_rows(rows):
+        stacked = rows.reshape(block_count, capacity, model_width)
+        return (
+            jnp.einsum("bst,bsd->btd", hot_b, stacked, preferred_element_type=jnp.float32)
+            .astype(jnp.bfloat16)
+            .reshape(block_count * local_len, model_width)
+        )
+
+    wide_input = input_rows.astype(jnp.float32)
+    normed_one, factor_one, first_hidden_state = rms_forward(wide_input, gain_one)
+    query_matrix = jnp.dot(
+        first_hidden_state, query_full, preferred_element_type=jnp.float32
+    ).reshape(local_len, local_heads, HEAD_SIZE)
+    key_value_rows = jnp.dot(
+        first_hidden_state, key_value_weight, preferred_element_type=jnp.float32
+    ).reshape(local_len, local_kv, 2, HEAD_SIZE)
+    place_rows = positions[0]
+    cosine_lookup, sine_lookup = rope_tables(place_rows, HEAD_SIZE)
+    rotated_query = (
+        apply_rotary(query_matrix, cosine_lookup, sine_lookup, 1.0)
+        .astype(jnp.bfloat16)
+        .reshape(local_len, local_kv, query_group_count, HEAD_SIZE)
+    )
+    k_rot = apply_rotary(key_value_rows[:, :, 0], cosine_lookup, sine_lookup, 1.0).astype(
+        jnp.bfloat16
+    )
+    v_rows = key_value_rows[:, :, 1].astype(jnp.bfloat16)
+    local_ids = jnp.arange(local_len, dtype=jnp.int32)
+    query_ids = ctx_rank * local_len + local_ids
+    query_starts = query_ids - place_rows
+    kv_pack = jnp.concatenate([k_rot, v_rows], axis=-1)
+    kv_blocks = [kv_pack]
+    key_ids = [query_ids]
+    for step in range(1, ctx_count):
+        kv_blocks.append(shifted(kv_blocks[-1], "ctx", 1))
+        key_ids.append((ctx_rank - step) * local_len + local_ids)
+    row_total = jnp.zeros((local_kv, query_group_count, local_len), jnp.float32)
+    weighted = jnp.zeros((local_kv, query_group_count, local_len, HEAD_SIZE), jnp.float32)
+    masks = []
+    for block_index in range(ctx_count):
+        allowed = attend_mask(query_ids, query_starts, key_ids[block_index])
+        masks.append(allowed)
+        key_rows = kv_blocks[block_index][..., :HEAD_SIZE]
+        value_rows = kv_blocks[block_index][..., HEAD_SIZE:]
+        scores = (
+            jnp.einsum(
+                "tkgd,skd->kgts", rotated_query, key_rows, preferred_element_type=jnp.float32
+            )
+            * factor
+        )
+        exp_scores = jnp.where(allowed[None, None], jnp.exp(scores), 0.0)
+        row_total = row_total + jnp.sum(exp_scores, axis=-1)
+        weighted = weighted + jnp.einsum(
+            "kgts,skd->kgtd",
+            exp_scores.astype(jnp.bfloat16),
+            value_rows,
+            preferred_element_type=jnp.float32,
+        )
+    head_out = (weighted / row_total[..., None]).astype(jnp.bfloat16)
+    flat_heads = head_out.transpose(2, 0, 1, 3).reshape(local_len, local_heads * HEAD_SIZE)
+    attn_part = jnp.dot(flat_heads, out_full, preferred_element_type=jnp.float32)
+
+    residual = own_rows(input_rows).astype(jnp.float32) + sum_over_tp(attn_part)
+    normed_two, factor_two, hidden_two = rms_forward(residual, gain_two)
+    hidden_all = lax.all_gather(hidden_two, everywhere, axis=0, tiled=True)
+    own_chosen = jnp.any(route_rows[:, :, None] == expert_ids[None, None, :], axis=1)
+
+    def gate_table(hidden, chosen):
+        logits = jnp.dot(hidden, router_full, preferred_element_type=jnp.float32)
+        exp_sel = jnp.where(chosen, jnp.exp(logits), 0.0)
+        return exp_sel / jnp.sum(exp_sel, axis=-1, keepdims=True)
+
+    own_gates = gate_table(hidden_two, own_chosen)
+    gates_all = gate_table(hidden_all, chosen_all)
+    expert_gate = jnp.sum(
+        jnp.where(expert_ids[None, :] == own_expert, gates_all, 0.0), axis=1
+    ).reshape(block_count, local_len)
+    scaled = jnp.sum(jnp.where(hot, expert_gate[:, None, :], 0.0), axis=2).reshape(-1)
+
+    picked = take_rows(hidden_all.reshape(block_count, local_len, model_width))
+    gate_pre = jnp.dot(picked, gate_weight, preferred_element_type=jnp.float32)
+    up_pre = jnp.dot(picked, up_weight, preferred_element_type=jnp.float32)
+    activation = (jax.nn.silu(gate_pre) * up_pre).astype(jnp.bfloat16)
+    result = jnp.einsum("cf,df->cd", activation, down_weight, preferred_element_type=jnp.float32)
+    mixture_part = put_rows((result * scaled[:, None]).astype(jnp.bfloat16))
+
+    grad_rows = take_rows(grad_all)
+    grad_wide_rows = grad_rows.astype(jnp.float32)
+    slot_grad = jnp.sum(grad_wide_rows * result, axis=1).reshape(block_count, capacity)
+    gate_grad_part = jnp.sum(jnp.where(hot, slot_grad[:, :, None], 0.0), axis=1)
+    out_grad = (grad_wide_rows * scaled[:, None]).astype(jnp.bfloat16)
+    act_grad = jnp.dot(out_grad, down_weight, preferred_element_type=jnp.float32)
+    sigmoid_gate = jax.nn.sigmoid(gate_pre)
+    gate_pre_grad = (
+        act_grad * up_pre * sigmoid_gate * (1.0 + gate_pre * (1.0 - sigmoid_gate))
+    ).astype(jnp.bfloat16)
+    up_pre_grad = (act_grad * gate_pre * sigmoid_gate).astype(jnp.bfloat16)
+    picked_grad = jnp.einsum(
+        "cf,df->cd", gate_pre_grad, gate_weight, preferred_element_type=jnp.float32
+    ) + jnp.einsum("cf,df->cd", up_pre_grad, up_weight, preferred_element_type=jnp.float32)
+    hidden_grad_part = put_rows(picked_grad.astype(jnp.bfloat16))
+    hidden_grad_sum = lax.psum_scatter(
+        hidden_grad_part, everywhere, scatter_dimension=0, tiled=True
+    ).astype(jnp.float32)
+    gate_grad = lax.all_to_all(
+        gate_grad_part.reshape(block_count * tp_count, own_len), everywhere, 0, 0, tiled=True
+    )
+    gate_grad = (
+        gate_grad.reshape(block_count, tp_count, own_len)
+        .transpose(2, 1, 0)
+        .reshape(own_len, expert_total)
+    )
+    mixture = lax.psum_scatter(mixture_part, everywhere, scatter_dimension=0, tiled=True)
+    own_out = (residual + mixture.astype(jnp.float32)).astype(jnp.bfloat16)
+
+    weight_grads = [
+        jnp.einsum("cd,cf->df", rows, columns, preferred_element_type=jnp.float32)
+        .astype(jnp.bfloat16)
+        .reshape(fsdp_count, slice_width, ff_width)
+        for rows, columns in (
+            (picked, gate_pre_grad),
+            (picked, up_pre_grad),
+            (out_grad, activation),
+        )
+    ]
+    weight_shape = (fsdp_count, ctx_count, slice_width, ff_width)
+    weight_outs = [jnp.zeros(weight_shape, jnp.float32) for _ in range(3)]
+    for step in range(fsdp_count):
+        target = (fsdp_rank + step) % fsdp_count
+        piece = jnp.stack([pick_block(grad, target) for grad in weight_grads])
+        if step:
+            piece = rotated(piece, "fsdp", step)
+        source = (fsdp_rank - step) % fsdp_count
+        for hop in range(ctx_count):
+            seen = rotated(piece, "ctx", hop) if hop else piece
+            seen_ctx = (ctx_rank - hop) % ctx_count
+            for kind in range(3):
+                weight_outs[kind] = lax.dynamic_update_slice(
+                    weight_outs[kind],
+                    seen[kind].astype(jnp.float32)[None, None],
+                    (source, seen_ctx, 0, 0),
+                )
+    weight_outs = [
+        grad.reshape(fsdp_count * ctx_count, slice_width, ff_width) for grad in weight_outs
+    ]
+
+    sel_grad = own_gates * (
+        gate_grad - jnp.sum(own_gates * gate_grad, axis=-1, keepdims=True)
+    )
+    logit_grad = jnp.where(own_chosen, sel_grad, 0.0).astype(jnp.bfloat16)
+    grad_router = jnp.einsum(
+        "te,td->ed", logit_grad, hidden_two, preferred_element_type=jnp.float32
+    )
+    hidden_grad = hidden_grad_sum + jnp.einsum(
+        "te,de->td", logit_grad, router_full, preferred_element_type=jnp.float32
+    )
+    back_two, grad_ffn_gain = rms_backward(hidden_grad, normed_two, factor_two, gain_two)
+    residual_grad = own_rows(cotangent[0]).astype(jnp.float32) + back_two
+    residual_gradient_second = lax.all_gather(
+        residual_grad.astype(jnp.bfloat16), "tp", axis=0, tiled=True
+    )
+    early = lax.psum(jnp.concatenate([grad_router, grad_ffn_gain[None]], axis=0), everywhere)
+    early = lax.dynamic_slice_in_dim(early, fsdp_rank * slice_width, slice_width, 1)
+
+    grad_out_proj = jnp.einsum(
+        "ti,td->id", flat_heads, residual_gradient_second, preferred_element_type=jnp.float32
+    )
+    grad_out_proj = grad_out_proj.astype(jnp.bfloat16).reshape(
+        head_width, fsdp_count, slice_width
+    )
+    out_proj_total = sum_over_ctx(scatter_over_fsdp(grad_out_proj.transpose(1, 0, 2)))
+    per_head_gradient = jnp.einsum(
+        "td,id->ti", residual_gradient_second, out_full, preferred_element_type=jnp.float32
+    ).astype(jnp.bfloat16)
+    per_head_gradient = per_head_gradient.reshape(
+        local_len, local_kv, query_group_count, HEAD_SIZE
+    ).transpose(1, 2, 0, 3)
+    row_delta = jnp.sum(
+        per_head_gradient.astype(jnp.float32) * head_out.astype(jnp.float32), axis=-1
+    )
+    log_total = jnp.log(row_total)
+    query_grad = jnp.zeros((local_len, local_kv, query_group_count, HEAD_SIZE), jnp.float32)
+    kv_grads = []
+    for block_index in range(ctx_count):
+        key_rows = kv_blocks[block_index][..., :HEAD_SIZE]
+        value_rows = kv_blocks[block_index][..., HEAD_SIZE:]
+        scores = (
+            jnp.einsum(
+                "tkgd,skd->kgts", rotated_query, key_rows, preferred_element_type=jnp.float32
+            )
+            * factor
+        )
+        probability = jnp.where(
+            masks[block_index][None, None], jnp.exp(scores - log_total[..., None]), 0.0
+        )
+        prob_grad = jnp.einsum(
+            "kgtd,skd->kgts", per_head_gradient, value_rows, preferred_element_type=jnp.float32
+        )
+        score_grad = (probability * (prob_grad - row_delta[..., None]) * factor).astype(
+            jnp.bfloat16
+        )
+        query_grad = query_grad + jnp.einsum(
+            "kgts,skd->tkgd", score_grad, key_rows, preferred_element_type=jnp.float32
+        )
+        key_grad = jnp.einsum(
+            "kgts,tkgd->skd", score_grad, rotated_query, preferred_element_type=jnp.float32
+        )
+        value_gradient = jnp.einsum(
+            "kgts,kgtd->skd",
+            probability.astype(jnp.bfloat16),
+            per_head_gradient,
+            preferred_element_type=jnp.float32,
+        )
+        kv_grads.append(jnp.concatenate([key_grad, value_gradient], axis=-1))
+    kv_grad_total = kv_grads[0]
+    for step in range(1, ctx_count):
+        kv_grad_total = kv_grad_total + shifted(
+            kv_grads[step].astype(jnp.bfloat16), "ctx", -step
+        ).astype(jnp.float32)
+    key_backward_rows = apply_rotary(
+        kv_grad_total[..., :HEAD_SIZE], cosine_lookup, sine_lookup, -1.0
+    )
+    key_value_backward = (
+        jnp.stack([key_backward_rows, kv_grad_total[..., HEAD_SIZE:]], axis=2)
+        .astype(jnp.bfloat16)
+        .reshape(local_len, kv_width)
+    )
+    query_back = (
+        apply_rotary(
+            query_grad.reshape(local_len, local_heads, HEAD_SIZE), cosine_lookup, sine_lookup, -1.0
+        )
+        .astype(jnp.bfloat16)
+        .reshape(local_len, head_width)
+    )
+    both_back = jnp.concatenate([query_back, key_value_backward], axis=1)
+    both_weight = packed[:, : head_width + kv_width]
+    hidden_one_part = jnp.einsum(
+        "tf,df->td", both_back, both_weight, preferred_element_type=jnp.float32
+    )
+    grad_attn_gain = lax.psum(jnp.sum(hidden_one_part * normed_one, axis=0), everywhere)
+    grad_attn_gain = lax.dynamic_slice_in_dim(
+        grad_attn_gain, fsdp_rank * slice_width, slice_width, 0
+    )
+    projection_grad = jnp.einsum(
+        "td,tf->df", first_hidden_state, both_back, preferred_element_type=jnp.float32
+    ).astype(jnp.bfloat16)
+    projection_total = sum_over_ctx(
+        scatter_over_fsdp(projection_grad.reshape(fsdp_count, slice_width, head_width + kv_width))
+    )
+    hidden_one_grad = sum_over_tp(hidden_one_part)
+    back_one, _ = rms_backward(
+        hidden_one_grad, own_rows(normed_one), own_rows(factor_one), gain_one
+    )
+    input_grad = residual_grad + back_one
+    finished = jnp.concatenate([own_out, input_grad.astype(jnp.bfloat16)], axis=1)
+    finished = lax.all_gather(finished, "tp", axis=0, tiled=True)
+    return (
+        finished[:, :model_width][None],
+        finished[:, model_width:].astype(jnp.float32)[None],
+        grad_attn_gain,
+        projection_total[:, :head_width],
+        projection_total[:, head_width:].reshape(key_value_projection.shape),
+        out_proj_total,
+        early[expert_total],
+        early[:expert_total].T,
+        weight_outs[0],
+        weight_outs[1],
+        weight_outs[2],
+    )
+
+
+def local_any(*args):
+    devices = math.prod(lax.axis_size(name) for name in ("fsdp", "ctx", "tp"))
+    return (local_spread if args[9].shape[1] == devices else local)(*args)
+
+
 def solution(mesh):
+
     return jax.shard_map(
-        local,
+        local_any,
         mesh=mesh,
         in_specs=(
             P("fsdp", "ctx", None),

time: 1290 us -> 818 us (0.63)
  waiting for transfers between devices: 891 us -> 501 us
  matrix products: 110 us -> 68.4 us
  starting transfers between devices: 6.26 us -> 39.7 us
  blocking collectives: 120 us -> 88.2 us
  local copies, waits for them, and re-layouts: 62.6 us -> 40.6 us
  other arithmetic: 76.1 us -> 56.4 us
    reduce_scatter x7 -> x2, waiting for transfers between devices: 489 us -> 174 us  [the longest x1 118 us: local_spread(): lax.psum_scatter(mixture_part, everywhere, scatter_dimension=0, tiled=True)]
    all_gather x6 -> x4, waiting for transfers between devices: 372 us -> 89.8 us  [the longest x1 71.9 us: local_spread(): hidden_all = lax.all_gather(hidden_two, everywhere, axis=0, tiled=True)]
    ppermute x0 -> x18, waiting for transfers between devices: none -> 134 us  [rotated(): lax.ppermute(block, axis, [(i, (i + distance) % count) for i in range(cou...]
    psum x4 -> x1, waiting for transfers between devices: 28.3 us -> 87.6 us  [local_spread(): lax.psum(jnp.concatenate([grad_router, grad_ffn_gain[None]], axis=0), eve...]
    all_gather x6 -> x2, blocking collectives: 87.6 us -> 31.3 us  [the longest x1 22.8 us: local_spread(): lax.all_gather(output_projection_weight, 'fsdp', axis=1, tiled=True)]
    dot_general x33 -> x36, matrix products: 110 us -> 68.4 us  [the longest x2 9.13 us: put_rows(): jnp.einsum('bst,bsd->btd', hot_b, stacked, preferred_element_type=jnp.flo...]
    scatter-add x2 -> x0, other arithmetic: 31.7 us -> none  [the longest x1 15.9 us: combine(): return jnp.zeros((token_count, model_width), jnp.float32).at[source].add(...]
    gather x5 -> x0, local copies, waits for them, and re-layouts: 30.8 us -> none  [the longest x3 19.2 us: expert_backward(): per_expert = padded[slot_ids]]
  transfers between devices with their start and end apart: 19 -> 29, of which waited for: 9 -> 16; matrix products, arithmetic and copies ran while one was open for 10% -> 14% of each run, Pallas kernels for 0% -> 0%
where the time goes in v1:
time: 818 us; the launch traced here: 810 us
  waiting for transfers between devices  501 us (61%)
  blocking collectives  88.2 us (11%)
  matrix products  68.4 us (8%)
  other arithmetic  56.4 us (7%)
  local copies, waits for them, and re-layouts  40.6 us (5%)
  starting transfers between devices  39.7 us (5%)
  between operations  16.1 us (2%)
    ppermute x18, waiting for transfers between devices, rotated(): lax.ppermute(block, axis, [(i, (i + distance) % count) for i in range(cou...  134 us
    reduce_scatter x1, waiting for transfers between devices, local_spread(): lax.psum_scatter(mixture_part, everywhere, scatter_dimension=0, tiled=True)  118 us
    psum x1, waiting for transfers between devices, local_spread(): lax.psum(jnp.concatenate([grad_router, grad_ffn_gain[None]], axis=0), eve...  87.6 us
    all_gather x1, waiting for transfers between devices, local_spread(): hidden_all = lax.all_gather(hidden_two, everywhere, axis=0, tiled=True)  71.9 us
    reduce_scatter x1, waiting for transfers between devices, local_spread(): lax.psum_scatter(hidden_grad_part, everywhere, scatter_dimension=0, tiled...  56 us
    psum x1, blocking collectives, local_spread(): lax.psum(jnp.sum(hidden_one_part * normed_one, axis=0), everywhere)  42.7 us
    ppermute x18, starting transfers between devices, rotated(): lax.ppermute(block, axis, [(i, (i + distance) % count) for i in range(cou...  26.9 us
    all_gather x1, blocking collectives, local_spread(): lax.all_gather(output_projection_weight, 'fsdp', axis=1, tiled=True)  22.8 us
  transfers between devices with their start and end apart: 29, of which 16 were waited for; matrix products, arithmetic and copies ran while one was open for 14% of the time, Pallas kernels for 0%

profile of v1, /device:TPU:0, one launch (start us, length us, event | category | flops | bytes accessed | tf_op | source)
XLA Modules:
  0.0 810.3 jit_solution(1267393773189498881)
XLA Ops:
  14.5 22.8 %all_gather.19 = bf16[256,1024]{1,0:T(8,128)(2,1)S(1)} all-gather(bf16[256,256]{1,0:T(8,128)(2,1)S(1)} %copy-done.52), channel_id=1, replica_groups=mesh['fsdp'=4,'ctx'=2,'tp'=4] {'fsdp'}, dimensions={1}, use_global_device_ids=true | all-gather | bytes 655360 | tf_op jit(solution)/shard_map/all_gather | solution.py:526
  38.5 13.1 %all-gather.5.cloned.1.call-done = bf16[1024,640]{1,0:T(8,128)(2,1)} async-done(((bf16[256,640]{1,0:T(8,128)(2,1)}), bf16[1024,640]{1,0:T(8,128)(2,1)}) %all-gather.5.cloned.1.call-update) | async-done | bytes 1310736 | tf_op jit(solution)/shard_map/all_gather | solution.py:525
  69.1 14.2 %all_to_all.19 = bf16[4,96,1024]{2,1,0:T(8,128)(2,1)S(1)} all-to-all(bf16[4,96,1024]{2,1,0:T(8,128)(2,1)S(1)} %bitcast.440), channel_id=1, replica_groups=mesh['fsdp'=4,'ctx'=2,'tp'=4] {'tp'}, dimensions={0} | all-to-all | bytes 1572864 | tf_op jit(solution)/shard_map/all_to_all | solution.py:461
  95.8 18.4 %collective-permute-done.1 = bf16[3,256,512]{2,1,0:T(8,128)(2,1)} collective-permute-done((bf16[3,256,512]{2,1,0:T(8,128)(2,1)}, bf16[3,256,512]{2,1,0:T(8,128)(2,1)}, u32[]{:S(2)}, u32[]{:S(2)}) %collective-permute-start.1) | collective-permute-done | bytes 786464 | tf_op jit(solution)/shard_map/ppermute | solution.py:451
  115.4 45.7 %collective-permute-done.2 = bf16[3,256,512]{2,1,0:T(8,128)(2,1)} collective-permute-done((bf16[3,256,512]{2,1,0:T(8,128)(2,1)}, bf16[3,256,512]{2,1,0:T(8,128)(2,1)}, u32[]{:S(2)}, u32[]{:S(2)}) %collective-permute-start.2) | collective-permute-done | bytes 786464 | tf_op jit(solution)/shard_map/ppermute | solution.py:451
  164.6 4.8 all-gather.7.cloned.1.call-done
  177.1 71.9 %all-gather.9.cloned.1.call-done = bf16[3072,1024]{1,0:T(8,128)(2,1)} async-done(((bf16[96,1024]{1,0:T(8,128)(2,1)}), bf16[3072,1024]{1,0:T(8,128)(2,1)}) %all-gather.9.cloned.1.call-update) | async-done | bytes 6291472 | tf_op jit(solution)/shard_map/all_gather | solution.py:640
  249.0 4.9 fusion.113
  256.0 4.7 fusion.13
  266.6 5.3 fusion.1
  277.7 5.0 multiply_convert_fusion.2
  286.7 4.5 convolution_convert_fusion
  292.6 4.6 fusion.2
  297.2 4.6 convolution_convert_fusion.1
  341.8 45.2 %collective-permute-done.16 = bf16[3,256,512]{2,1,0:T(8,128)(2,1)} collective-permute-done((bf16[3,256,512]{2,1,0:T(8,128)(2,1)}, bf16[3,256,512]{2,1,0:T(8,128)(2,1)}, u32[]{:S(2)}, u32[]{:S(2)}) %collective-permute-start.16) | collective-permute-done | bytes 786464 | tf_op jit(solution)/shard_map/ppermute | solution.py:451
  397.2 56.0 %reduce-scatter.9.cloned.1.call-done = bf16[96,1024]{1,0:T(8,128)(2,1)} async-done(((bf16[3072,1024]{1,0:T(8,128)(2,1)}), bf16[96,1024]{1,0:T(8,128)(2,1)}) %reduce-scatter.9.cloned.1.call-update) | async-done | bytes 196624 | tf_op jit(solution)/shard_map/reduce_scatter | solution.py:677
  454.5 118.1 %reduce-scatter.7.cloned.1.call-done = bf16[96,1024]{1,0:T(8,128)(2,1)} async-done(((bf16[3072,1024]{1,0:T(8,128)(2,1)}), bf16[96,1024]{1,0:T(8,128)(2,1)}) %reduce-scatter.7.cloned.1.call-update) | async-done | bytes 196624 | tf_op jit(solution)/shard_map/reduce_scatter | solution.py:688
  574.7 8.6 %all_gather.22 = bf16[384,1024]{1,0:T(8,128)(2,1)S(1)} all-gather(bf16[96,1024]{1,0:T(8,128)(2,1)S(1)} %get-tuple-element.111), channel_id=1, replica_groups=mesh['fsdp'=4,'ctx'=2,'tp'=4] {'tp'}, dimensions={0}, use_global_device_ids=true | all-gather | bytes 983040 | tf_op jit(solution)/shard_map/all_gather | solution.py:734
  592.8 6.2 collective-permute-done.4
  611.7 6.1 all-to-all-done.2
  633.8 4.3 collective-permute-start.5
  643.4 19.3 %collective-permute-done.6 = bf16[256,512]{1,0:T(8,128)(2,1)S(1)} collective-permute-done((bf16[256,512]{1,0:T(8,128)(2,1)S(1)}, bf16[256,512]{1,0:T(8,128)(2,1)S(1)}, u32[]{:S(2)}, u32[]{:S(2)}) %collective-permute-start.6) | collective-permute-done | bytes 262176 | tf_op jit(solution)/shard_map/ppermute | solution.py:451
  662.9 87.6 %all-reduce.4.cloned.1.call-done = f32[33,1024]{1,0:T(8,128)} async-done(((f32[33,1024]{1,0:T(8,128)}), f32[33,1024]{1,0:T(8,128)}) %all-reduce.4.cloned.1.call-update) | async-done | bytes 135184 | tf_op jit(solution)/shard_map/psum | solution.py:737
  753.2 42.7 %psum.14 = f32[1024]{0:T(1024)S(1)} all-reduce(f32[1024]{0:T(1024)S(1)} %copy-done.62), channel_id=1, replica_groups=mesh['fsdp'=4,'ctx'=2,'tp'=4] {'fsdp','ctx','tp'}, use_global_device_ids=true, to_apply=%region_24.25 | all-reduce | flops 1024 | bytes 8192 | tf_op jit(solution)/shard_map/psum | solution.py:815
  (366 shorter events, 175.7 us)
Async XLA Ops:
  7.2 44.4 %all-gather.5.cloned.1.call-start = ((), (), s32[]{:S(2)}) async-start(), calls=%async_computation.5 | async-start | bytes 1638400 | tf_op jit(solution)/shard_map/all_gather | solution.py:525
  12.2 157.1 %all-gather.7.cloned.1.call-start = ((), (), s32[]{:S(2)}) async-start(), calls=%async_computation.6 | async-start | bytes 7299072 | tf_op jit(solution)/shard_map/all_gather | solution.py:556
  14.1 234.9 %all-gather.9.cloned.1.call-start = ((), (), s32[]{:S(2)}) async-start(), calls=%async_computation.7 | async-start | bytes 6488064 | tf_op jit(solution)/shard_map/all_gather | solution.py:640
  84.8 368.4 %reduce-scatter.9.cloned.1.call-start = ((), (), s32[]{:S(2)}) async-start(), calls=%async_computation.11 | async-start | bytes 6488064 | tf_op jit(solution)/shard_map/reduce_scatter | solution.py:677
  89.3 24.9 %collective-permute-start.1 = (bf16[3,256,512]{2,1,0:T(8,128)(2,1)}, bf16[3,256,512]{2,1,0:T(8,128)(2,1)}, u32[]{:S(2)}, u32[]{:S(2)}) collective-permute-start(bf16[3,256,512]{2,1,0:T(8,128)(2,1)} %pad_maximum_fusion), channel_id=1, source_target_pairs={{0,8},{8,16},{16,24},{24,0},{1,9},{9,17},{17,25},{25,1},{2,10},{10... | collective-permute-start | bytes 2359304 | tf_op jit(solution)/shard_map/ppermute | solution.py:451
  90.6 70.5 %collective-permute-start.2 = (bf16[3,256,512]{2,1,0:T(8,128)(2,1)}, bf16[3,256,512]{2,1,0:T(8,128)(2,1)}, u32[]{:S(2)}, u32[]{:S(2)}) collective-permute-start(bf16[3,256,512]{2,1,0:T(8,128)(2,1)} %pad_maximum_fusion.1), channel_id=1, source_target_pairs={{0,16},{8,24},{16,0},{24,8},{1,17},{9,25},{17,1},{25,9},{2,18},{10... | collective-permute-start | bytes 2359304 | tf_op jit(solution)/shard_map/ppermute | solution.py:451
  93.2 69.1 %collective-permute-start.3 = (bf16[3,256,512]{2,1,0:T(8,128)(2,1)}, bf16[3,256,512]{2,1,0:T(8,128)(2,1)}, u32[]{:S(2)}, u32[]{:S(2)}) collective-permute-start(bf16[3,256,512]{2,1,0:T(8,128)(2,1)} %pad_maximum_fusion.2), channel_id=1, source_target_pairs={{0,24},{8,0},{16,8},{24,16},{1,25},{9,1},{17,9},{25,17},{2,26},{10... | collective-permute-start | bytes 2359304 | tf_op jit(solution)/shard_map/ppermute | solution.py:451
  291.2 281.4 %reduce-scatter.7.cloned.1.call-start = ((), (), s32[]{:S(2)}) async-start(), calls=%async_computation.10 | async-start | bytes 6488064 | tf_op jit(solution)/shard_map/reduce_scatter | solution.py:688
  304.2 32.6 %all-to-all-start.1 = ((f32[32,1,96]{2,1,0:T(1,128)}), f32[32,1,96]{2,1,0:T(1,128)S(1)}, u32[]{:S(2)}, u32[]{:S(2)}) async-start(f32[32,1,96]{2,1,0:T(1,128)} %all_to_all.13), calls=%async_computation.1 | async-start | bytes 32768 | tf_op jit(solution)/shard_map/all_to_all | solution.py:680
  316.5 22.7 %collective-permute-start.14 = (bf16[3,256,512]{2,1,0:T(8,128)(2,1)}, bf16[3,256,512]{2,1,0:T(8,128)(2,1)}, u32[]{:S(2)}, u32[]{:S(2)}) collective-permute-start(bf16[3,256,512]{2,1,0:T(8,128)(2,1)} %pad_maximum_fusion.4), channel_id=1, source_target_pairs={{0,8},{8,16},{16,24},{24,0},{1,9},{9,17},{17,25},{25,1},{2,10},{10... | collective-permute-start | bytes 2359304 | tf_op jit(solution)/shard_map/ppermute | solution.py:451
  319.3 69.7 %collective-permute-start.13 = (bf16[3,256,512]{2,1,0:T(8,128)(2,1)}, bf16[3,256,512]{2,1,0:T(8,128)(2,1)}, u32[]{:S(2)}, u32[]{:S(2)}) collective-permute-start(bf16[3,256,512]{2,1,0:T(8,128)(2,1)} %pad_maximum_fusion.3), channel_id=1, source_target_pairs={{0,4},{4,0},{1,5},{5,1},{2,6},{6,2},{3,7},{7,3},{8,12},{12,8},{9,1... | collective-permute-start | bytes 2359304 | tf_op jit(solution)/shard_map/ppermute | solution.py:451
  321.8 65.3 %collective-permute-start.16 = (bf16[3,256,512]{2,1,0:T(8,128)(2,1)}, bf16[3,256,512]{2,1,0:T(8,128)(2,1)}, u32[]{:S(2)}, u32[]{:S(2)}) collective-permute-start(bf16[3,256,512]{2,1,0:T(8,128)(2,1)} %pad_maximum_fusion.5), channel_id=1, source_target_pairs={{0,16},{8,24},{16,0},{24,8},{1,17},{9,25},{17,1},{25,9},{2,18},{10... | collective-permute-start | bytes 2359304 | tf_op jit(solution)/shard_map/ppermute | solution.py:451
  325.2 63.5 %collective-permute-start.18 = (bf16[3,256,512]{2,1,0:T(8,128)(2,1)}, bf16[3,256,512]{2,1,0:T(8,128)(2,1)}, u32[]{:S(2)}, u32[]{:S(2)}) collective-permute-start(bf16[3,256,512]{2,1,0:T(8,128)(2,1)} %pad_maximum_fusion.6), channel_id=1, source_target_pairs={{0,24},{8,0},{16,8},{24,16},{1,25},{9,1},{17,9},{25,17},{2,26},{10... | collective-permute-start | bytes 2359304 | tf_op jit(solution)/shard_map/ppermute | solution.py:451
  339.1 54.6 %collective-permute-start.15 = (bf16[3,256,512]{2,1,0:T(8,128)(2,1)}, bf16[3,256,512]{2,1,0:T(8,128)(2,1)S(1)}, u32[]{:S(2)}, u32[]{:S(2)}) collective-permute-start(bf16[3,256,512]{2,1,0:T(8,128)(2,1)} %collective-permute-done.14), channel_id=1, source_target_pairs={{0,4},{4,0},{1,5},{5,1},{2,6},{6,2},{3,7},{7,3},{8,12},{12,8},{9,1... | collective-permute-start | bytes 2359304 | tf_op jit(solution)/shard_map/ppermute | solution.py:451
  387.0 219.2 %collective-permute-start.17 = (bf16[3,256,512]{2,1,0:T(8,128)(2,1)}, bf16[3,256,512]{2,1,0:T(8,128)(2,1)}, u32[]{:S(2)}, u32[]{:S(2)}) collective-permute-start(bf16[3,256,512]{2,1,0:T(8,128)(2,1)} %collective-permute-done.16), channel_id=1, source_target_pairs={{0,4},{4,0},{1,5},{5,1},{2,6},{6,2},{3,7},{7,3},{8,12},{12,8},{9,1... | collective-permute-start | bytes 2359304 | tf_op jit(solution)/shard_map/ppermute | solution.py:451
  388.7 244.5 %collective-permute-start.19 = (bf16[3,256,512]{2,1,0:T(8,128)(2,1)}, bf16[3,256,512]{2,1,0:T(8,128)(2,1)}, u32[]{:S(2)}, u32[]{:S(2)}) collective-permute-start(bf16[3,256,512]{2,1,0:T(8,128)(2,1)} %collective-permute-done.18), channel_id=1, source_target_pairs={{0,4},{4,0},{1,5},{5,1},{2,6},{6,2},{3,7},{7,3},{8,12},{12,8},{9,1... | collective-permute-start | bytes 2359304 | tf_op jit(solution)/shard_map/ppermute | solution.py:451
  601.9 15.9 %all-to-all-start.2 = ((bf16[4,96,1024]{2,1,0:T(8,128)(2,1)}), bf16[4,96,1024]{2,1,0:T(8,128)(2,1)}, u32[]{:S(2)}, u32[]{:S(2)}) async-start(bf16[4,96,1024]{2,1,0:T(8,128)(2,1)} %bitcast.438), calls=%async_computation.2 | async-start | bytes 1572864 | tf_op jit(solution)/shard_map/all_to_all | solution.py:461
  606.2 144.4 %all-reduce.4.cloned.1.call-start = ((), (), s32[]{:S(2)}) async-start(), calls=%async_computation.9 | async-start | bytes 327680 | tf_op jit(solution)/shard_map/psum | solution.py:737
  611.7 188.3 %all-gather.11.cloned.1.call-start = ((), (), s32[]{:S(2)}) async-start(), calls=%async_computation.8 | async-start | bytes 1966080 | tf_op jit(solution)/shard_map/all_gather | solution.py:831
  627.7 13.5 %collective-permute-start.10 = (bf16[256,256]{1,0:T(8,128)(2,1)S(1)}, bf16[256,256]{1,0:T(8,128)(2,1)S(1)}, u32[]{:S(2)}, u32[]{:S(2)}) collective-permute-start(bf16[256,256]{1,0:T(8,128)(2,1)S(1)} %bitcast.476), channel_id=1, source_target_pairs={{0,16},{8,24},{16,0},{24,8},{1,17},{9,25},{17,1},{25,9},{2,18},{10... | collective-permute-start | bytes 393224 | tf_op jit(solution)/shard_map/ppermute | solution.py:451
  633.2 29.5 %collective-permute-start.6 = (bf16[256,512]{1,0:T(8,128)(2,1)S(1)}, bf16[256,512]{1,0:T(8,128)(2,1)S(1)}, u32[]{:S(2)}, u32[]{:S(2)}) collective-permute-start(bf16[256,512]{1,0:T(8,128)(2,1)S(1)} %get-tuple-element.66), channel_id=1, source_target_pairs={{0,16},{8,24},{16,0},{24,8},{1,17},{9,25},{17,1},{25,9},{2,18},{10... | collective-permute-start | bytes 786440 | tf_op jit(solution)/shard_map/ppermute | solution.py:451
  633.8 28.9 %collective-permute-start.5 = (bf16[256,512]{1,0:T(8,128)(2,1)S(1)}, bf16[256,512]{1,0:T(8,128)(2,1)S(1)}, u32[]{:S(2)}, u32[]{:S(2)}) collective-permute-start(bf16[256,512]{1,0:T(8,128)(2,1)S(1)} %get-tuple-element.64), channel_id=1, source_target_pairs={{0,8},{8,16},{16,24},{24,0},{1,9},{9,17},{17,25},{25,1},{2,10},{10... | collective-permute-start | bytes 786440 | tf_op jit(solution)/shard_map/ppermute | solution.py:451
  641.2 155.3 %collective-permute-start.12 = (bf16[256,256]{1,0:T(8,128)(2,1)S(1)}, bf16[256,256]{1,0:T(8,128)(2,1)}, u32[]{:S(2)}, u32[]{:S(2)}) collective-permute-start(bf16[256,256]{1,0:T(8,128)(2,1)S(1)} %fusion.94), channel_id=1, source_target_pairs={{0,4},{4,0},{1,5},{5,1},{2,6},{6,2},{3,7},{7,3},{8,12},{12,8},{9,1... | collective-permute-start | bytes 393224 | tf_op jit(solution)/shard_map/ppermute | solution.py:451
  662.9 135.3 %collective-permute-start.8 = (bf16[256,512]{1,0:T(8,128)(2,1)S(1)}, bf16[256,512]{1,0:T(8,128)(2,1)S(1)}, u32[]{:S(2)}, u32[]{:S(2)}) collective-permute-start(bf16[256,512]{1,0:T(8,128)(2,1)S(1)} %fusion.82), channel_id=1, source_target_pairs={{0,4},{4,0},{1,5},{5,1},{2,6},{6,2},{3,7},{7,3},{8,12},{12,8},{9,1... | collective-permute-start | bytes 786440 | tf_op jit(solution)/shard_map/ppermute | solution.py:451
  (85 other events, 1290.6 us)
Sparse Core Ops, SparseCore 0:
  12.3 39.2 all-gather.4
  55.1 114.1 all-gather.6
  172.8 76.1 all-gather.8
  291.3 161.8 reduce-scatter.8
  458.7 113.8 reduce-scatter.6
  612.8 137.7 all-reduce.3
  752.7 21.8 all-gather.10

commit v2 on v1

v2 whole, which is shorter than its diff:
```python
import math

import jax
import jax.numpy as jnp
from jax import lax
from jax.experimental.layout import Layout, with_layout_constraint
from jax.sharding import PartitionSpec as P

CF_DF_TO_CD = "cf,df->cd"
CTX = "ctx"
ECD_ECF_TO_EDF = "ecd,ecf->edf"
ECD_EDF_TO_ECF = "ecd,edf->ecf"
ECF_EDF_TO_ECD = "ecf,edf->ecd"
FSDP = "fsdp"
KGTD_SKD_TO_KGTS = "kgtd,skd->kgts"
KGTS_KGTD_TO_SKD = "kgts,kgtd->skd"
KGTS_SKD_TO_KGTD = "kgts,skd->kgtd"
KGTS_SKD_TO_TKGD = "kgts,skd->tkgd"
KGTS_TKGD_TO_SKD = "kgts,tkgd->skd"
TD_ID_TO_TI = "td,id->ti"
TD_TE_TO_DE = "td,te->de"
TD_TF_TO_DF = "td,tf->df"
TE_DE_TO_TD = "te,de->td"
TF_DF_TO_TD = "tf,df->td"
TKGD_SKD_TO_KGTS = "tkgd,skd->kgts"
TP = "tp"


QUERY_HEADS = 16
KEY_VALUE_HEADS = 8
HEAD_SIZE = 64


EPS = 1e-06
THETA = 10000.0


def shifted(block, axis, distance):
    devices = range(lax.axis_size(axis))
    route = [(i - distance, i) for i in devices if i - distance in devices]
    return lax.ppermute(block, axis, route)


def rope_tables(place_rows, head_width):
    half_width = head_width // 2
    inverse = THETA ** (-2.0 * jnp.arange(half_width, dtype=jnp.float32) / head_width)
    angle = place_rows.astype(jnp.float32)[:, None] * inverse[None, :]
    return (jnp.cos(angle)[:, None, :], jnp.sin(angle)[:, None, :])


def apply_rotary(vector, cosine_lookup, sine_lookup, direction):
    half_width = vector.shape[-1] // 2
    first_half = vector[..., :half_width]
    second_half = vector[..., half_width:]
    return jnp.concatenate(
        [
            first_half * cosine_lookup - direction * second_half * sine_lookup,
            direction * first_half * sine_lookup + second_half * cosine_lookup,
        ],
        axis=-1,
    )


def rms_forward(wide_rows, gain_vector):
    factor = lax.rsqrt(jnp.mean(wide_rows * wide_rows, axis=-1, keepdims=True) + EPS)
    normed = wide_rows * factor
    return (normed, factor, (normed * gain_vector.astype(jnp.float32)).astype(jnp.bfloat16))


def rms_backward(gradient, normed, factor, gain_vector):
    gain_grad = jnp.sum(gradient * normed, axis=0)
    inner_term = gradient * gain_vector.astype(jnp.float32)
    back_term = factor * (
        inner_term - normed * jnp.mean(inner_term * normed, axis=-1, keepdims=True)
    )
    return (back_term, gain_grad)


def attend_mask(query_ids, query_starts, key_ids):
    return (key_ids[None, :] <= query_ids[:, None]) & (key_ids[None, :] >= query_starts[:, None])


def router_gates(logits, picks):
    selected = jnp.sum(jnp.where(picks, logits[:, None, :], 0.0), axis=-1)
    exp_sel = jnp.exp(selected)
    return exp_sel / jnp.sum(exp_sel, axis=-1, keepdims=True)


def slot_tables(route_rows, gate_weights, first_expert, expert_count, capacity):
    token_count = route_rows.shape[0]
    owners = first_expert + jnp.arange(expert_count, dtype=jnp.int32)
    hit_mask = route_rows[:, :, None] == owners[None, None, :]
    member = jnp.sum(hit_mask.astype(jnp.int32), axis=1)
    weight_rows = jnp.sum(jnp.where(hit_mask, gate_weights[:, :, None], 0.0), axis=1)
    places = jnp.cumsum(member, axis=0) - 1
    expert_ids = jnp.arange(expert_count, dtype=jnp.int32)
    slot_ids = jnp.where(
        member > 0, expert_ids[None, :] * capacity + places, expert_count * capacity
    )
    flat_slots = slot_ids.reshape(-1)
    token_ids = jnp.broadcast_to(
        jnp.arange(token_count, dtype=jnp.int32)[:, None], (token_count, expert_count)
    ).reshape(-1)
    source = jnp.zeros((expert_count * capacity + 1,), jnp.int32).at[flat_slots].set(token_ids)[:-1]
    scaled = (
        jnp.zeros((expert_count * capacity + 1,), jnp.float32)
        .at[flat_slots]
        .set(weight_rows.reshape(-1))[:-1]
    )
    return (hit_mask, slot_ids, source, scaled)


def expert_forward(hidden, source, w_gate, w_up, w_down, expert_count, capacity):
    picked = hidden[source].reshape(expert_count, capacity, hidden.shape[1])
    gate_pre = jnp.einsum(ECD_EDF_TO_ECF, picked, w_gate, preferred_element_type=jnp.float32)
    up_pre = jnp.einsum(ECD_EDF_TO_ECF, picked, w_up, preferred_element_type=jnp.float32)
    activation = (jax.nn.silu(gate_pre) * up_pre).astype(jnp.bfloat16)
    result = jnp.einsum(ECF_EDF_TO_ECD, activation, w_down, preferred_element_type=jnp.float32)
    return (picked, gate_pre, up_pre, activation, result)


def combine(result, source, scaled, token_count):
    model_width = result.shape[-1]
    flat_result = result.reshape(-1, model_width)
    return (
        jnp.zeros((token_count, model_width), jnp.float32)
        .at[source]
        .add(flat_result * scaled[:, None])
    )


def expert_backward(
    grad_rows,
    hit_mask,
    slot_ids,
    source,
    scaled,
    saved,
    w_gate,
    w_up,
    w_down,
    expert_count,
    capacity,
    token_count,
):
    picked, gate_pre, up_pre, activation, result = saved
    model_width = grad_rows.shape[1]
    slot_grad = jnp.sum(grad_rows * result.reshape(expert_count * capacity, model_width), axis=1)
    padded = jnp.concatenate([slot_grad, jnp.zeros((1,), jnp.float32)])
    per_expert = padded[slot_ids]
    gate_grad = jnp.sum(jnp.where(hit_mask, per_expert[:, None, :], 0.0), axis=2)
    out_grad = (
        (grad_rows * scaled[:, None])
        .astype(jnp.bfloat16)
        .reshape(expert_count, capacity, model_width)
    )
    grad_down = jnp.einsum(ECD_ECF_TO_EDF, out_grad, activation, preferred_element_type=jnp.float32)
    act_grad = jnp.einsum(ECD_EDF_TO_ECF, out_grad, w_down, preferred_element_type=jnp.float32)
    sigmoid_gate = jax.nn.sigmoid(gate_pre)
    gate_pre_grad = (
        act_grad * up_pre * sigmoid_gate * (1.0 + gate_pre * (1.0 - sigmoid_gate))
    ).astype(jnp.bfloat16)
    up_pre_grad = (act_grad * gate_pre * sigmoid_gate).astype(jnp.bfloat16)
    grad_gate = jnp.einsum(
        ECD_ECF_TO_EDF, picked, gate_pre_grad, preferred_element_type=jnp.float32
    )
    grad_up = jnp.einsum(ECD_ECF_TO_EDF, picked, up_pre_grad, preferred_element_type=jnp.float32)
    picked_grad = jnp.einsum(
        ECF_EDF_TO_ECD, gate_pre_grad, w_gate, preferred_element_type=jnp.float32
    ) + jnp.einsum(ECF_EDF_TO_ECD, up_pre_grad, w_up, preferred_element_type=jnp.float32)
    hidden_grad = (
        jnp.zeros((token_count, model_width), jnp.float32)
        .at[source]
        .add(picked_grad.reshape(-1, model_width))
    )
    return (gate_grad, hidden_grad, grad_gate, grad_up, grad_down)


def local(
    tokens,
    cotangent,
    positions,
    routes,
    attn_gain,
    w_query,
    key_value_projection,
    output_projection_weight,
    ffn_gain,
    w_router,
    w_gate,
    w_up,
    w_down,
):
    gain_one, gain_two, query_full, keyval_full, out_full, router_full = (
        lax.all_gather(attn_gain, FSDP, axis=0, tiled=True),
        lax.all_gather(ffn_gain, FSDP, axis=0, tiled=True),
        lax.all_gather(w_query, FSDP, axis=0, tiled=True),
        lax.all_gather(key_value_projection, FSDP, axis=0, tiled=True),
        lax.all_gather(output_projection_weight, FSDP, axis=1, tiled=True),
        lax.all_gather(w_router, FSDP, axis=0, tiled=True),
    )
    expert_full = (
        lax.all_gather(w_gate, FSDP, axis=1, tiled=True),
        lax.all_gather(w_up, FSDP, axis=1, tiled=True),
        lax.all_gather(w_down, FSDP, axis=1, tiled=True),
    )
    input_rows = tokens[0]
    local_len = input_rows.shape[0]
    model_width = input_rows.shape[1]
    query_group_count = QUERY_HEADS // KEY_VALUE_HEADS
    local_heads = w_query.shape[1] // HEAD_SIZE
    local_kv = local_heads // query_group_count
    expert_count = w_gate.shape[0]
    capacity = local_len // 2
    ctx_count = lax.axis_size(CTX)
    ctx_rank = lax.axis_index(CTX)
    factor = 1.0 / math.sqrt(HEAD_SIZE)
    key_value_weight = keyval_full.reshape(model_width, local_kv * 2 * HEAD_SIZE)
    wide_input = input_rows.astype(jnp.float32)
    normed_one, factor_one, first_hidden_state = rms_forward(wide_input, gain_one)
    query_matrix = jnp.dot(
        first_hidden_state, query_full, preferred_element_type=jnp.float32
    ).reshape(local_len, local_heads, HEAD_SIZE)
    key_value_rows = jnp.dot(
        first_hidden_state, key_value_weight, preferred_element_type=jnp.float32
    ).reshape(local_len, local_kv, 2, HEAD_SIZE)
    place_rows = positions[0]
    cosine_lookup, sine_lookup = rope_tables(place_rows, HEAD_SIZE)
    rotated_query = (
        apply_rotary(query_matrix, cosine_lookup, sine_lookup, 1.0)
        .astype(jnp.bfloat16)
        .reshape(local_len, local_kv, query_group_count, HEAD_SIZE)
    )
    k_rot = apply_rotary(key_value_rows[:, :, 0], cosine_lookup, sine_lookup, 1.0).astype(
        jnp.bfloat16
    )
    v_rows = key_value_rows[:, :, 1].astype(jnp.bfloat16)
    local_ids = jnp.arange(local_len, dtype=jnp.int32)
    query_ids = ctx_rank * local_len + local_ids
    query_starts = query_ids - place_rows
    kv_pack = jnp.concatenate([k_rot, v_rows], axis=-1)
    kv_blocks = [kv_pack]
    key_ids = [query_ids]
    travelling = kv_pack
    cycle_step = 1
    travelling = shifted(travelling, CTX, 1)
    kv_blocks.append(travelling)
    key_ids.append((ctx_rank - cycle_step) * local_len + local_ids)
    row_total = jnp.zeros((local_kv, query_group_count, local_len), jnp.float32)
    weighted = jnp.zeros((local_kv, query_group_count, local_len, HEAD_SIZE), jnp.float32)
    masks = []
    for block_index in range(ctx_count):
        allowed = attend_mask(query_ids, query_starts, key_ids[block_index])
        masks.append(allowed)
        key_rows = kv_blocks[block_index][..., :HEAD_SIZE]
        value_rows = kv_blocks[block_index][..., HEAD_SIZE:]
        scores = (
            jnp.einsum(
                TKGD_SKD_TO_KGTS, rotated_query, key_rows, preferred_element_type=jnp.float32
            )
            * factor
        )
        exp_scores = jnp.where(allowed[None, None], jnp.exp(scores), 0.0)
        row_total = row_total + jnp.sum(exp_scores, axis=-1)
        weighted = weighted + jnp.einsum(
            KGTS_SKD_TO_KGTD,
            exp_scores.astype(jnp.bfloat16),
            value_rows,
            preferred_element_type=jnp.float32,
        )
    head_out = (weighted / row_total[..., None]).astype(jnp.bfloat16)
    flat_heads = head_out.transpose(2, 0, 1, 3).reshape(local_len, local_heads * HEAD_SIZE)
    attn_part = jnp.dot(flat_heads, out_full, preferred_element_type=jnp.float32)
    residual = wide_input + lax.psum(attn_part, TP)
    normed_two, factor_two, hidden_two = rms_forward(residual, gain_two)
    logits = jnp.dot(hidden_two, router_full, preferred_element_type=jnp.float32)
    route_rows = routes[0]
    picks = (
        route_rows[:, :, None] == jnp.arange(router_full.shape[1], dtype=jnp.int32)[None, None, :]
    )
    gate_weights = router_gates(logits, picks)
    first_expert = lax.axis_index(TP) * expert_count
    hit_mask, slot_ids, source, scaled = slot_tables(
        route_rows, gate_weights, first_expert, expert_count, capacity
    )
    saved = expert_forward(
        hidden_two, source, expert_full[0], expert_full[1], expert_full[2], expert_count, capacity
    )
    mixture_part = combine(saved[4], source, scaled, local_len)
    mixture = lax.psum(mixture_part.astype(jnp.bfloat16), TP).astype(jnp.float32)
    out_rows = (residual + mixture).astype(jnp.bfloat16)
    grad_wide = cotangent[0].astype(jnp.float32)
    back_weights = (
        lax.all_gather(w_gate, FSDP, axis=1, tiled=True),
        lax.all_gather(w_up, FSDP, axis=1, tiled=True),
        lax.all_gather(w_down, FSDP, axis=1, tiled=True),
    )
    grad_rows = grad_wide[source]
    gate_grad_part, hidden_grad_part, grad_gate, grad_up, grad_down = expert_backward(
        grad_rows,
        hit_mask,
        slot_ids,
        source,
        scaled,
        saved,
        back_weights[0],
        back_weights[1],
        back_weights[2],
        expert_count,
        capacity,
        local_len,
    )
    hidden_grad_sum, gate_grad = lax.psum((hidden_grad_part, gate_grad_part), TP)
    sel_grad = gate_weights * (
        gate_grad - jnp.sum(gate_weights * gate_grad, axis=-1, keepdims=True)
    )
    logit_grad = jnp.sum(jnp.where(picks, sel_grad[:, :, None], 0.0), axis=1).astype(jnp.bfloat16)
    grad_router = jnp.einsum(
        TD_TE_TO_DE, hidden_two, logit_grad, preferred_element_type=jnp.float32
    )
    hidden_grad = hidden_grad_sum + jnp.einsum(
        TE_DE_TO_TD, logit_grad, router_full, preferred_element_type=jnp.float32
    )
    back_two, grad_ffn_gain = rms_backward(hidden_grad, normed_two, factor_two, gain_two)
    residual_grad = grad_wide + back_two
    residual_gradient_second = residual_grad.astype(jnp.bfloat16)
    grad_out_proj = jnp.einsum(
        "ti,td->id", flat_heads, residual_gradient_second, preferred_element_type=jnp.float32
    )
    per_head_gradient = jnp.einsum(
        TD_ID_TO_TI, residual_gradient_second, out_full, preferred_element_type=jnp.float32
    ).astype(jnp.bfloat16)
    per_head_gradient = per_head_gradient.reshape(
        local_len, local_kv, query_group_count, HEAD_SIZE
    ).transpose(1, 2, 0, 3)
    row_delta = jnp.sum(
        per_head_gradient.astype(jnp.float32) * head_out.astype(jnp.float32), axis=-1
    )
    log_total = jnp.log(row_total)
    query_grad = jnp.zeros((local_len, local_kv, query_group_count, HEAD_SIZE), jnp.float32)
    kv_grads = []
    for block_index in range(ctx_count):
        key_rows = kv_blocks[block_index][..., :HEAD_SIZE]
        value_rows = kv_blocks[block_index][..., HEAD_SIZE:]
        scores = (
            jnp.einsum(
                TKGD_SKD_TO_KGTS, rotated_query, key_rows, preferred_element_type=jnp.float32
            )
            * factor
        )
        probability = jnp.where(
            masks[block_index][None, None], jnp.exp(scores - log_total[..., None]), 0.0
        )
        prob_grad = jnp.einsum(
            KGTD_SKD_TO_KGTS, per_head_gradient, value_rows, preferred_element_type=jnp.float32
        )
        score_grad = (probability * (prob_grad - row_delta[..., None]) * factor).astype(
            jnp.bfloat16
        )
        query_grad = query_grad + jnp.einsum(
            KGTS_SKD_TO_TKGD, score_grad, key_rows, preferred_element_type=jnp.float32
        )
        key_grad = jnp.einsum(
            KGTS_TKGD_TO_SKD, score_grad, rotated_query, preferred_element_type=jnp.float32
        )
        value_gradient = jnp.einsum(
            KGTS_KGTD_TO_SKD,
            probability.astype(jnp.bfloat16),
            per_head_gradient,
            preferred_element_type=jnp.float32,
        )
        kv_grads.append(jnp.concatenate([key_grad, value_gradient], axis=-1))
    cycle_step = 1
    returning = shifted(kv_grads[cycle_step].astype(jnp.bfloat16), CTX, -1).astype(jnp.float32)
    kv_grad_total = kv_grads[0] + returning
    key_backward_rows = apply_rotary(
        kv_grad_total[..., :HEAD_SIZE], cosine_lookup, sine_lookup, -1.0
    )
    key_value_backward = (
        jnp.stack([key_backward_rows, kv_grad_total[..., HEAD_SIZE:]], axis=2)
        .astype(jnp.bfloat16)
        .reshape(local_len, local_kv * 2 * HEAD_SIZE)
    )
    query_back = (
        apply_rotary(
            query_grad.reshape(local_len, local_heads, HEAD_SIZE), cosine_lookup, sine_lookup, -1.0
        )
        .astype(jnp.bfloat16)
        .reshape(local_len, local_heads * HEAD_SIZE)
    )
    grad_query = jnp.einsum(
        TD_TF_TO_DF, first_hidden_state, query_back, preferred_element_type=jnp.float32
    )
    key_value_gradient = jnp.einsum(
        TD_TF_TO_DF, first_hidden_state, key_value_backward, preferred_element_type=jnp.float32
    ).reshape(model_width, local_kv, 2, HEAD_SIZE)
    hidden_one_part = jnp.einsum(
        TF_DF_TO_TD, query_back, query_full, preferred_element_type=jnp.float32
    ) + jnp.einsum(
        TF_DF_TO_TD, key_value_backward, key_value_weight, preferred_element_type=jnp.float32
    )
    hidden_one_grad = lax.psum(hidden_one_part.astype(jnp.bfloat16), TP).astype(jnp.float32)
    back_one, grad_attn_gain = rms_backward(hidden_one_grad, normed_one, factor_one, gain_one)
    input_grad = residual_grad + back_one
    shards = (
        lax.psum_scatter(
            grad_attn_gain.astype(jnp.bfloat16), FSDP, scatter_dimension=0, tiled=True
        ).astype(jnp.float32),
        lax.psum_scatter(
            grad_ffn_gain.astype(jnp.bfloat16), FSDP, scatter_dimension=0, tiled=True
        ).astype(jnp.float32),
        lax.psum_scatter(
            grad_query.astype(jnp.bfloat16), FSDP, scatter_dimension=0, tiled=True
        ).astype(jnp.float32),
        lax.psum_scatter(
            key_value_gradient.astype(jnp.bfloat16), FSDP, scatter_dimension=0, tiled=True
        ).astype(jnp.float32),
        lax.psum_scatter(
            grad_out_proj.astype(jnp.bfloat16), FSDP, scatter_dimension=1, tiled=True
        ).astype(jnp.float32),
        lax.psum_scatter(
            grad_router.astype(jnp.bfloat16), FSDP, scatter_dimension=0, tiled=True
        ).astype(jnp.float32),
    )
    piece_gate, piece_up, piece_down = (
        lax.psum_scatter(
            grad_gate.astype(jnp.bfloat16), (FSDP, CTX), scatter_dimension=1, tiled=True
        ).astype(jnp.float32),
        lax.psum_scatter(
            grad_up.astype(jnp.bfloat16), (FSDP, CTX), scatter_dimension=1, tiled=True
        ).astype(jnp.float32),
        lax.psum_scatter(
            grad_down.astype(jnp.bfloat16), (FSDP, CTX), scatter_dimension=1, tiled=True
        ).astype(jnp.float32),
    )
    expert_totals = (
        lax.all_gather(piece_gate.astype(jnp.bfloat16), CTX, axis=1, tiled=True).astype(
            piece_gate.dtype
        ),
        lax.all_gather(piece_up.astype(jnp.bfloat16), CTX, axis=1, tiled=True).astype(
            piece_up.dtype
        ),
        lax.all_gather(piece_down.astype(jnp.bfloat16), CTX, axis=1, tiled=True).astype(
            piece_down.dtype
        ),
    )
    small_totals = (
        lax.psum(shards[0].astype(jnp.bfloat16), CTX).astype(jnp.float32),
        lax.psum(shards[1].astype(jnp.bfloat16), CTX).astype(jnp.float32),
        lax.psum(shards[2].astype(jnp.bfloat16), CTX).astype(jnp.float32),
        lax.psum(shards[3].astype(jnp.bfloat16), CTX).astype(jnp.float32),
        lax.psum(shards[4].astype(jnp.bfloat16), CTX).astype(jnp.float32),
        lax.psum(shards[5].astype(jnp.bfloat16), CTX).astype(jnp.float32),
    )
    return (
        out_rows[None],
        input_grad[None],
        small_totals[0],
        small_totals[2],
        small_totals[3],
        small_totals[4],
        small_totals[1],
        small_totals[5],
        expert_totals[0],
        expert_totals[1],
        expert_totals[2],
    )


def rotated(block, axis, distance):
    count = lax.axis_size(axis)
    return lax.ppermute(block, axis, [(i, (i + distance) % count) for i in range(count)])


def pick_block(stacked, index):
    return lax.dynamic_index_in_dim(stacked, index, 0, keepdims=False)


def sum_over_tp(part, shared=None):
    count = lax.axis_size(TP)
    pieces = part.astype(jnp.bfloat16).reshape(count, part.shape[0] // count, part.shape[1])
    if shared is not None:
        shared = jnp.pad(shared.astype(jnp.bfloat16)[None, None], ((0, 0), (0, 15), (0, 0)))
        shared = jnp.broadcast_to(shared, (count,) + shared.shape[1:])
        pieces = jnp.concatenate([pieces, shared], axis=1)
    pieces = lax.all_to_all(pieces, TP, 0, 0, tiled=True)
    return jnp.sum(pieces.astype(jnp.float32), axis=0)


def row_major(rows):
    return with_layout_constraint(rows, Layout(major_to_minor=tuple(range(rows.ndim))))


def after(value, earlier):
    return lax.optimization_barrier((value, earlier))[0]


def in_order(pieces, axis, place=0):
    count = lax.axis_size(axis)
    rank = lax.axis_index(axis)
    shape = pieces[0].shape
    whole = jnp.zeros(shape[:place] + (count,) + shape[place:], pieces[0].dtype)
    for step in range(count):
        whole = lax.dynamic_update_index_in_dim(
            whole, pieces[step], (rank - step) % count, place
        )
    return whole


def all_steps(block, axis):
    return [block] + [rotated(block, axis, step) for step in range(1, lax.axis_size(axis))]


def tp_partner(block, distance):
    count = lax.axis_size(TP)
    return lax.ppermute(block, TP, [(i, i ^ distance) for i in range(count)])


def tp_stages():
    distances = []
    distance = lax.axis_size(TP) // 2
    while distance:
        distances.append(distance)
        distance //= 2
    return distances


def spread(pieces):
    far, *near = tp_stages()
    result = []
    for flip, block in enumerate(halves(in_order(pieces, FSDP))):
        done = [FSDP]
        for stage in ([far, CTX] if flip else [CTX, far]) + near:
            place = sum(1 for other in done if rank_of(other) < rank_of(stage))
            if isinstance(stage, str):
                pieces = all_steps(block, stage)
            else:
                pieces = [block, tp_partner(block, stage)]
            if isinstance(stage, str):
                block = in_order(pieces, stage, place)
            else:
                bit = (lax.axis_index(TP) // stage) % 2
                shape = block.shape
                whole = jnp.zeros(shape[:place] + (2,) + shape[place:], block.dtype)
                whole = lax.dynamic_update_index_in_dim(whole, pieces[0], bit, place)
                block = lax.dynamic_update_index_in_dim(whole, pieces[1], 1 - bit, place)
            done.append(stage)
        result.append(block)
    return result


def rank_of(stage):
    return {FSDP: 0, CTX: 1}[stage] if isinstance(stage, str) else 2 + 1.0 / stage


def collect(parts):
    far, *near = tp_stages()
    summed = []
    for flip, stacked in enumerate(parts):
        stages = list(reversed(near)) + ([CTX, far] if flip else [far, CTX])
        left = sorted(stages + [FSDP], key=rank_of)
        for stage in stages:
            place = left.index(stage)
            left.remove(stage)
            if isinstance(stage, str):
                count = lax.axis_size(stage)
                rank = lax.axis_index(stage)
                pieces = [lax.dynamic_index_in_dim(stacked, rank, place, keepdims=False)]
                for step in range(1, count):
                    leaving = lax.dynamic_index_in_dim(
                        stacked, (rank + step) % count, place, keepdims=False
                    )
                    pieces.append(rotated(leaving, stage, step))
            else:
                bit = (lax.axis_index(TP) // stage) % 2
                leaving = lax.dynamic_index_in_dim(stacked, 1 - bit, place, keepdims=False)
                pieces = [
                    lax.dynamic_index_in_dim(stacked, bit, place, keepdims=False),
                    tp_partner(leaving, stage),
                ]
            total = sum(piece.astype(jnp.float32) for piece in pieces)
            stacked = total.astype(jnp.bfloat16)
        summed.append(stacked)
    pieces = scatter_start(jnp.concatenate(summed, axis=-1))
    return sum(piece.astype(jnp.float32) for piece in pieces)


def halves(rows):
    width = rows.shape[-1] // 2
    return rows[..., :width], rows[..., width:]


def scatter_start(stacked):
    count = lax.axis_size(FSDP)
    rank = lax.axis_index(FSDP)
    pieces = [pick_block(stacked, rank)]
    for step in range(1, count):
        pieces.append(rotated(pick_block(stacked, (rank + step) % count), FSDP, step))
    return pieces


def scatter_finish(pieces):
    total = sum(piece.astype(jnp.float32) for piece in pieces)
    sent = total.astype(jnp.bfloat16)
    for step in range(1, lax.axis_size(CTX)):
        total = total + rotated(sent, CTX, step).astype(jnp.float32)
    return total


def local_spread(
    tokens,
    cotangent,
    positions,
    routes,
    attn_gain,
    w_query,
    key_value_projection,
    output_projection_weight,
    ffn_gain,
    w_router,
    w_gate,
    w_up,
    w_down,
):
    everywhere = (FSDP, CTX, TP)
    fsdp_count, ctx_count, tp_count = (lax.axis_size(name) for name in everywhere)
    fsdp_rank, ctx_rank, tp_rank = (lax.axis_index(name) for name in everywhere)
    input_rows = tokens[0]
    local_len, model_width = input_rows.shape
    slice_width = w_query.shape[0]
    own_len = local_len // tp_count
    block_count = fsdp_count * ctx_count
    expert_total = w_router.shape[1]
    ff_width = w_gate.shape[2]
    query_group_count = QUERY_HEADS // KEY_VALUE_HEADS
    head_width = w_query.shape[1]
    local_heads = head_width // HEAD_SIZE
    local_kv = local_heads // query_group_count
    capacity = local_len // 2
    factor = 1.0 / math.sqrt(HEAD_SIZE)
    own_start = tp_rank * own_len

    def own_rows(rows):
        return lax.dynamic_slice_in_dim(rows, own_start, own_len, 0)

    route_rows = own_rows(routes[0])
    kv_width = key_value_projection.shape[1] * 2 * HEAD_SIZE
    side = jnp.concatenate([w_router, attn_gain[:, None], ffn_gain[:, None]], axis=1)
    side = jnp.pad(side, ((0, 0), (0, -side.shape[1] % 128)))
    packed = jnp.concatenate(
        [w_query, key_value_projection.reshape(slice_width, kv_width), side], axis=1
    )
    packed_parts = all_steps(row_major(packed), FSDP)
    both_width = head_width + kv_width
    both_weight = in_order([p[:, :both_width] for p in packed_parts], FSDP).reshape(
        model_width, both_width
    )
    both_weight = row_major(both_weight)
    side_full = in_order([p[:, both_width:] for p in packed_parts], FSDP).reshape(
        model_width, side.shape[1]
    )
    out_parts = all_steps(after(output_projection_weight, packed_parts), FSDP)
    out_full = (
        in_order(out_parts, FSDP).transpose(1, 0, 2).reshape(head_width, model_width)
    )
    query_full = both_weight[:, :head_width]
    key_value_weight = both_weight[:, head_width:]
    router_full = side_full[:, :expert_total]
    gain_one = side_full[:, expert_total]
    gain_two = side_full[:, expert_total + 1]

    route_tail = jnp.pad(
        route_rows.astype(jnp.bfloat16), ((0, 0), (0, -route_rows.shape[1] % 256))
    )
    carried = jnp.concatenate([own_rows(cotangent[0]), route_tail], axis=1)
    grad_pieces = all_steps(after(carried, out_parts), FSDP)

    def weight_packet(weights, earlier):
        packets = []
        for step in range(fsdp_count):
            index = ((fsdp_rank + step) % fsdp_count) * ctx_count + ctx_rank
            packet = jnp.stack([pick_block(weight, index) for weight in weights])
            if step:
                packet = after(packet, earlier)
                packet = rotated(packet, FSDP, step)
            packets.append(packet)
        return packets

    def whole_weights(packets):
        return [
            in_order([packet[kind] for packet in packets], FSDP).reshape(
                fsdp_count * slice_width, ff_width
            )
            for kind in range(packets[0].shape[0])
        ]

    wide_input = input_rows.astype(jnp.float32)
    normed_one, factor_one, first_hidden_state = rms_forward(wide_input, gain_one)
    query_matrix = jnp.dot(
        first_hidden_state, query_full, preferred_element_type=jnp.float32
    ).reshape(local_len, local_heads, HEAD_SIZE)
    key_value_rows = jnp.dot(
        first_hidden_state, key_value_weight, preferred_element_type=jnp.float32
    ).reshape(local_len, local_kv, 2, HEAD_SIZE)
    place_rows = positions[0]
    cosine_lookup, sine_lookup = rope_tables(place_rows, HEAD_SIZE)
    rotated_query = (
        apply_rotary(query_matrix, cosine_lookup, sine_lookup, 1.0)
        .astype(jnp.bfloat16)
        .reshape(local_len, local_kv, query_group_count, HEAD_SIZE)
    )
    k_rot = apply_rotary(key_value_rows[:, :, 0], cosine_lookup, sine_lookup, 1.0).astype(
        jnp.bfloat16
    )
    v_rows = key_value_rows[:, :, 1].astype(jnp.bfloat16)
    local_ids = jnp.arange(local_len, dtype=jnp.int32)
    query_ids = ctx_rank * local_len + local_ids
    query_starts = query_ids - place_rows
    kv_pack = jnp.concatenate([k_rot, v_rows], axis=-1)
    kv_blocks = [kv_pack]
    key_ids = [query_ids]
    for step in range(1, ctx_count):
        kv_blocks.append(shifted(kv_blocks[-1], CTX, 1))
        key_ids.append((ctx_rank - step) * local_len + local_ids)
    row_total = jnp.zeros((local_kv, query_group_count, local_len), jnp.float32)
    weighted = jnp.zeros((local_kv, query_group_count, local_len, HEAD_SIZE), jnp.float32)
    masks = []
    for block_index in range(ctx_count):
        allowed = attend_mask(query_ids, query_starts, key_ids[block_index])
        masks.append(allowed)
        key_rows = kv_blocks[block_index][..., :HEAD_SIZE]
        value_rows = kv_blocks[block_index][..., HEAD_SIZE:]
        scores = (
            jnp.einsum(
                TKGD_SKD_TO_KGTS, rotated_query, key_rows, preferred_element_type=jnp.float32
            )
            * factor
        )
        exp_scores = jnp.where(allowed[None, None], jnp.exp(scores), 0.0)
        row_total = row_total + jnp.sum(exp_scores, axis=-1)
        weighted = weighted + jnp.einsum(
            KGTS_SKD_TO_KGTD,
            exp_scores.astype(jnp.bfloat16),
            value_rows,
            preferred_element_type=jnp.float32,
        )
    head_out = (weighted / row_total[..., None]).astype(jnp.bfloat16)
    flat_heads = head_out.transpose(2, 0, 1, 3).reshape(local_len, local_heads * HEAD_SIZE)
    attn_part = jnp.dot(flat_heads, out_full, preferred_element_type=jnp.float32)

    attn_total = sum_over_tp(attn_part)
    residual = own_rows(input_rows).astype(jnp.float32) + attn_total
    normed_two, factor_two, hidden_two = rms_forward(residual, gain_two)
    hidden_pieces = all_steps(hidden_two, FSDP)
    grad_halves = [
        half.reshape(block_count, local_len, half.shape[-1])
        for half in spread(after(grad_pieces, hidden_two))
    ]
    hidden_halves = [
        half.reshape(block_count, local_len, half.shape[-1])
        for half in spread(hidden_pieces)
    ]
    tail_start = grad_halves[1].shape[-1] - route_tail.shape[1]
    routes_all = grad_halves[1][:, :, tail_start : tail_start + route_rows.shape[1]]
    routes_all = routes_all.astype(jnp.int32).reshape(-1, route_rows.shape[1])
    expert_ids = jnp.arange(expert_total, dtype=jnp.int32)
    chosen_all = jnp.any(routes_all[:, :, None] == expert_ids[None, None, :], axis=1)
    own_expert = tp_rank * block_count + fsdp_rank * ctx_count + ctx_rank
    member = jnp.any(routes_all == own_expert, axis=1).reshape(block_count, local_len)
    places = jnp.cumsum(member.astype(jnp.int32), axis=1) - 1
    slots = jnp.where(member, places, capacity)
    slot_ids = jnp.arange(capacity, dtype=jnp.int32)
    hot = slots[:, None, :] == slot_ids[None, :, None]
    hot_b = hot.astype(jnp.bfloat16)

    def take_rows(rows):
        return (
            jnp.einsum("bst,btd->bsd", hot_b, rows, preferred_element_type=jnp.float32)
            .astype(jnp.bfloat16)
            .reshape(block_count * capacity, rows.shape[2])
        )

    slot_chosen = take_rows(
        chosen_all.astype(jnp.bfloat16).reshape(block_count, local_len, expert_total)
    ).astype(jnp.float32)

    def put_rows(rows):
        stacked = rows.reshape(block_count, capacity, rows.shape[1])
        return (
            jnp.einsum("bst,bsd->btd", hot_b, stacked, preferred_element_type=jnp.float32)
            .astype(jnp.bfloat16)
            .reshape(
                (fsdp_count, ctx_count)
                + (2,) * len(tp_stages())
                + (own_len, rows.shape[1])
            )
        )

    first_packets = weight_packet((w_gate, w_up), hidden_pieces)
    down_packets = weight_packet((w_down,), hidden_pieces)
    hidden_halves, first_packets, down_packets = lax.optimization_barrier(
        (hidden_halves, first_packets, down_packets)
    )
    gate_weight, up_weight = whole_weights(first_packets)
    (down_weight,) = whole_weights(down_packets)
    own_chosen = jnp.any(route_rows[:, :, None] == expert_ids[None, None, :], axis=1)

    def exp_logits(hidden, chosen):
        logits = jnp.dot(hidden, router_full, preferred_element_type=jnp.float32)
        return jnp.where(chosen, jnp.exp(logits), 0.0)

    own_exp = exp_logits(hidden_two, own_chosen)
    own_gates = own_exp / jnp.sum(own_exp, axis=-1, keepdims=True)

    picked = jnp.concatenate([take_rows(half) for half in hidden_halves], axis=1)
    slot_exp = exp_logits(picked, slot_chosen > 0)
    slot_live = jnp.sum(slot_chosen, axis=1) > 0
    slot_total = jnp.where(slot_live, jnp.sum(slot_exp, axis=1), 1.0)
    slot_own = jnp.sum(jnp.where(expert_ids[None, :] == own_expert, slot_exp, 0.0), axis=1)
    scaled = jnp.where(slot_live, slot_own / slot_total, 0.0)
    gate_pre = jnp.dot(picked, gate_weight, preferred_element_type=jnp.float32)
    up_pre = jnp.dot(picked, up_weight, preferred_element_type=jnp.float32)
    activation = (jax.nn.silu(gate_pre) * up_pre).astype(jnp.bfloat16)
    result = jnp.einsum(CF_DF_TO_CD, activation, down_weight, preferred_element_type=jnp.float32)

    mixture_rows = (result * scaled[:, None]).astype(jnp.bfloat16)

    grad_rows = jnp.concatenate([take_rows(half) for half in grad_halves], axis=1)
    grad_rows = grad_rows[:, :model_width]
    grad_wide_rows = grad_rows.astype(jnp.float32)
    slot_grad = jnp.sum(grad_wide_rows * result, axis=1).reshape(block_count, capacity)
    out_grad = row_major((grad_wide_rows * scaled[:, None]).astype(jnp.bfloat16))
    act_grad = jnp.dot(out_grad, down_weight, preferred_element_type=jnp.float32)
    sigmoid_gate = jax.nn.sigmoid(gate_pre)
    gate_pre_grad = (
        act_grad * up_pre * sigmoid_gate * (1.0 + gate_pre * (1.0 - sigmoid_gate))
    ).astype(jnp.bfloat16)
    up_pre_grad = (act_grad * gate_pre * sigmoid_gate).astype(jnp.bfloat16)
    picked_grad = jnp.einsum(
        CF_DF_TO_CD, gate_pre_grad, gate_weight, preferred_element_type=jnp.float32
    ) + jnp.einsum(CF_DF_TO_CD, up_pre_grad, up_weight, preferred_element_type=jnp.float32)
    gate_grad_part = jnp.sum(jnp.where(hot, slot_grad[:, :, None], 0.0), axis=1)
    gate_grad = lax.all_to_all(
        gate_grad_part.reshape(block_count * tp_count, own_len), everywhere, 0, 0, tiled=True
    )
    gate_grad = (
        gate_grad.reshape(block_count, tp_count, own_len)
        .transpose(2, 1, 0)
        .reshape(own_len, expert_total)
    )
    back_parts = [put_rows(half) for half in halves(picked_grad.astype(jnp.bfloat16))]
    (back_parts, picked, gate_pre_grad, up_pre_grad, out_grad, activation, mixture_rows) = (
        lax.optimization_barrier(
            (
                back_parts,
                picked,
                gate_pre_grad,
                up_pre_grad,
                out_grad,
                activation,
                mixture_rows,
            )
        )
    )
    hidden_grad_sum = collect(back_parts)
    mixture = collect([put_rows(half) for half in halves(mixture_rows)])
    own_out = (residual + mixture).astype(jnp.bfloat16)

    def weight_grad(rows, columns):
        return (
            jnp.einsum("cd,cf->df", rows, columns, preferred_element_type=jnp.float32)
            .astype(jnp.bfloat16)
            .reshape(fsdp_count, slice_width, ff_width)
        )

    early_grads = [weight_grad(picked, rows) for rows in (gate_pre_grad, up_pre_grad)]
    late_grads = [weight_grad(out_grad, activation)]
    grad_packets = []
    for kinds in (early_grads, late_grads):
        packets = []
        for step in range(fsdp_count):
            target = (fsdp_rank + step) % fsdp_count
            packet = jnp.stack([pick_block(grad, target) for grad in kinds])
            if step:
                if len(grad_packets):
                    packet = after(packet, hidden_grad_sum)
                packet = rotated(packet, FSDP, step)
            packets.append(packet)
        grad_packets.append(packets)

    sel_grad = own_gates * (
        gate_grad - jnp.sum(own_gates * gate_grad, axis=-1, keepdims=True)
    )
    logit_grad = jnp.where(own_chosen, sel_grad, 0.0).astype(jnp.bfloat16)
    hidden_grad = hidden_grad_sum + jnp.einsum(
        TE_DE_TO_TD, logit_grad, router_full, preferred_element_type=jnp.float32
    )
    back_two, grad_ffn_gain = rms_backward(hidden_grad, normed_two, factor_two, gain_two)
    residual_grad = own_rows(cotangent[0]).astype(jnp.float32) + back_two
    row_pad = 16
    sent = jnp.concatenate(
        [
            residual_grad.astype(jnp.bfloat16),
            jnp.pad(grad_ffn_gain.astype(jnp.bfloat16)[None], ((0, row_pad - 1), (0, 0))),
        ],
        axis=0,
    )
    logit_tail = jnp.pad(logit_grad, ((0, row_pad), (0, -expert_total % 128)))
    sent = lax.all_gather(jnp.concatenate([sent, logit_tail], axis=1), TP, axis=0)
    residual_gradient_second = sent[:, :own_len, :model_width].reshape(local_len, model_width)
    logit_grad = sent[:, :own_len, model_width : model_width + expert_total].reshape(
        local_len, expert_total
    )
    grad_ffn_gain = jnp.sum(sent[:, own_len, :model_width].astype(jnp.float32), axis=0)
    own_block = fsdp_rank * ctx_count + ctx_rank
    block_hidden = jnp.concatenate(
        [pick_block(half, own_block) for half in hidden_halves], axis=1
    )
    grad_router = jnp.einsum(
        TD_TE_TO_DE, block_hidden, logit_grad, preferred_element_type=jnp.float32
    )

    grad_out_proj = jnp.einsum(
        "td,ti->di", residual_gradient_second, flat_heads, preferred_element_type=jnp.float32
    )
    early = jnp.concatenate([grad_out_proj, grad_router, grad_ffn_gain[:, None]], axis=1)
    early = jnp.pad(early, ((0, 0), (0, -early.shape[1] % 128))).astype(jnp.bfloat16)
    early = early.reshape(fsdp_count, slice_width, early.shape[1])
    early_parts = scatter_start(early)
    per_head_gradient = jnp.einsum(
        TD_ID_TO_TI, residual_gradient_second, out_full, preferred_element_type=jnp.float32
    ).astype(jnp.bfloat16)
    per_head_gradient = per_head_gradient.reshape(
        local_len, local_kv, query_group_count, HEAD_SIZE
    ).transpose(1, 2, 0, 3)
    row_delta = jnp.sum(
        per_head_gradient.astype(jnp.float32) * head_out.astype(jnp.float32), axis=-1
    )
    log_total = jnp.log(row_total)
    query_grad = jnp.zeros((local_len, local_kv, query_group_count, HEAD_SIZE), jnp.float32)
    kv_grads = []
    for block_index in range(ctx_count):
        key_rows = kv_blocks[block_index][..., :HEAD_SIZE]
        value_rows = kv_blocks[block_index][..., HEAD_SIZE:]
        scores = (
            jnp.einsum(
                TKGD_SKD_TO_KGTS, rotated_query, key_rows, preferred_element_type=jnp.float32
            )
            * factor
        )
        probability = jnp.where(
            masks[block_index][None, None], jnp.exp(scores - log_total[..., None]), 0.0
        )
        prob_grad = jnp.einsum(
            KGTD_SKD_TO_KGTS, per_head_gradient, value_rows, preferred_element_type=jnp.float32
        )
        score_grad = (probability * (prob_grad - row_delta[..., None]) * factor).astype(
            jnp.bfloat16
        )
        query_grad = query_grad + jnp.einsum(
            KGTS_SKD_TO_TKGD, score_grad, key_rows, preferred_element_type=jnp.float32
        )
        key_grad = jnp.einsum(
            KGTS_TKGD_TO_SKD, score_grad, rotated_query, preferred_element_type=jnp.float32
        )
        value_gradient = jnp.einsum(
            KGTS_KGTD_TO_SKD,
            probability.astype(jnp.bfloat16),
            per_head_gradient,
            preferred_element_type=jnp.float32,
        )
        kv_grads.append(jnp.concatenate([key_grad, value_gradient], axis=-1))
    weight_shape = (fsdp_count, ctx_count, slice_width, ff_width)
    weight_outs = [jnp.zeros(weight_shape, jnp.float32) for _ in range(3)]
    weight_hops = []
    for step in range(fsdp_count):
        early_hops = all_steps(grad_packets[0][step], CTX)
        late_hops = all_steps(grad_packets[1][step], CTX)
        weight_hops.append((early_hops, late_hops))
    kv_grad_total = kv_grads[0]
    for step in range(1, ctx_count):
        returning = shifted(kv_grads[step].astype(jnp.bfloat16), CTX, -step)
        kv_grad_total = kv_grad_total + returning.astype(jnp.float32)
    key_backward_rows = apply_rotary(
        kv_grad_total[..., :HEAD_SIZE], cosine_lookup, sine_lookup, -1.0
    )
    key_value_backward = (
        jnp.stack([key_backward_rows, kv_grad_total[..., HEAD_SIZE:]], axis=2)
        .astype(jnp.bfloat16)
        .reshape(local_len, kv_width)
    )
    query_back = (
        apply_rotary(
            query_grad.reshape(local_len, local_heads, HEAD_SIZE), cosine_lookup, sine_lookup, -1.0
        )
        .astype(jnp.bfloat16)
        .reshape(local_len, head_width)
    )
    both_back = jnp.concatenate([query_back, key_value_backward], axis=1)
    hidden_one_part = jnp.einsum(
        TF_DF_TO_TD, both_back, both_weight, preferred_element_type=jnp.float32
    )
    grad_attn_gain = jnp.sum(hidden_one_part * normed_one, axis=0)
    projection_grad = jnp.einsum(
        TD_TF_TO_DF, first_hidden_state, both_back, preferred_element_type=jnp.float32
    )
    projection_grad = projection_grad.astype(jnp.bfloat16).reshape(
        fsdp_count, slice_width, both_width
    )
    projection_parts = scatter_start(projection_grad)
    summed = sum_over_tp(hidden_one_part, grad_attn_gain)
    hidden_one_grad = summed[:own_len]
    grad_attn_gain = summed[own_len].astype(jnp.bfloat16).reshape(fsdp_count, 1, slice_width)
    gain_parts = scatter_start(grad_attn_gain)
    grad_attn_gain = scatter_finish(gain_parts)[0]
    early_total = scatter_finish(after(early_parts, hidden_one_grad))
    out_rows = lax.all_gather(own_out, TP, axis=0, tiled=True)
    projection_total = scatter_finish(after(projection_parts, (hidden_one_grad, out_rows)))
    for step in range(fsdp_count):
        for hops, kinds in zip(weight_hops[step], ((0, 1), (2,))):
            for hop, seen in enumerate(hops):
                seen = after(seen, hidden_one_part)
                place = ((fsdp_rank - step) % fsdp_count, (ctx_rank - hop) % ctx_count, 0, 0)
                for number, kind in enumerate(kinds):
                    weight_outs[kind] = lax.dynamic_update_slice(
                        weight_outs[kind], seen[number].astype(jnp.float32)[None, None], place
                    )
    weight_outs = [
        grad.reshape(fsdp_count * ctx_count, slice_width, ff_width) for grad in weight_outs
    ]
    back_one, _ = rms_backward(
        hidden_one_grad, own_rows(normed_one), own_rows(factor_one), gain_one
    )
    input_grad = residual_grad + back_one
    input_grad = lax.all_gather(
        after(input_grad.astype(jnp.bfloat16), gain_parts), TP, axis=0, tiled=True
    )
    return (
        out_rows[None],
        input_grad.astype(jnp.float32)[None],
        grad_attn_gain,
        projection_total[:, :head_width],
        projection_total[:, head_width:].reshape(key_value_projection.shape),
        early_total[:, :head_width].T,
        early_total[:, head_width + expert_total],
        early_total[:, head_width : head_width + expert_total],
        weight_outs[0],
        weight_outs[1],
        weight_outs[2],
    )


def local_any(*args):
    devices = math.prod(lax.axis_size(name) for name in (FSDP, CTX, TP))
    if args[9].shape[1] != devices:
        return local(*args)
    return local_spread(*args)


def solution(mesh):

    return jax.shard_map(
        local_any,
        mesh=mesh,
        in_specs=(
            P(FSDP, CTX, None),
            P(FSDP, CTX, None),
            P(FSDP, CTX),
            P(FSDP, CTX, None),
            P(FSDP),
            P(FSDP, TP),
            P(FSDP, TP, None, None),
            P(TP, FSDP),
            P(FSDP),
            P(FSDP, None),
            P(TP, FSDP, None),
            P(TP, FSDP, None),
            P(TP, FSDP, None),
        ),
        out_specs=(
            P(FSDP, CTX, None),
            P(FSDP, CTX, None),
            P(FSDP),
            P(FSDP, TP),
            P(FSDP, TP, None, None),
            P(TP, FSDP),
            P(FSDP),
            P(FSDP, None),
            P(TP, FSDP, None),
            P(TP, FSDP, None),
            P(TP, FSDP, None),
        ),
        check_vma=False,
    )
```

time: 818 us -> 599 us (0.73)
  waiting for transfers between devices: 501 us -> 199 us
  starting transfers between devices: 39.7 us -> 144 us
  blocking collectives: 88.2 us -> 26.4 us
  local copies, waits for them, and re-layouts: 40.6 us -> 83.7 us
  other arithmetic: 56.4 us -> 72.8 us
  between operations: 16.1 us -> 4.01 us
  matrix products: 68.4 us -> 60 us
    reduce_scatter x2 -> x0, waiting for transfers between devices: 174 us -> none  [the longest x1 118 us: local_spread(): lax.psum_scatter(mixture_part, everywhere, scatter_dimension=0, tiled=True)]
    all_gather x4 -> x0, waiting for transfers between devices: 89.8 us -> none  [the longest x1 71.9 us: local_spread(): hidden_all = lax.all_gather(hidden_two, everywhere, axis=0, tiled=True)]
    ppermute x18 -> x58, starting transfers between devices: 26.9 us -> 116 us  [rotated(): lax.ppermute(block, axis, [(i, (i + distance) % count) for i in range(cou...]
    psum x1 -> x0, waiting for transfers between devices: 87.6 us -> none  [local_spread(): lax.psum(jnp.concatenate([grad_router, grad_ffn_gain[None]], axis=0), eve...]
    ppermute x0 -> x16, waiting for transfers between devices: none -> 54.3 us  [tp_partner(): return lax.ppermute(block, TP, [(i, i ^ distance) for i in range(count)])]
    psum x1 -> x0, blocking collectives: 42.7 us -> none  [local_spread(): lax.psum(jnp.sum(hidden_one_part * normed_one, axis=0), everywhere)]
    dynamic_update_slice x5 -> x52, local copies, waits for them, and re-layouts: 4.94 us -> 24 us  [the longest x36 16.3 us: in_order(): lax.dynamic_update_index_in_dim(whole, pieces[step], (rank - step) % coun...]
    all_to_all x1 -> x0, blocking collectives: 14.2 us -> none  [sum_over_tp(): pieces = lax.all_to_all(pieces, 'tp', 0, 0, tiled=True)]
  transfers between devices with their start and end apart: 29 -> 79, of which waited for: 16 -> 25; matrix products, arithmetic and copies ran while one was open for 14% -> 25% of each run, Pallas kernels for 0% -> 0%
where the time goes in v2:
time: 599 us; the launch traced here: 589 us
  waiting for transfers between devices  199 us (33%)
  starting transfers between devices  144 us (24%)
  local copies, waits for them, and re-layouts  83.7 us (14%)
  other arithmetic  72.8 us (12%)
  matrix products  60 us (10%)
  blocking collectives  26.4 us (4%)
    ppermute x58, waiting for transfers between devices, rotated(): lax.ppermute(block, axis, [(i, (i + distance) % count) for i in range(cou...  139 us
    ppermute x58, starting transfers between devices, rotated(): lax.ppermute(block, axis, [(i, (i + distance) % count) for i in range(cou...  116 us
    ppermute x16, waiting for transfers between devices, tp_partner(): return lax.ppermute(block, TP, [(i, i ^ distance) for i in range(count)])  54.3 us
    unnamed x228, local copies, waits for them, and re-layouts  18.2 us
    dynamic_update_slice x17, other arithmetic, local_spread(): lax.dynamic_update_slice(weight_outs[kind], seen[number].astype(jnp.float...  17.8 us
    dynamic_update_slice x36, local copies, waits for them, and re-layouts, in_order(): lax.dynamic_update_index_in_dim(whole, pieces[step], (rank - step) % coun...  16.3 us
    ppermute x16, starting transfers between devices, tp_partner(): return lax.ppermute(block, TP, [(i, i ^ distance) for i in range(count)])  12.6 us
  transfers between devices with their start and end apart: 79, of which 25 were waited for; matrix products, arithmetic and copies ran while one was open for 25% of the time, Pallas kernels for 0%

profile of v2, /device:TPU:0, one launch (start us, length us, event | category | flops | bytes accessed | tf_op | source)
XLA Modules:
  0.0 589.5 jit_solution(6387988685938288604)
XLA Ops:
  51.4 6.6 %collective-permute-start.4 = (bf16[256,256]{0,1:T(8,128)(2,1)S(1)}, bf16[256,256]{0,1:T(8,128)(2,1)}, u32[]{:S(2)}, u32[]{:S(2)}) collective-permute-start(bf16[256,256]{0,1:T(8,128)(2,1)S(1)} %copy.245), channel_id=1, source_target_pairs={{0,8},{8,16},{16,24},{24,0},{1,9},{9,17},{17,25},{25,1},{2,10},{10... | collective-permute-start | bytes 393224 | tf_op jit(solution)/shard_map/ppermute | solution.py:472
  85.3 5.3 all-to-all-done
  95.5 6.7 %collective-permute-done.8 = bf16[96,1280]{1,0:T(8,128)(2,1)S(1)} collective-permute-done((bf16[96,1280]{1,0:T(8,128)(2,1)S(1)}, bf16[96,1280]{1,0:T(8,128)(2,1)S(1)}, u32[]{:S(2)}, u32[]{:S(2)}) %collective-permute-start.8) | collective-permute-done | bytes 245792 | tf_op jit(solution)/shard_map/ppermute | solution.py:472
  107.8 11.6 %collective-permute-done.17 = bf16[96,1024]{1,0:T(8,128)(2,1)S(1)} collective-permute-done((bf16[96,1024]{1,0:T(8,128)(2,1)S(1)}, bf16[96,1024]{1,0:T(8,128)(2,1)S(1)}, u32[]{:S(2)}, u32[]{:S(2)}) %collective-permute-start.17) | collective-permute-done | bytes 196640 | tf_op jit(solution)/shard_map/ppermute | solution.py:472
  122.3 4.8 collective-permute-start.25
  137.4 31.8 %collective-permute-done.20 = bf16[4,2,96,512]{3,2,1,0:T(8,128)(2,1)S(1)} collective-permute-done((bf16[4,2,96,512]{3,2,1,0:T(8,128)(2,1)S(1)}, bf16[4,2,96,512]{3,2,1,0:T(8,128)(2,1)S(1)}, u32[]{:S(2)}, u32[]{:S(2)}) %collective-permute-start.20) | collective-permute-done | bytes 786464 | tf_op jit(solution)/shard_map/ppermute | solution.py:516
  172.0 6.0 %collective-permute-start.26 = (bf16[2,256,512]{2,1,0:T(8,128)(2,1)S(1)}, bf16[2,256,512]{2,1,0:T(8,128)(2,1)S(1)}, u32[]{:S(2)}, u32[]{:S(2)}) collective-permute-start(bf16[2,256,512]{2,1,0:T(8,128)(2,1)S(1)} %copy-done.61), channel_id=1, source_target_pairs={{0,16},{8,24},{16,0},{24,8},{1,17},{9,25},{17,1},{25,9},{2,18},{10... | collective-permute-start | bytes 1572872 | tf_op jit(solution)/shard_map/ppermute | solution.py:472
  183.7 15.7 %collective-permute-done.28 = bf16[1,256,512]{2,1,0:T(8,128)(2,1)S(1)} collective-permute-done((bf16[1,256,512]{2,1,0:T(8,128)(2,1)S(1)}, bf16[1,256,512]{2,1,0:T(8,128)(2,1)S(1)}, u32[]{:S(2)}, u32[]{:S(2)}) %collective-permute-start.28) | collective-permute-done | bytes 262176 | tf_op jit(solution)/shard_map/ppermute | solution.py:472
  199.4 21.8 %collective-permute-start.29 = (bf16[1,256,512]{2,1,0:T(8,128)(2,1)S(1)}, bf16[1,256,512]{2,1,0:T(8,128)(2,1)S(1)}, u32[]{:S(2)}, u32[]{:S(2)}) collective-permute-start(bf16[1,256,512]{2,1,0:T(8,128)(2,1)S(1)} %copy-done.74), channel_id=1, source_target_pairs={{0,16},{8,24},{16,0},{24,8},{1,17},{9,25},{17,1},{25,9},{2,18},{10... | collective-permute-start | bytes 786440 | tf_op jit(solution)/shard_map/ppermute | solution.py:472
  221.4 23.2 %collective-permute-done.29 = bf16[1,256,512]{2,1,0:T(8,128)(2,1)S(1)} collective-permute-done((bf16[1,256,512]{2,1,0:T(8,128)(2,1)S(1)}, bf16[1,256,512]{2,1,0:T(8,128)(2,1)S(1)}, u32[]{:S(2)}, u32[]{:S(2)}) %collective-permute-start.29) | collective-permute-done | bytes 262176 | tf_op jit(solution)/shard_map/ppermute | solution.py:472
  244.9 7.0 %collective-permute-done.30 = bf16[1,256,512]{2,1,0:T(8,128)(2,1)S(1)} collective-permute-done((bf16[1,256,512]{2,1,0:T(8,128)(2,1)S(1)}, bf16[1,256,512]{2,1,0:T(8,128)(2,1)S(1)}, u32[]{:S(2)}, u32[]{:S(2)}) %collective-permute-start.30) | collective-permute-done | bytes 262176 | tf_op jit(solution)/shard_map/ppermute | solution.py:472
  295.1 4.3 multiply_convert_fusion.1
  355.4 11.5 %collective-permute-done.41 = bf16[4,2,96,512]{3,2,0,1:T(8,128)(2,1)S(1)} collective-permute-done((bf16[4,2,96,512]{3,2,0,1:T(8,128)(2,1)S(1)}, bf16[4,2,96,512]{3,2,0,1:T(8,128)(2,1)S(1)}, u32[]{:S(2)}, u32[]{:S(2)}) %collective-permute-start.41) | collective-permute-done | bytes 786464 | tf_op jit(solution)/shard_map/ppermute | solution.py:516
  371.3 11.0 %collective-permute-done.32 = bf16[4,2,96,512]{3,2,0,1:T(8,128)(2,1)S(1)} collective-permute-done((bf16[4,2,96,512]{3,2,0,1:T(8,128)(2,1)S(1)}, bf16[4,2,96,512]{3,2,0,1:T(8,128)(2,1)S(1)}, u32[]{:S(2)}, u32[]{:S(2)}) %collective-permute-start.32) | collective-permute-done | bytes 786464 | tf_op jit(solution)/shard_map/ppermute | solution.py:516
  388.2 7.5 %collective-permute-done.42 = bf16[4,96,512]{2,1,0:T(8,128)(2,1)S(1)} collective-permute-done((bf16[4,96,512]{2,1,0:T(8,128)(2,1)S(1)}, bf16[4,96,512]{2,1,0:T(8,128)(2,1)S(1)}, u32[]{:S(2)}, u32[]{:S(2)}) %collective-permute-start.42) | collective-permute-done | bytes 393248 | tf_op jit(solution)/shard_map/ppermute | solution.py:472
  408.1 21.1 %collective-permute-done.47 = bf16[96,1024]{1,0:T(8,128)(2,1)S(1)} collective-permute-done((bf16[96,1024]{1,0:T(8,128)(2,1)S(1)}, bf16[96,1024]{1,0:T(8,128)(2,1)S(1)}, u32[]{:S(2)}, u32[]{:S(2)}) %collective-permute-start.47) | collective-permute-done | bytes 196640 | tf_op jit(solution)/shard_map/ppermute | solution.py:472
  432.4 9.0 %all-gather = bf16[448,1152]{1,0:T(8,128)(2,1)S(1)} all-gather(bf16[112,1152]{1,0:T(8,128)(2,1)S(1)} %fusion.121), channel_id=2, replica_groups=mesh['fsdp'=4,'ctx'=2,'tp'=4] {'tp'}, dimensions={0}, use_global_device_ids=true | all-gather | bytes 1290240 | tf_op jit(solution)/shard_map/all_gather | solution.py:909
  469.3 7.9 %collective-permute-done.64 = bf16[2,256,512]{2,1,0:T(8,128)(2,1)} collective-permute-done((bf16[2,256,512]{2,1,0:T(8,128)(2,1)}, bf16[2,256,512]{2,1,0:T(8,128)(2,1)}, u32[]{:S(2)}, u32[]{:S(2)}) %collective-permute-start.64) | collective-permute-done | bytes 524320 | tf_op jit(solution)/shard_map/ppermute | solution.py:472
  482.3 6.1 %collective-permute-done.66 = bf16[2,256,512]{2,1,0:T(8,128)(2,1)} collective-permute-done((bf16[2,256,512]{2,1,0:T(8,128)(2,1)}, bf16[2,256,512]{2,1,0:T(8,128)(2,1)}, u32[]{:S(2)}, u32[]{:S(2)}) %collective-permute-start.66) | collective-permute-done | bytes 524320 | tf_op jit(solution)/shard_map/ppermute | solution.py:472
  516.9 5.0 collective-permute-done.73
  539.3 8.7 %all_gather.12 = bf16[384,1024]{1,0:T(8,128)(2,1)S(1)} all-gather(bf16[96,1024]{1,0:T(8,128)(2,1)S(1)} %get-tuple-element.270), channel_id=1, replica_groups=mesh['fsdp'=4,'ctx'=2,'tp'=4] {'tp'}, dimensions={0}, use_global_device_ids=true | all-gather | bytes 983040 | tf_op jit(solution)/shard_map/all_gather | solution.py:1017
  548.8 4.8 collective-permute-done.55
  553.7 8.5 %collective-permute-start.50 = (bf16[1,256]{1,0:T(2,128)(2,1)S(1)}, bf16[1,256]{1,0:T(2,128)(2,1)S(1)}, u32[]{:S(2)}, u32[]{:S(2)}) collective-permute-start(bf16[1,256]{1,0:T(2,128)(2,1)S(1)} %get-tuple-element.282), channel_id=1, source_target_pairs={{0,8},{8,16},{16,24},{24,0},{1,9},{9,17},{17,25},{25,1},{2,10},{10... | collective-permute-start | bytes 1544 | tf_op jit(solution)/shard_map/ppermute | solution.py:472
  569.2 8.7 %all_gather.15 = bf16[384,1024]{1,0:T(8,128)(2,1)S(1)} all-gather(bf16[96,1024]{1,0:T(8,128)(2,1)S(1)} %get-tuple-element.94), channel_id=1, replica_groups=mesh['fsdp'=4,'ctx'=2,'tp'=4] {'tp'}, dimensions={0}, use_global_device_ids=true | all-gather | bytes 983040 | tf_op jit(solution)/shard_map/all_gather | solution.py:1035
  (653 shorter events, 330.7 us)
Async XLA Ops:
  122.3 129.7 %collective-permute-start.25 = (bf16[2,256,512]{2,1,0:T(8,128)(2,1)S(1)}, bf16[2,256,512]{2,1,0:T(8,128)(2,1)S(1)}, u32[]{:S(2)}, u32[]{:S(2)}) collective-permute-start(bf16[2,256,512]{2,1,0:T(8,128)(2,1)S(1)} %copy-done.62), channel_id=1, source_target_pairs={{0,8},{8,16},{16,24},{24,0},{1,9},{9,17},{17,25},{25,1},{2,10},{10... | collective-permute-start | bytes 1572872 | tf_op jit(solution)/shard_map/ppermute | solution.py:472
  127.4 43.7 %collective-permute-start.11 = (bf16[4,2,96,640]{3,2,1,0:T(8,128)(2,1)S(1)}, bf16[4,2,96,640]{3,2,1,0:T(8,128)(2,1)S(1)}, u32[]{:S(2)}, u32[]{:S(2)}) collective-permute-start(bf16[4,2,96,640]{3,2,1,0:T(8,128)(2,1)S(1)} %bitcast_dynamic-update-slice_fusion.18), channel_id=1, source_target_pairs={{0,4},{4,0},{1,5},{5,1},{2,6},{6,2},{3,7},{7,3},{8,12},{12,8},{9,1... | collective-permute-start | bytes 2949128 | tf_op jit(solution)/shard_map/ppermute | solution.py:472
  128.6 49.6 %collective-permute-start.14 = (bf16[4,2,96,640]{3,2,1,0:T(8,128)(2,1)S(1)}, bf16[4,2,96,640]{3,2,1,0:T(8,128)(2,1)S(1)}, u32[]{:S(2)}, u32[]{:S(2)}) collective-permute-start(bf16[4,2,96,640]{3,2,1,0:T(8,128)(2,1)S(1)} %bitcast_dynamic-update-slice_fusion.16), channel_id=1, source_target_pairs={{0,2},{1,3},{2,0},{3,1},{4,6},{5,7},{6,4},{7,5},{8,10},{9,11},{10,... | collective-permute-start | bytes 2949128 | tf_op jit(solution)/shard_map/ppermute | solution.py:516
  131.6 37.6 %collective-permute-start.20 = (bf16[4,2,96,512]{3,2,1,0:T(8,128)(2,1)S(1)}, bf16[4,2,96,512]{3,2,1,0:T(8,128)(2,1)S(1)}, u32[]{:S(2)}, u32[]{:S(2)}) collective-permute-start(bf16[4,2,96,512]{3,2,1,0:T(8,128)(2,1)S(1)} %bitcast_dynamic-update-slice_fusion.22), channel_id=1, source_target_pairs={{0,2},{1,3},{2,0},{3,1},{4,6},{5,7},{6,4},{7,5},{8,10},{9,11},{10,... | collective-permute-start | bytes 2359304 | tf_op jit(solution)/shard_map/ppermute | solution.py:516
  135.9 33.5 %collective-permute-start.23 = (bf16[4,2,96,512]{3,2,1,0:T(8,128)(2,1)S(1)}, bf16[4,2,96,512]{3,2,1,0:T(8,128)(2,1)S(1)}, u32[]{:S(2)}, u32[]{:S(2)}) collective-permute-start(bf16[4,2,96,512]{3,2,1,0:T(8,128)(2,1)S(1)} %bitcast_dynamic-update-slice_fusion.20), channel_id=1, source_target_pairs={{0,4},{4,0},{1,5},{5,1},{2,6},{6,2},{3,7},{7,3},{8,12},{12,8},{9,1... | collective-permute-start | bytes 2359304 | tf_op jit(solution)/shard_map/ppermute | solution.py:472
  169.3 30.1 %collective-permute-start.21 = (bf16[4,2,2,96,512]{4,3,2,1,0:T(8,128)(2,1)S(1)}, bf16[4,2,2,96,512]{4,3,2,1,0:T(8,128)(2,1)S(1)}, u32[]{:S(2)}, u32[]{:S(2)}) collective-permute-start(bf16[4,2,2,96,512]{4,3,2,1,0:T(8,128)(2,1)S(1)} %bitcast_dynamic-update-slice_fusion.13), channel_id=1, source_target_pairs={{0,1},{1,0},{2,3},{3,2},{4,5},{5,4},{6,7},{7,6},{8,9},{9,8},{10,11... | collective-permute-start | bytes 4718600 | tf_op jit(solution)/shard_map/ppermute | solution.py:516
  169.5 75.2 %collective-permute-start.24 = (bf16[4,2,2,96,512]{4,3,2,1,0:T(8,128)(2,1)S(1)}, bf16[4,2,2,96,512]{4,3,2,1,0:T(8,128)(2,1)S(1)}, u32[]{:S(2)}, u32[]{:S(2)}) collective-permute-start(bf16[4,2,2,96,512]{4,3,2,1,0:T(8,128)(2,1)S(1)} %bitcast_dynamic-update-slice_fusion.15), channel_id=1, source_target_pairs={{0,1},{1,0},{2,3},{3,2},{4,5},{5,4},{6,7},{7,6},{8,9},{9,8},{10,11... | collective-permute-start | bytes 4718600 | tf_op jit(solution)/shard_map/ppermute | solution.py:516
  172.0 80.0 %collective-permute-start.26 = (bf16[2,256,512]{2,1,0:T(8,128)(2,1)S(1)}, bf16[2,256,512]{2,1,0:T(8,128)(2,1)S(1)}, u32[]{:S(2)}, u32[]{:S(2)}) collective-permute-start(bf16[2,256,512]{2,1,0:T(8,128)(2,1)S(1)} %copy-done.61), channel_id=1, source_target_pairs={{0,16},{8,24},{16,0},{24,8},{1,17},{9,25},{17,1},{25,9},{2,18},{10... | collective-permute-start | bytes 1572872 | tf_op jit(solution)/shard_map/ppermute | solution.py:472
  199.4 52.6 %collective-permute-start.27 = (bf16[2,256,512]{2,1,0:T(8,128)(2,1)S(1)}, bf16[2,256,512]{2,1,0:T(8,128)(2,1)S(1)}, u32[]{:S(2)}, u32[]{:S(2)}) collective-permute-start(bf16[2,256,512]{2,1,0:T(8,128)(2,1)S(1)} %copy-done.63), channel_id=1, source_target_pairs={{0,24},{8,0},{16,8},{24,16},{1,25},{9,1},{17,9},{25,17},{2,26},{10... | collective-permute-start | bytes 1572872 | tf_op jit(solution)/shard_map/ppermute | solution.py:472
  199.4 45.2 %collective-permute-start.29 = (bf16[1,256,512]{2,1,0:T(8,128)(2,1)S(1)}, bf16[1,256,512]{2,1,0:T(8,128)(2,1)S(1)}, u32[]{:S(2)}, u32[]{:S(2)}) collective-permute-start(bf16[1,256,512]{2,1,0:T(8,128)(2,1)S(1)} %copy-done.74), channel_id=1, source_target_pairs={{0,16},{8,24},{16,0},{24,8},{1,17},{9,25},{17,1},{25,9},{2,18},{10... | collective-permute-start | bytes 786440 | tf_op jit(solution)/shard_map/ppermute | solution.py:472
  304.0 36.2 %all-to-all-start.1 = ((f32[32,1,96]{2,1,0:T(1,128)}), f32[32,1,96]{2,1,0:T(1,128)}, u32[]{:S(2)}, u32[]{:S(2)}) async-start(f32[32,1,96]{2,1,0:T(1,128)} %all_to_all.13), calls=%async_computation.1 | async-start | bytes 32768 | tf_op jit(solution)/shard_map/all_to_all | solution.py:843
  332.9 135.3 %collective-permute-start.62 = (bf16[2,256,512]{2,1,0:T(8,128)(2,1)}, bf16[2,256,512]{2,1,0:T(8,128)(2,1)}, u32[]{:S(2)}, u32[]{:S(2)}) collective-permute-start(bf16[2,256,512]{2,1,0:T(8,128)(2,1)} %pad_maximum_fusion.8), channel_id=1, source_target_pairs={{0,4},{4,0},{1,5},{5,1},{2,6},{6,2},{3,7},{7,3},{8,12},{12,8},{9,1... | collective-permute-start | bytes 1572872 | tf_op jit(solution)/shard_map/ppermute | solution.py:472
  342.4 112.7 %collective-permute-start.63 = (bf16[2,256,512]{2,1,0:T(8,128)(2,1)}, bf16[2,256,512]{2,1,0:T(8,128)(2,1)}, u32[]{:S(2)}, u32[]{:S(2)}) collective-permute-start(bf16[2,256,512]{2,1,0:T(8,128)(2,1)} %pad_maximum_fusion.9), channel_id=1, source_target_pairs={{0,8},{8,16},{16,24},{24,0},{1,9},{9,17},{17,25},{25,1},{2,10},{10... | collective-permute-start | bytes 1572872 | tf_op jit(solution)/shard_map/ppermute | solution.py:472
  352.8 29.6 %collective-permute-start.32 = (bf16[4,2,96,512]{3,2,0,1:T(8,128)(2,1)S(1)}, bf16[4,2,96,512]{3,2,0,1:T(8,128)(2,1)S(1)}, u32[]{:S(2)}, u32[]{:S(2)}) collective-permute-start(bf16[4,2,96,512]{3,2,0,1:T(8,128)(2,1)S(1)} %dynamic-slice_bitcast_fusion.3), channel_id=1, source_target_pairs={{0,2},{1,3},{2,0},{3,1},{4,6},{5,7},{6,4},{7,5},{8,10},{9,11},{10,... | collective-permute-start | bytes 2359304 | tf_op jit(solution)/shard_map/ppermute | solution.py:516
  406.5 52.0 %collective-permute-start.65 = (bf16[2,256,512]{2,1,0:T(8,128)(2,1)}, bf16[2,256,512]{2,1,0:T(8,128)(2,1)}, u32[]{:S(2)}, u32[]{:S(2)}) collective-permute-start(bf16[2,256,512]{2,1,0:T(8,128)(2,1)} %pad_maximum_fusion.10), channel_id=1, source_target_pairs={{0,16},{8,24},{16,0},{24,8},{1,17},{9,25},{17,1},{25,9},{2,18},{10... | collective-permute-start | bytes 1572872 | tf_op jit(solution)/shard_map/ppermute | solution.py:472
  429.3 29.3 %collective-permute-start.67 = (bf16[2,256,512]{2,1,0:T(8,128)(2,1)}, bf16[2,256,512]{2,1,0:T(8,128)(2,1)}, u32[]{:S(2)}, u32[]{:S(2)}) collective-permute-start(bf16[2,256,512]{2,1,0:T(8,128)(2,1)} %pad_maximum_fusion.11), channel_id=1, source_target_pairs={{0,24},{8,0},{16,8},{24,16},{1,25},{9,1},{17,9},{25,17},{2,26},{10... | collective-permute-start | bytes 1572872 | tf_op jit(solution)/shard_map/ppermute | solution.py:472
  455.1 46.3 %collective-permute-start.69 = (bf16[1,256,512]{2,1,0:T(8,128)(2,1)}, bf16[1,256,512]{2,1,0:T(8,128)(2,1)}, u32[]{:S(2)}, u32[]{:S(2)}) collective-permute-start(bf16[1,256,512]{2,1,0:T(8,128)(2,1)} %get-tuple-element.116), channel_id=1, source_target_pairs={{0,4},{4,0},{1,5},{5,1},{2,6},{6,2},{3,7},{7,3},{8,12},{12,8},{9,1... | collective-permute-start | bytes 786440 | tf_op jit(solution)/shard_map/ppermute | solution.py:472
  458.6 29.9 %collective-permute-start.66 = (bf16[2,256,512]{2,1,0:T(8,128)(2,1)}, bf16[2,256,512]{2,1,0:T(8,128)(2,1)}, u32[]{:S(2)}, u32[]{:S(2)}) collective-permute-start(bf16[2,256,512]{2,1,0:T(8,128)(2,1)} %collective-permute-done.65), channel_id=1, source_target_pairs={{0,4},{4,0},{1,5},{5,1},{2,6},{6,2},{3,7},{7,3},{8,12},{12,8},{9,1... | collective-permute-start | bytes 1572872 | tf_op jit(solution)/shard_map/ppermute | solution.py:472
  460.5 46.3 %collective-permute-start.68 = (bf16[2,256,512]{2,1,0:T(8,128)(2,1)}, bf16[2,256,512]{2,1,0:T(8,128)(2,1)S(1)}, u32[]{:S(2)}, u32[]{:S(2)}) collective-permute-start(bf16[2,256,512]{2,1,0:T(8,128)(2,1)} %collective-permute-done.67), channel_id=1, source_target_pairs={{0,4},{4,0},{1,5},{5,1},{2,6},{6,2},{3,7},{7,3},{8,12},{12,8},{9,1... | collective-permute-start | bytes 1572872 | tf_op jit(solution)/shard_map/ppermute | solution.py:472
  464.7 67.1 %all-to-all-start.2 = ((bf16[4,112,1024]{2,1,0:T(8,128)(2,1)}), bf16[4,112,1024]{2,1,0:T(8,128)(2,1)S(1)}, u32[]{:S(2)}, u32[]{:S(2)}) async-start(bf16[4,112,1024]{2,1,0:T(8,128)(2,1)} %pad_maximum_fusion.2), calls=%async_computation.2 | async-start | bytes 1835008 | tf_op jit(solution)/shard_map/all_to_all | solution.py:486
  468.2 64.9 %collective-permute-start.39 = (bf16[96,1024]{1,0:T(8,128)(2,1)}, bf16[96,1024]{1,0:T(8,128)(2,1)}, u32[]{:S(2)}, u32[]{:S(2)}) collective-permute-start(bf16[96,1024]{1,0:T(8,128)(2,1)} %get-tuple-element.238), channel_id=1, source_target_pairs={{0,24},{8,0},{16,8},{24,16},{1,25},{9,1},{17,9},{25,17},{2,26},{10... | collective-permute-start | bytes 589832 | tf_op jit(solution)/shard_map/ppermute | solution.py:472
  477.2 29.8 %collective-permute-start.70 = (bf16[1,256,512]{2,1,0:T(8,128)(2,1)S(1)}, bf16[1,256,512]{2,1,0:T(8,128)(2,1)S(1)}, u32[]{:S(2)}, u32[]{:S(2)}) collective-permute-start(bf16[1,256,512]{2,1,0:T(8,128)(2,1)S(1)} %copy-done.78), channel_id=1, source_target_pairs={{0,8},{8,16},{16,24},{24,0},{1,9},{9,17},{17,25},{25,1},{2,10},{10... | collective-permute-start | bytes 786440 | tf_op jit(solution)/shard_map/ppermute | solution.py:472
  521.9 43.7 %collective-permute-start.58 = (bf16[256,384]{1,0:T(8,128)(2,1)}, bf16[256,384]{1,0:T(8,128)(2,1)S(1)}, u32[]{:S(2)}, u32[]{:S(2)}) collective-permute-start(bf16[256,384]{1,0:T(8,128)(2,1)} %get-tuple-element.231), channel_id=1, source_target_pairs={{0,8},{8,16},{16,24},{24,0},{1,9},{9,17},{17,25},{25,1},{2,10},{10... | collective-permute-start | bytes 589832 | tf_op jit(solution)/shard_map/ppermute | solution.py:472
  524.9 40.8 %collective-permute-start.59 = (bf16[256,384]{1,0:T(8,128)(2,1)}, bf16[256,384]{1,0:T(8,128)(2,1)}, u32[]{:S(2)}, u32[]{:S(2)}) collective-permute-start(bf16[256,384]{1,0:T(8,128)(2,1)} %get-tuple-element.230), channel_id=1, source_target_pairs={{0,16},{8,24},{16,0},{24,8},{1,17},{9,25},{17,1},{25,9},{2,18},{10... | collective-permute-start | bytes 589832 | tf_op jit(solution)/shard_map/ppermute | solution.py:472
  (166 other events, 2041.3 us)

commit v3 on v2

--- a/solution.py
+++ b/solution.py
@@ -3,6 +3,8 @@
 import jax
 import jax.numpy as jnp
 from jax import lax
+from jax.experimental import pallas as pl
+from jax.experimental.pallas import tpu as pltpu
 from jax.experimental.layout import Layout, with_layout_constraint
 from jax.sharding import PartitionSpec as P
 
@@ -553,7 +555,7 @@
     return {FSDP: 0, CTX: 1}[stage] if isinstance(stage, str) else 2 + 1.0 / stage
 
 
-def collect(parts):
+def collect(parts, ready=None):
     far, *near = tp_stages()
     summed = []
     for flip, stacked in enumerate(parts):
@@ -582,7 +584,35 @@
             stacked = total.astype(jnp.bfloat16)
         summed.append(stacked)
     pieces = scatter_start(jnp.concatenate(summed, axis=-1))
+    if ready is not None:
+        pieces = after(pieces, ready)
     return sum(piece.astype(jnp.float32) for piece in pieces)
+
+
+def assemble(pieces, places):
+    kinds, rows, columns = pieces[0].shape
+    count = len(pieces)
+
+    def kernel(places_ref, *refs):
+        for number in range(count):
+
+            @pl.when(pl.program_id(0) == number)
+            def _():
+                for kind in range(kinds):
+                    refs[count + kind][0] = refs[number][kind].astype(jnp.float32)
+
+    size = kinds * count * rows * columns
+    return pl.pallas_call(
+        kernel,
+        out_shape=[jax.ShapeDtypeStruct((count, rows, columns), jnp.float32)] * kinds,
+        grid_spec=pltpu.PrefetchScalarGridSpec(
+            num_scalar_prefetch=1,
+            grid=(count,),
+            in_specs=[pl.BlockSpec((kinds, rows, columns), lambda i, p: (0, 0, 0))] * count,
+            out_specs=[pl.BlockSpec((1, rows, columns), lambda i, p: (p[i], 0, 0))] * kinds,
+        ),
+        cost_estimate=pl.CostEstimate(flops=size, bytes_accessed=6 * size, transcendentals=0),
+    )(places, *pieces)
 
 
 def halves(rows):
@@ -645,29 +675,27 @@
 
     route_rows = own_rows(routes[0])
     kv_width = key_value_projection.shape[1] * 2 * HEAD_SIZE
-    side = jnp.concatenate([w_router, attn_gain[:, None], ffn_gain[:, None]], axis=1)
-    side = jnp.pad(side, ((0, 0), (0, -side.shape[1] % 128)))
+    gains = jnp.pad(jnp.stack([attn_gain, ffn_gain]), ((0, 14), (0, 0)))
+    gains = in_order(all_steps(gains, FSDP), FSDP)
+    gain_one, gain_two = (gains[:, row].reshape(model_width) for row in range(2))
     packed = jnp.concatenate(
-        [w_query, key_value_projection.reshape(slice_width, kv_width), side], axis=1
+        [w_query, key_value_projection.reshape(slice_width, kv_width)], axis=1
     )
     packed_parts = all_steps(row_major(packed), FSDP)
     both_width = head_width + kv_width
-    both_weight = in_order([p[:, :both_width] for p in packed_parts], FSDP).reshape(
-        model_width, both_width
-    )
-    both_weight = row_major(both_weight)
-    side_full = in_order([p[:, both_width:] for p in packed_parts], FSDP).reshape(
-        model_width, side.shape[1]
-    )
-    out_parts = all_steps(after(output_projection_weight, packed_parts), FSDP)
-    out_full = (
-        in_order(out_parts, FSDP).transpose(1, 0, 2).reshape(head_width, model_width)
-    )
+    both_weight = row_major(in_order(packed_parts, FSDP).reshape(model_width, both_width))
     query_full = both_weight[:, :head_width]
     key_value_weight = both_weight[:, head_width:]
-    router_full = side_full[:, :expert_total]
-    gain_one = side_full[:, expert_total]
-    gain_two = side_full[:, expert_total + 1]
+    router = jnp.pad(w_router, ((0, 0), (0, -expert_total % 128)))
+    out_parts = jnp.concatenate([output_projection_weight, router], axis=1)
+    out_parts = all_steps(after(out_parts, packed_parts), FSDP)
+    out_full = (
+        in_order([part[:, :slice_width] for part in out_parts], FSDP)
+        .transpose(1, 0, 2)
+        .reshape(head_width, model_width)
+    )
+    router_full = in_order([part[:, slice_width:] for part in out_parts], FSDP)
+    router_full = router_full.reshape(model_width, router.shape[1])[:, :expert_total]
 
     route_tail = jnp.pad(
         route_rows.astype(jnp.bfloat16), ((0, 0), (0, -route_rows.shape[1] % 256))
@@ -754,7 +782,7 @@
     hidden_pieces = all_steps(hidden_two, FSDP)
     grad_halves = [
         half.reshape(block_count, local_len, half.shape[-1])
-        for half in spread(after(grad_pieces, hidden_two))
+        for half in spread(grad_pieces)
     ]
     hidden_halves = [
         half.reshape(block_count, local_len, half.shape[-1])
@@ -849,22 +877,14 @@
         .reshape(own_len, expert_total)
     )
     back_parts = [put_rows(half) for half in halves(picked_grad.astype(jnp.bfloat16))]
-    (back_parts, picked, gate_pre_grad, up_pre_grad, out_grad, activation, mixture_rows) = (
+    back_parts, picked, gate_pre_grad, up_pre_grad, out_grad, activation = (
         lax.optimization_barrier(
-            (
-                back_parts,
-                picked,
-                gate_pre_grad,
-                up_pre_grad,
-                out_grad,
-                activation,
-                mixture_rows,
-            )
-        )
-    )
-    hidden_grad_sum = collect(back_parts)
+            (back_parts, picked, gate_pre_grad, up_pre_grad, out_grad, activation)
+        )
+    )
     mixture = collect([put_rows(half) for half in halves(mixture_rows)])
     own_out = (residual + mixture).astype(jnp.bfloat16)
+    hidden_grad_sum = collect(back_parts)
 
     def weight_grad(rows, columns):
         return (
@@ -970,8 +990,6 @@
             preferred_element_type=jnp.float32,
         )
         kv_grads.append(jnp.concatenate([key_grad, value_gradient], axis=-1))
-    weight_shape = (fsdp_count, ctx_count, slice_width, ff_width)
-    weight_outs = [jnp.zeros(weight_shape, jnp.float32) for _ in range(3)]
     weight_hops = []
     for step in range(fsdp_count):
         early_hops = all_steps(grad_packets[0][step], CTX)
@@ -1012,28 +1030,26 @@
     hidden_one_grad = summed[:own_len]
     grad_attn_gain = summed[own_len].astype(jnp.bfloat16).reshape(fsdp_count, 1, slice_width)
     gain_parts = scatter_start(grad_attn_gain)
-    grad_attn_gain = scatter_finish(gain_parts)[0]
-    early_total = scatter_finish(after(early_parts, hidden_one_grad))
-    out_rows = lax.all_gather(own_out, TP, axis=0, tiled=True)
-    projection_total = scatter_finish(after(projection_parts, (hidden_one_grad, out_rows)))
-    for step in range(fsdp_count):
-        for hops, kinds in zip(weight_hops[step], ((0, 1), (2,))):
-            for hop, seen in enumerate(hops):
-                seen = after(seen, hidden_one_part)
-                place = ((fsdp_rank - step) % fsdp_count, (ctx_rank - hop) % ctx_count, 0, 0)
-                for number, kind in enumerate(kinds):
-                    weight_outs[kind] = lax.dynamic_update_slice(
-                        weight_outs[kind], seen[number].astype(jnp.float32)[None, None], place
-                    )
-    weight_outs = [
-        grad.reshape(fsdp_count * ctx_count, slice_width, ff_width) for grad in weight_outs
-    ]
     back_one, _ = rms_backward(
         hidden_one_grad, own_rows(normed_one), own_rows(factor_one), gain_one
     )
-    input_grad = residual_grad + back_one
-    input_grad = lax.all_gather(
-        after(input_grad.astype(jnp.bfloat16), gain_parts), TP, axis=0, tiled=True
+    input_grad = (residual_grad + back_one).astype(jnp.bfloat16)
+    input_grad = lax.all_gather(input_grad, TP, axis=0, tiled=True)
+    out_rows = lax.all_gather(after(own_out, input_grad), TP, axis=0, tiled=True)
+    grad_attn_gain = scatter_finish(after(gain_parts, out_rows))[0]
+    early_total = scatter_finish(after(early_parts, out_rows))
+    projection_total = scatter_finish(after(projection_parts, out_rows))
+    hop_places = jnp.stack(
+        [
+            (fsdp_rank - step) % fsdp_count * ctx_count + (ctx_rank - hop) % ctx_count
+            for step in range(fsdp_count)
+            for hop in range(ctx_count)
+        ]
+    ).astype(jnp.int32)
+    weight_outs = assemble(
+        after([seen for hops, _ in weight_hops for seen in hops], out_rows), hop_places
+    ) + assemble(
+        after([seen for _, hops in weight_hops for seen in hops], out_rows), hop_places
     )
     return (
         out_rows[None],

time: 599 us -> 607 us (1.013)
  other arithmetic: 72.8 us -> 51.9 us
  Pallas kernels: 0 us -> 13.1 us
  matrix products: 60 us -> 67.1 us
    dynamic_update_slice x17 -> x0, other arithmetic: 17.8 us -> none  [local_spread(): lax.dynamic_update_slice(weight_outs[kind], seen[number].astype(jnp.float...]
    ppermute x16, waiting for transfers between devices: 54.3 us -> 40.1 us  [tp_partner(): return lax.ppermute(block, TP, [(i, i ^ distance) for i in range(count)])]
    pallas_call x0 -> x2, Pallas kernels: none -> 13.1 us  [assemble(): pl.pallas_call(kernel, out_shape=[jax.ShapeDtypeStruct((count, rows, colu...]
    all_to_all x1, starting transfers between devices: 3.36 us -> 14.8 us  [local_spread(): lax.all_to_all(gate_grad_part.reshape(block_count * tp_count, own_len), e...]
    ppermute x58 -> x61, waiting for transfers between devices: 139 us -> 149 us  [rotated(): lax.ppermute(block, axis, [(i, (i + distance) % count) for i in range(cou...]
    dot_general x1, matrix products: 3.38 us -> 12.8 us  [local_spread(): jnp.einsum(CF_DF_TO_CD, activation, down_weight, preferred_element_type=j...]
    ppermute x58 -> x61, starting transfers between devices: 116 us -> 107 us  [rotated(): lax.ppermute(block, axis, [(i, (i + distance) % count) for i in range(cou...]
    dynamic_update_slice x36 -> x38, local copies, waits for them, and re-layouts: 16.3 us -> 12 us  [in_order(): lax.dynamic_update_index_in_dim(whole, pieces[step], (rank - step) % coun...]
  transfers between devices with their start and end apart: 79 -> 82, of which waited for: 25 -> 26; matrix products, arithmetic and copies ran while one was open for 25% -> 28% of each run, Pallas kernels for 0% -> 2%
where the time goes in v3:
time: 607 us; the launch traced here: 597 us
  waiting for transfers between devices  203 us (33%)
  starting transfers between devices  146 us (24%)
  local copies, waits for them, and re-layouts  88.4 us (15%)
  matrix products  67.1 us (11%)
  other arithmetic  51.9 us (9%)
  blocking collectives  24 us (4%)
  Pallas kernels  13.1 us (2%)
    ppermute x61, waiting for transfers between devices, rotated(): lax.ppermute(block, axis, [(i, (i + distance) % count) for i in range(cou...  149 us
    ppermute x61, starting transfers between devices, rotated(): lax.ppermute(block, axis, [(i, (i + distance) % count) for i in range(cou...  107 us
    ppermute x16, waiting for transfers between devices, tp_partner(): return lax.ppermute(block, TP, [(i, i ^ distance) for i in range(count)])  40.1 us
    unnamed x260, local copies, waits for them, and re-layouts  19.8 us
    all_to_all x1, starting transfers between devices, local_spread(): lax.all_to_all(gate_grad_part.reshape(block_count * tp_count, own_len), e...  14.8 us
    pallas_call x2, Pallas kernels, assemble(): pl.pallas_call(kernel, out_shape=[jax.ShapeDtypeStruct((count, rows, colu...  13.1 us
    dot_general x1, matrix products, local_spread(): jnp.einsum(CF_DF_TO_CD, activation, down_weight, preferred_element_type=j...  12.8 us
  transfers between devices with their start and end apart: 82, of which 26 were waited for; matrix products, arithmetic and copies ran while one was open for 28% of the time, Pallas kernels for 2%

profile of v3, /device:TPU:0, one launch (start us, length us, event | category | flops | bytes accessed | tf_op | source)
XLA Modules:
  0.0 596.8 jit_solution(5146710955051416312)
XLA Ops:
  114.4 19.1 %collective-permute-done.19 = bf16[4,96,512]{2,1,0:T(8,128)(2,1)S(1)} collective-permute-done((bf16[4,96,512]{2,1,0:T(8,128)(2,1)S(1)}, bf16[4,96,512]{2,1,0:T(8,128)(2,1)S(1)}, u32[]{:S(2)}, u32[]{:S(2)}) %collective-permute-start.19) | collective-permute-done | bytes 393248 | tf_op jit(solution)/shard_map/ppermute | solution.py:474
  140.8 11.7 %collective-permute-done.20 = bf16[4,2,96,512]{3,2,1,0:T(8,128)(2,1)S(1)} collective-permute-done((bf16[4,2,96,512]{3,2,1,0:T(8,128)(2,1)S(1)}, bf16[4,2,96,512]{3,2,1,0:T(8,128)(2,1)S(1)}, u32[]{:S(2)}, u32[]{:S(2)}) %collective-permute-start.20) | collective-permute-done | bytes 786464 | tf_op jit(solution)/shard_map/ppermute | solution.py:518
  167.4 27.6 %collective-permute-done.30 = bf16[1,256,512]{2,1,0:T(8,128)(2,1)S(1)} collective-permute-done((bf16[1,256,512]{2,1,0:T(8,128)(2,1)S(1)}, bf16[1,256,512]{2,1,0:T(8,128)(2,1)S(1)}, u32[]{:S(2)}, u32[]{:S(2)}) %collective-permute-start.30) | collective-permute-done | bytes 262176 | tf_op jit(solution)/shard_map/ppermute | solution.py:474
  242.4 12.8 %fusion.1 = (f32[1536]{0:T(1024)S(1)}, bf16[1536,1024]{1,0:T(8,128)(2,1)}) fusion(bf16[1536,640]{1,0:T(8,128)(2,1)S(1)} %bitcast.566, bf16[1536,640]{1,0:T(8,128)(2,1)S(1)} %bitcast.568, f32[1536]{0:T(1024)S(1)} %divide_select_fusion, bf16[1536,512]{1,0:T(8,128)(2,1)S(1)} %get-tuple-element.117, bf16[1024,512]{1,0:T(8,128)(2,1)S(1)} %bitcast.601), kind=kOutput, calls=%fused_computation.3 | convolution fusion | flops 1623194112 | bytes 9711616 | tf_op jit(solution)/shard_map/cf,df->cd/dot_general | solution.py:852
  256.4 14.8 %all-to-all-start.1 = ((f32[32,1,96]{2,1,0:T(1,128)}), f32[32,1,96]{2,1,0:T(1,128)}, u32[]{:S(2)}, u32[]{:S(2)}) async-start(f32[32,1,96]{2,1,0:T(1,128)} %all_to_all.13), calls=%async_computation.1 | async-start | bytes 32768 | tf_op jit(solution)/shard_map/all_to_all | solution.py:871
  320.6 10.6 %collective-permute-done.32 = bf16[4,2,96,512]{3,2,0,1:T(8,128)(2,1)S(1)} collective-permute-done((bf16[4,2,96,512]{3,2,0,1:T(8,128)(2,1)S(1)}, bf16[4,2,96,512]{3,2,0,1:T(8,128)(2,1)S(1)}, u32[]{:S(2)}, u32[]{:S(2)}) %collective-permute-start.32) | collective-permute-done | bytes 786464 | tf_op jit(solution)/shard_map/ppermute | solution.py:518
  336.6 10.2 %collective-permute-done.44 = bf16[4,2,96,512]{3,2,0,1:T(8,128)(2,1)S(1)} collective-permute-done((bf16[4,2,96,512]{3,2,0,1:T(8,128)(2,1)S(1)}, bf16[4,2,96,512]{3,2,0,1:T(8,128)(2,1)S(1)}, u32[]{:S(2)}, u32[]{:S(2)}) %collective-permute-start.44) | collective-permute-done | bytes 786464 | tf_op jit(solution)/shard_map/ppermute | solution.py:518
  358.3 8.7 %collective-permute-done.45 = bf16[4,96,512]{2,1,0:T(8,128)(2,1)S(1)} collective-permute-done((bf16[4,96,512]{2,1,0:T(8,128)(2,1)S(1)}, bf16[4,96,512]{2,1,0:T(8,128)(2,1)S(1)}, u32[]{:S(2)}, u32[]{:S(2)}) %collective-permute-start.45) | collective-permute-done | bytes 393248 | tf_op jit(solution)/shard_map/ppermute | solution.py:474
  372.4 4.5 collective-permute-done.49
  376.9 6.1 %collective-permute-done.50 = bf16[96,1024]{1,0:T(8,128)(2,1)S(1)} collective-permute-done((bf16[96,1024]{1,0:T(8,128)(2,1)S(1)}, bf16[96,1024]{1,0:T(8,128)(2,1)S(1)}, u32[]{:S(2)}, u32[]{:S(2)}) %collective-permute-start.50) | collective-permute-done | bytes 196640 | tf_op jit(solution)/shard_map/ppermute | solution.py:474
  386.3 8.3 %all-gather = bf16[448,1152]{1,0:T(8,128)(2,1)S(1)} all-gather(bf16[112,1152]{1,0:T(8,128)(2,1)S(1)} %fusion.118), channel_id=2, replica_groups=mesh['fsdp'=4,'ctx'=2,'tp'=4] {'tp'}, dimensions={0}, use_global_device_ids=true | all-gather | bytes 1290240 | tf_op jit(solution)/shard_map/all_gather | solution.py:929
  406.8 4.7 collective-permute-done.52
  411.6 13.0 %collective-permute-start.37 = (bf16[96,1024]{1,0:T(8,128)(2,1)}, bf16[96,1024]{1,0:T(8,128)(2,1)}, u32[]{:S(2)}, u32[]{:S(2)}) collective-permute-start(bf16[96,1024]{1,0:T(8,128)(2,1)} %get-tuple-element.238), channel_id=1, source_target_pairs={{0,8},{8,16},{16,24},{24,0},{1,9},{9,17},{17,25},{25,1},{2,10},{10... | collective-permute-start | bytes 589832 | tf_op jit(solution)/shard_map/ppermute | solution.py:474
  437.7 6.5 %all-to-all-done.2 = bf16[4,112,1024]{2,1,0:T(8,128)(2,1)S(1)} async-done(((bf16[4,112,1024]{2,1,0:T(8,128)(2,1)}), bf16[4,112,1024]{2,1,0:T(8,128)(2,1)S(1)}, u32[]{:S(2)}, u32[]{:S(2)}) %all-to-all-start.2) | async-done | bytes 917536 | tf_op jit(solution)/shard_map/all_to_all | solution.py:488
  451.6 5.0 collective-permute-done.38
  456.6 12.4 %collective-permute-start.77 = (bf16[1,256,512]{2,1,0:T(8,128)(2,1)}, bf16[1,256,512]{2,1,0:T(8,128)(2,1)}, u32[]{:S(2)}, u32[]{:S(2)}) collective-permute-start(bf16[1,256,512]{2,1,0:T(8,128)(2,1)} %get-tuple-element.120), channel_id=1, source_target_pairs={{0,24},{8,0},{16,8},{24,16},{1,25},{9,1},{17,9},{25,17},{2,26},{10... | collective-permute-start | bytes 786440 | tf_op jit(solution)/shard_map/ppermute | solution.py:474
  470.4 7.2 %collective-permute-start.61 = (bf16[256,384]{1,0:T(8,128)(2,1)}, bf16[256,384]{1,0:T(8,128)(2,1)S(1)}, u32[]{:S(2)}, u32[]{:S(2)}) collective-permute-start(bf16[256,384]{1,0:T(8,128)(2,1)} %get-tuple-element.233), channel_id=1, source_target_pairs={{0,8},{8,16},{16,24},{24,0},{1,9},{9,17},{17,25},{25,1},{2,10},{10... | collective-permute-start | bytes 589832 | tf_op jit(solution)/shard_map/ppermute | solution.py:474
  478.9 21.2 %collective-permute-done.62 = bf16[256,384]{1,0:T(8,128)(2,1)S(1)} collective-permute-done((bf16[256,384]{1,0:T(8,128)(2,1)}, bf16[256,384]{1,0:T(8,128)(2,1)S(1)}, u32[]{:S(2)}, u32[]{:S(2)}) %collective-permute-start.62) | collective-permute-done | bytes 196640 | tf_op jit(solution)/shard_map/ppermute | solution.py:474
  504.3 7.8 %all_gather.14 = bf16[384,1024]{1,0:T(8,128)(2,1)S(1)} all-gather(bf16[96,1024]{1,0:T(8,128)(2,1)S(1)} %get-tuple-element.257), channel_id=1, replica_groups=mesh['fsdp'=4,'ctx'=2,'tp'=4] {'tp'}, dimensions={0}, use_global_device_ids=true | all-gather | bytes 983040 | tf_op jit(solution)/shard_map/all_gather | solution.py:1037
  512.3 10.8 %collective-permute-done.58 = bf16[256,512]{1,0:T(8,128)(2,1)S(1)} collective-permute-done((bf16[256,512]{1,0:T(8,128)(2,1)S(1)}, bf16[256,512]{1,0:T(8,128)(2,1)S(1)}, u32[]{:S(2)}, u32[]{:S(2)}) %collective-permute-start.58) | collective-permute-done | bytes 262176 | tf_op jit(solution)/shard_map/ppermute | solution.py:474
  527.2 7.9 %all_gather.15 = bf16[384,1024]{1,0:T(8,128)(2,1)S(1)} all-gather(bf16[96,1024]{1,0:T(8,128)(2,1)S(1)} %get-tuple-element.90), channel_id=1, replica_groups=mesh['fsdp'=4,'ctx'=2,'tp'=4] {'tp'}, dimensions={0}, use_global_device_ids=true | all-gather | bytes 983040 | tf_op jit(solution)/shard_map/all_gather | solution.py:1038
  535.2 31.1 %collective-permute-done.78.refs_7_ = bf16[1,256,512]{2,1,0:T(8,128)(2,1)} collective-permute-done((bf16[1,256,512]{2,1,0:T(8,128)(2,1)}, bf16[1,256,512]{2,1,0:T(8,128)(2,1)}, u32[]{:S(2)}, u32[]{:S(2)}) %collective-permute-start.78) | collective-permute-done | bytes 262176 | tf_op jit(solution)/shard_map/ppermute | solution.py:474
  576.2 5.8 shard_map.213
  582.4 7.4 %shard_map.212 = (f32[8,256,512]{2,1,0:T(8,128)}, f32[8,256,512]{2,1,0:T(8,128)}) custom-call(s32[8]{0:T(128)} %stack.114.places_ref, bf16[2,256,512]{2,1,0:T(8,128)(2,1)} %pad_maximum_fusion.8.refs_0_, bf16[2,256,512]{2,1,0:T(8,128)(2,1)} %collective-permute-done.65.refs_1_, bf16[2,256,512]{2,1,0:T(8,128)(2,1)} %collective-permute-done.66.refs_2_, ...), custom_call_target="tpu_custom_call" | custom-call | flops 2097152 | bytes 12582912 | tf_op jit(solution)/shard_map/pallas_call | solution.py:605
  (682 shorter events, 317.9 us)
Async XLA Ops:
  101.8 35.4 %collective-permute-start.14 = (bf16[4,2,96,640]{3,2,1,0:T(8,128)(2,1)S(1)}, bf16[4,2,96,640]{3,2,1,0:T(8,128)(2,1)S(1)}, u32[]{:S(2)}, u32[]{:S(2)}) collective-permute-start(bf16[4,2,96,640]{3,2,1,0:T(8,128)(2,1)S(1)} %bitcast_dynamic-update-slice_fusion.18), channel_id=1, source_target_pairs={{0,4},{4,0},{1,5},{5,1},{2,6},{6,2},{3,7},{7,3},{8,12},{12,8},{9,1... | collective-permute-start | bytes 2949128 | tf_op jit(solution)/shard_map/ppermute | solution.py:474
  104.2 50.1 %collective-permute-start.41 = (bf16[4,2,96,640]{3,2,1,0:T(8,128)(2,1)S(1)}, bf16[4,2,96,640]{3,2,1,0:T(8,128)(2,1)S(1)}, u32[]{:S(2)}, u32[]{:S(2)}) collective-permute-start(bf16[4,2,96,640]{3,2,1,0:T(8,128)(2,1)S(1)} %bitcast_dynamic-update-slice_fusion.16), channel_id=1, source_target_pairs={{0,2},{1,3},{2,0},{3,1},{4,6},{5,7},{6,4},{7,5},{8,10},{9,11},{10,... | collective-permute-start | bytes 2949128 | tf_op jit(solution)/shard_map/ppermute | solution.py:518
  112.8 48.9 %collective-permute-start.28 = (bf16[1,256,512]{2,1,0:T(8,128)(2,1)S(1)}, bf16[1,256,512]{2,1,0:T(8,128)(2,1)S(1)}, u32[]{:S(2)}, u32[]{:S(2)}) collective-permute-start(bf16[1,256,512]{2,1,0:T(8,128)(2,1)S(1)} %copy-done.88), channel_id=1, source_target_pairs={{0,8},{8,16},{16,24},{24,0},{1,9},{9,17},{17,25},{25,1},{2,10},{10... | collective-permute-start | bytes 786440 | tf_op jit(solution)/shard_map/ppermute | solution.py:474
  152.5 42.5 %collective-permute-start.25 = (bf16[2,256,512]{2,1,0:T(8,128)(2,1)S(1)}, bf16[2,256,512]{2,1,0:T(8,128)(2,1)S(1)}, u32[]{:S(2)}, u32[]{:S(2)}) collective-permute-start(bf16[2,256,512]{2,1,0:T(8,128)(2,1)S(1)} %copy-done.73), channel_id=1, source_target_pairs={{0,8},{8,16},{16,24},{24,0},{1,9},{9,17},{17,25},{25,1},{2,10},{10... | collective-permute-start | bytes 1572872 | tf_op jit(solution)/shard_map/ppermute | solution.py:474
  162.5 32.5 %collective-permute-start.26 = (bf16[2,256,512]{2,1,0:T(8,128)(2,1)S(1)}, bf16[2,256,512]{2,1,0:T(8,128)(2,1)S(1)}, u32[]{:S(2)}, u32[]{:S(2)}) collective-permute-start(bf16[2,256,512]{2,1,0:T(8,128)(2,1)S(1)} %copy-done.74), channel_id=1, source_target_pairs={{0,16},{8,24},{16,0},{24,8},{1,17},{9,25},{17,1},{25,9},{2,18},{10... | collective-permute-start | bytes 1572872 | tf_op jit(solution)/shard_map/ppermute | solution.py:474
  167.2 32.5 %collective-permute-start.15 = (bf16[4,2,2,96,640]{4,3,2,1,0:T(8,128)(2,1)S(1)}, bf16[4,2,2,96,640]{4,3,2,1,0:T(8,128)(2,1)S(1)}, u32[]{:S(2)}, u32[]{:S(2)}) collective-permute-start(bf16[4,2,2,96,640]{4,3,2,1,0:T(8,128)(2,1)S(1)} %bitcast_dynamic-update-slice_fusion.11), channel_id=1, source_target_pairs={{0,1},{1,0},{2,3},{3,2},{4,5},{5,4},{6,7},{7,6},{8,9},{9,8},{10,11... | collective-permute-start | bytes 5898248 | tf_op jit(solution)/shard_map/ppermute | solution.py:518
  195.0 37.5 %collective-permute-start.42 = (bf16[4,2,2,96,640]{4,3,2,1,0:T(8,128)(2,1)}, bf16[4,2,2,96,640]{4,3,2,1,0:T(8,128)(2,1)}, u32[]{:S(2)}, u32[]{:S(2)}) collective-permute-start(bf16[4,2,2,96,640]{4,3,2,1,0:T(8,128)(2,1)} %bitcast_dynamic-update-slice_fusion.8), channel_id=1, source_target_pairs={{0,1},{1,0},{2,3},{3,2},{4,5},{5,4},{6,7},{7,6},{8,9},{9,8},{10,11... | collective-permute-start | bytes 5898248 | tf_op jit(solution)/shard_map/ppermute | solution.py:518
  256.4 47.1 %all-to-all-start.1 = ((f32[32,1,96]{2,1,0:T(1,128)}), f32[32,1,96]{2,1,0:T(1,128)}, u32[]{:S(2)}, u32[]{:S(2)}) async-start(f32[32,1,96]{2,1,0:T(1,128)} %all_to_all.13), calls=%async_computation.1 | async-start | bytes 32768 | tf_op jit(solution)/shard_map/all_to_all | solution.py:871
  280.5 37.5 %collective-permute-start.34 = (bf16[4,2,2,96,512]{4,3,0,2,1:T(8,128)(2,1)}, bf16[4,2,2,96,512]{4,3,0,2,1:T(8,128)(2,1)}, u32[]{:S(2)}, u32[]{:S(2)}) collective-permute-start(bf16[4,2,2,96,512]{4,3,0,2,1:T(8,128)(2,1)} %bitcast.546), channel_id=1, source_target_pairs={{0,1},{1,0},{2,3},{3,2},{4,5},{5,4},{6,7},{7,6},{8,9},{9,8},{10,11... | collective-permute-start | bytes 4718600 | tf_op jit(solution)/shard_map/ppermute | solution.py:518
  293.2 154.9 %collective-permute-start.66 = (bf16[2,256,512]{2,1,0:T(8,128)(2,1)}, bf16[2,256,512]{2,1,0:T(8,128)(2,1)}, u32[]{:S(2)}, u32[]{:S(2)}) collective-permute-start(bf16[2,256,512]{2,1,0:T(8,128)(2,1)} %pad_maximum_fusion.9), channel_id=1, source_target_pairs={{0,8},{8,16},{16,24},{24,0},{1,9},{9,17},{17,25},{25,1},{2,10},{10... | collective-permute-start | bytes 1572872 | tf_op jit(solution)/shard_map/ppermute | solution.py:474
  305.7 142.3 %collective-permute-start.68 = (bf16[2,256,512]{2,1,0:T(8,128)(2,1)}, bf16[2,256,512]{2,1,0:T(8,128)(2,1)}, u32[]{:S(2)}, u32[]{:S(2)}) collective-permute-start(bf16[2,256,512]{2,1,0:T(8,128)(2,1)} %pad_maximum_fusion.10), channel_id=1, source_target_pairs={{0,16},{8,24},{16,0},{24,8},{1,17},{9,25},{17,1},{25,9},{2,18},{10... | collective-permute-start | bytes 1572872 | tf_op jit(solution)/shard_map/ppermute | solution.py:474
  334.8 32.9 %collective-permute-start.33 = (bf16[4,96,512]{2,1,0:T(8,128)(2,1)S(1)}, bf16[4,96,512]{2,1,0:T(8,128)(2,1)S(1)}, u32[]{:S(2)}, u32[]{:S(2)}) collective-permute-start(bf16[4,96,512]{2,1,0:T(8,128)(2,1)S(1)} %dynamic-slice_bitcast_fusion.9), channel_id=1, source_target_pairs={{0,4},{4,0},{1,5},{5,1},{2,6},{6,2},{3,7},{7,3},{8,12},{12,8},{9,1... | collective-permute-start | bytes 1179656 | tf_op jit(solution)/shard_map/ppermute | solution.py:474
  376.9 72.7 %collective-permute-start.70 = (bf16[2,256,512]{2,1,0:T(8,128)(2,1)}, bf16[2,256,512]{2,1,0:T(8,128)(2,1)}, u32[]{:S(2)}, u32[]{:S(2)}) collective-permute-start(bf16[2,256,512]{2,1,0:T(8,128)(2,1)} %pad_maximum_fusion.11), channel_id=1, source_target_pairs={{0,24},{8,0},{16,8},{24,16},{1,25},{9,1},{17,9},{25,17},{2,26},{10... | collective-permute-start | bytes 1572872 | tf_op jit(solution)/shard_map/ppermute | solution.py:474
  383.0 61.6 %collective-permute-start.72 = (bf16[1,256,512]{2,1,0:T(8,128)(2,1)}, bf16[1,256,512]{2,1,0:T(8,128)(2,1)}, u32[]{:S(2)}, u32[]{:S(2)}) collective-permute-start(bf16[1,256,512]{2,1,0:T(8,128)(2,1)} %get-tuple-element.121.refs_0_), channel_id=1, source_target_pairs={{0,4},{4,0},{1,5},{5,1},{2,6},{6,2},{3,7},{7,3},{8,12},{12,8},{9,1... | collective-permute-start | bytes 786440 | tf_op jit(solution)/shard_map/ppermute | solution.py:474
  411.6 38.6 %collective-permute-start.37 = (bf16[96,1024]{1,0:T(8,128)(2,1)}, bf16[96,1024]{1,0:T(8,128)(2,1)}, u32[]{:S(2)}, u32[]{:S(2)}) collective-permute-start(bf16[96,1024]{1,0:T(8,128)(2,1)} %get-tuple-element.238), channel_id=1, source_target_pairs={{0,8},{8,16},{16,24},{24,0},{1,9},{9,17},{17,25},{25,1},{2,10},{10... | collective-permute-start | bytes 589832 | tf_op jit(solution)/shard_map/ppermute | solution.py:474
  449.6 52.3 %collective-permute-start.73 = (bf16[1,256,512]{2,1,0:T(8,128)(2,1)}, bf16[1,256,512]{2,1,0:T(8,128)(2,1)S(1)}, u32[]{:S(2)}, u32[]{:S(2)}) collective-permute-start(bf16[1,256,512]{2,1,0:T(8,128)(2,1)} %get-tuple-element.118), channel_id=1, source_target_pairs={{0,8},{8,16},{16,24},{24,0},{1,9},{9,17},{17,25},{25,1},{2,10},{10... | collective-permute-start | bytes 786440 | tf_op jit(solution)/shard_map/ppermute | solution.py:474
  450.1 52.1 %collective-permute-start.75 = (bf16[1,256,512]{2,1,0:T(8,128)(2,1)}, bf16[1,256,512]{2,1,0:T(8,128)(2,1)S(1)}, u32[]{:S(2)}, u32[]{:S(2)}) collective-permute-start(bf16[1,256,512]{2,1,0:T(8,128)(2,1)} %get-tuple-element.119), channel_id=1, source_target_pairs={{0,16},{8,24},{16,0},{24,8},{1,17},{9,25},{17,1},{25,9},{2,18},{10... | collective-permute-start | bytes 786440 | tf_op jit(solution)/shard_map/ppermute | solution.py:474
  456.6 45.7 %collective-permute-start.77 = (bf16[1,256,512]{2,1,0:T(8,128)(2,1)}, bf16[1,256,512]{2,1,0:T(8,128)(2,1)}, u32[]{:S(2)}, u32[]{:S(2)}) collective-permute-start(bf16[1,256,512]{2,1,0:T(8,128)(2,1)} %get-tuple-element.120), channel_id=1, source_target_pairs={{0,24},{8,0},{16,8},{24,16},{1,25},{9,1},{17,9},{25,17},{2,26},{10... | collective-permute-start | bytes 786440 | tf_op jit(solution)/shard_map/ppermute | solution.py:474
  469.0 31.0 %collective-permute-start.62 = (bf16[256,384]{1,0:T(8,128)(2,1)}, bf16[256,384]{1,0:T(8,128)(2,1)S(1)}, u32[]{:S(2)}, u32[]{:S(2)}) collective-permute-start(bf16[256,384]{1,0:T(8,128)(2,1)} %get-tuple-element.232), channel_id=1, source_target_pairs={{0,16},{8,24},{16,0},{24,8},{1,17},{9,25},{17,1},{25,9},{2,18},{10... | collective-permute-start | bytes 589832 | tf_op jit(solution)/shard_map/ppermute | solution.py:474
  512.2 58.4 %collective-permute-start.65 = (bf16[2,256,512]{2,1,0:T(8,128)(2,1)S(1)}, bf16[2,256,512]{2,1,0:T(8,128)(2,1)}, u32[]{:S(2)}, u32[]{:S(2)}) collective-permute-start(bf16[2,256,512]{2,1,0:T(8,128)(2,1)S(1)} %copy-done.36), channel_id=1, source_target_pairs={{0,4},{4,0},{1,5},{5,1},{2,6},{6,2},{3,7},{7,3},{8,12},{12,8},{9,1... | collective-permute-start | bytes 1572872 | tf_op jit(solution)/shard_map/ppermute | solution.py:474
  523.1 47.5 %collective-permute-start.67 = (bf16[2,256,512]{2,1,0:T(8,128)(2,1)}, bf16[2,256,512]{2,1,0:T(8,128)(2,1)}, u32[]{:S(2)}, u32[]{:S(2)}) collective-permute-start(bf16[2,256,512]{2,1,0:T(8,128)(2,1)} %collective-permute-done.66.refs_2_), channel_id=1, source_target_pairs={{0,4},{4,0},{1,5},{5,1},{2,6},{6,2},{3,7},{7,3},{8,12},{12,8},{9,1... | collective-permute-start | bytes 1572872 | tf_op jit(solution)/shard_map/ppermute | solution.py:474
  523.1 49.1 %collective-permute-start.69 = (bf16[2,256,512]{2,1,0:T(8,128)(2,1)}, bf16[2,256,512]{2,1,0:T(8,128)(2,1)}, u32[]{:S(2)}, u32[]{:S(2)}) collective-permute-start(bf16[2,256,512]{2,1,0:T(8,128)(2,1)} %collective-permute-done.68.refs_4_), channel_id=1, source_target_pairs={{0,4},{4,0},{1,5},{5,1},{2,6},{6,2},{3,7},{7,3},{8,12},{12,8},{9,1... | collective-permute-start | bytes 1572872 | tf_op jit(solution)/shard_map/ppermute | solution.py:474
  525.1 47.1 %collective-permute-start.71 = (bf16[2,256,512]{2,1,0:T(8,128)(2,1)}, bf16[2,256,512]{2,1,0:T(8,128)(2,1)}, u32[]{:S(2)}, u32[]{:S(2)}) collective-permute-start(bf16[2,256,512]{2,1,0:T(8,128)(2,1)} %collective-permute-done.70.refs_6_), channel_id=1, source_target_pairs={{0,4},{4,0},{1,5},{5,1},{2,6},{6,2},{3,7},{7,3},{8,12},{12,8},{9,1... | collective-permute-start | bytes 1572872 | tf_op jit(solution)/shard_map/ppermute | solution.py:474
  525.8 40.4 %collective-permute-start.78 = (bf16[1,256,512]{2,1,0:T(8,128)(2,1)}, bf16[1,256,512]{2,1,0:T(8,128)(2,1)}, u32[]{:S(2)}, u32[]{:S(2)}) collective-permute-start(bf16[1,256,512]{2,1,0:T(8,128)(2,1)} %collective-permute-done.77.refs_6_), channel_id=1, source_target_pairs={{0,4},{4,0},{1,5},{5,1},{2,6},{6,2},{3,7},{7,3},{8,12},{12,8},{9,1... | collective-permute-start | bytes 786440 | tf_op jit(solution)/shard_map/ppermute | solution.py:474
  (185 other events, 2648.5 us)

commit v4 on v3

--- a/solution.py
+++ b/solution.py
@@ -697,9 +697,9 @@
     router_full = in_order([part[:, slice_width:] for part in out_parts], FSDP)
     router_full = router_full.reshape(model_width, router.shape[1])[:, :expert_total]
 
-    route_tail = jnp.pad(
-        route_rows.astype(jnp.bfloat16), ((0, 0), (0, -route_rows.shape[1] % 256))
-    )
+    expert_ids = jnp.arange(expert_total, dtype=jnp.int32)
+    own_chosen = jnp.any(route_rows[:, :, None] == expert_ids[None, None, :], axis=1)
+    route_tail = jnp.pad(own_chosen.astype(jnp.bfloat16), ((0, 0), (0, -expert_total % 256)))
     carried = jnp.concatenate([own_rows(cotangent[0]), route_tail], axis=1)
     grad_pieces = all_steps(after(carried, out_parts), FSDP)
 
@@ -789,12 +789,9 @@
         for half in spread(hidden_pieces)
     ]
     tail_start = grad_halves[1].shape[-1] - route_tail.shape[1]
-    routes_all = grad_halves[1][:, :, tail_start : tail_start + route_rows.shape[1]]
-    routes_all = routes_all.astype(jnp.int32).reshape(-1, route_rows.shape[1])
-    expert_ids = jnp.arange(expert_total, dtype=jnp.int32)
-    chosen_all = jnp.any(routes_all[:, :, None] == expert_ids[None, None, :], axis=1)
+    chosen_all = grad_halves[1][:, :, tail_start : tail_start + expert_total]
     own_expert = tp_rank * block_count + fsdp_rank * ctx_count + ctx_rank
-    member = jnp.any(routes_all == own_expert, axis=1).reshape(block_count, local_len)
+    member = jnp.any((expert_ids == own_expert) & (chosen_all > 0), axis=2)
     places = jnp.cumsum(member.astype(jnp.int32), axis=1) - 1
     slots = jnp.where(member, places, capacity)
     slot_ids = jnp.arange(capacity, dtype=jnp.int32)
@@ -808,9 +805,8 @@
             .reshape(block_count * capacity, rows.shape[2])
         )
 
-    slot_chosen = take_rows(
-        chosen_all.astype(jnp.bfloat16).reshape(block_count, local_len, expert_total)
-    ).astype(jnp.float32)
+    grad_rows = jnp.concatenate([take_rows(half) for half in grad_halves], axis=1)
+    slot_chosen = grad_rows[:, model_width : model_width + expert_total].astype(jnp.float32)
 
     def put_rows(rows):
         stacked = rows.reshape(block_count, capacity, rows.shape[1])
@@ -831,7 +827,6 @@
     )
     gate_weight, up_weight = whole_weights(first_packets)
     (down_weight,) = whole_weights(down_packets)
-    own_chosen = jnp.any(route_rows[:, :, None] == expert_ids[None, None, :], axis=1)
 
     def exp_logits(hidden, chosen):
         logits = jnp.dot(hidden, router_full, preferred_element_type=jnp.float32)
@@ -853,7 +848,6 @@
 
     mixture_rows = (result * scaled[:, None]).astype(jnp.bfloat16)
 
-    grad_rows = jnp.concatenate([take_rows(half) for half in grad_halves], axis=1)
     grad_rows = grad_rows[:, :model_width]
     grad_wide_rows = grad_rows.astype(jnp.float32)
     slot_grad = jnp.sum(grad_wide_rows * result, axis=1).reshape(block_count, capacity)

time: 607 us -> 592 us (0.975)
  matrix products: 67.1 us -> 56.4 us
  local copies, waits for them, and re-layouts: 88.4 us -> 80.3 us
    dot_general x1, matrix products: 12.8 us -> 3.39 us  [local_spread(): jnp.einsum(CF_DF_TO_CD, activation, down_weight, preferred_element_type=j...]
    ppermute x61, starting transfers between devices: 107 us -> 114 us  [rotated(): lax.ppermute(block, axis, [(i, (i + distance) % count) for i in range(cou...]
    unnamed x260 -> x256, local copies, waits for them, and re-layouts: 19.8 us -> 18.7 us
  transfers between devices with their start and end apart: 82 -> 82, of which waited for: 26 -> 26; matrix products, arithmetic and copies ran while one was open for 28% -> 26% of each run, Pallas kernels for 2% -> 2%
where the time goes in v4:
time: 592 us; the launch traced here: 582 us
  waiting for transfers between devices  203 us (34%)
  starting transfers between devices  152 us (26%)
  local copies, waits for them, and re-layouts  80.3 us (14%)
  matrix products  56.4 us (10%)
  other arithmetic  48.8 us (8%)
  blocking collectives  24.9 us (4%)
  Pallas kernels  13.1 us (2%)
    ppermute x61, waiting for transfers between devices, rotated(): lax.ppermute(block, axis, [(i, (i + distance) % count) for i in range(cou...  149 us
    ppermute x61, starting transfers between devices, rotated(): lax.ppermute(block, axis, [(i, (i + distance) % count) for i in range(cou...  114 us
    ppermute x16, waiting for transfers between devices, tp_partner(): return lax.ppermute(block, TP, [(i, i ^ distance) for i in range(count)])  40.5 us
    unnamed x256, local copies, waits for them, and re-layouts  18.7 us
    all_to_all x1, starting transfers between devices, local_spread(): lax.all_to_all(gate_grad_part.reshape(block_count * tp_count, own_len), e...  14.9 us
    pallas_call x2, Pallas kernels, assemble(): pl.pallas_call(kernel, out_shape=[jax.ShapeDtypeStruct((count, rows, colu...  13.1 us
    dynamic_update_slice x38, local copies, waits for them, and re-layouts, in_order(): lax.dynamic_update_index_in_dim(whole, pieces[step], (rank - step) % coun...  12 us
  transfers between devices with their start and end apart: 82, of which 26 were waited for; matrix products, arithmetic and copies ran while one was open for 26% of the time, Pallas kernels for 2%

profile of v4, /device:TPU:0, one launch (start us, length us, event | category | flops | bytes accessed | tf_op | source)
XLA Modules:
  0.0 582.3 jit_solution(13264208429103388006)
XLA Ops:
  114.8 19.1 %collective-permute-done.19 = bf16[4,96,512]{2,1,0:T(8,128)(2,1)S(1)} collective-permute-done((bf16[4,96,512]{2,1,0:T(8,128)(2,1)S(1)}, bf16[4,96,512]{2,1,0:T(8,128)(2,1)S(1)}, u32[]{:S(2)}, u32[]{:S(2)}) %collective-permute-start.19) | collective-permute-done | bytes 393248 | tf_op jit(solution)/shard_map/ppermute | solution.py:474
  141.2 11.7 %collective-permute-done.20 = bf16[4,2,96,512]{3,2,1,0:T(8,128)(2,1)S(1)} collective-permute-done((bf16[4,2,96,512]{3,2,1,0:T(8,128)(2,1)S(1)}, bf16[4,2,96,512]{3,2,1,0:T(8,128)(2,1)S(1)}, u32[]{:S(2)}, u32[]{:S(2)}) %collective-permute-start.20) | collective-permute-done | bytes 786464 | tf_op jit(solution)/shard_map/ppermute | solution.py:518
  167.8 27.5 %collective-permute-done.30 = bf16[1,256,512]{2,1,0:T(8,128)(2,1)S(1)} collective-permute-done((bf16[1,256,512]{2,1,0:T(8,128)(2,1)S(1)}, bf16[1,256,512]{2,1,0:T(8,128)(2,1)S(1)}, u32[]{:S(2)}, u32[]{:S(2)}) %collective-permute-start.30) | collective-permute-done | bytes 262176 | tf_op jit(solution)/shard_map/ppermute | solution.py:474
  234.9 14.9 %all-to-all-start.1 = ((f32[32,1,96]{2,1,0:T(1,128)}), f32[32,1,96]{2,1,0:T(1,128)}, u32[]{:S(2)}, u32[]{:S(2)}) async-start(f32[32,1,96]{2,1,0:T(1,128)} %all_to_all.13), calls=%async_computation.1 | async-start | bytes 32768 | tf_op jit(solution)/shard_map/all_to_all | solution.py:865
  271.7 8.4 %collective-permute-start.66 = (bf16[2,256,512]{2,1,0:T(8,128)(2,1)}, bf16[2,256,512]{2,1,0:T(8,128)(2,1)}, u32[]{:S(2)}, u32[]{:S(2)}) collective-permute-start(bf16[2,256,512]{2,1,0:T(8,128)(2,1)} %pad_maximum_fusion.9), channel_id=1, source_target_pairs={{0,8},{8,16},{16,24},{24,0},{1,9},{9,17},{17,25},{25,1},{2,10},{10... | collective-permute-start | bytes 1572872 | tf_op jit(solution)/shard_map/ppermute | solution.py:474
  305.1 10.7 %collective-permute-done.32 = bf16[4,2,96,512]{3,2,0,1:T(8,128)(2,1)S(1)} collective-permute-done((bf16[4,2,96,512]{3,2,0,1:T(8,128)(2,1)S(1)}, bf16[4,2,96,512]{3,2,0,1:T(8,128)(2,1)S(1)}, u32[]{:S(2)}, u32[]{:S(2)}) %collective-permute-start.32) | collective-permute-done | bytes 786464 | tf_op jit(solution)/shard_map/ppermute | solution.py:518
  320.7 10.7 %collective-permute-done.44 = bf16[4,2,96,512]{3,2,0,1:T(8,128)(2,1)S(1)} collective-permute-done((bf16[4,2,96,512]{3,2,0,1:T(8,128)(2,1)S(1)}, bf16[4,2,96,512]{3,2,0,1:T(8,128)(2,1)S(1)}, u32[]{:S(2)}, u32[]{:S(2)}) %collective-permute-start.44) | collective-permute-done | bytes 786464 | tf_op jit(solution)/shard_map/ppermute | solution.py:518
  342.5 8.7 %collective-permute-done.45 = bf16[4,96,512]{2,1,0:T(8,128)(2,1)S(1)} collective-permute-done((bf16[4,96,512]{2,1,0:T(8,128)(2,1)S(1)}, bf16[4,96,512]{2,1,0:T(8,128)(2,1)S(1)}, u32[]{:S(2)}, u32[]{:S(2)}) %collective-permute-start.45) | collective-permute-done | bytes 393248 | tf_op jit(solution)/shard_map/ppermute | solution.py:474
  356.5 4.5 collective-permute-done.49
  361.1 5.8 collective-permute-done.50
  370.2 9.2 %all-gather = bf16[448,1152]{1,0:T(8,128)(2,1)S(1)} all-gather(bf16[112,1152]{1,0:T(8,128)(2,1)S(1)} %fusion.110), channel_id=2, replica_groups=mesh['fsdp'=4,'ctx'=2,'tp'=4] {'tp'}, dimensions={0}, use_global_device_ids=true | all-gather | bytes 1290240 | tf_op jit(solution)/shard_map/all_gather | solution.py:923
  391.6 4.7 collective-permute-done.52
  396.4 13.7 %collective-permute-start.37 = (bf16[96,1024]{1,0:T(8,128)(2,1)}, bf16[96,1024]{1,0:T(8,128)(2,1)}, u32[]{:S(2)}, u32[]{:S(2)}) collective-permute-start(bf16[96,1024]{1,0:T(8,128)(2,1)} %get-tuple-element.238), channel_id=1, source_target_pairs={{0,8},{8,16},{16,24},{24,0},{1,9},{9,17},{17,25},{25,1},{2,10},{10... | collective-permute-start | bytes 589832 | tf_op jit(solution)/shard_map/ppermute | solution.py:474
  423.2 6.5 %all-to-all-done.2 = bf16[4,112,1024]{2,1,0:T(8,128)(2,1)S(1)} async-done(((bf16[4,112,1024]{2,1,0:T(8,128)(2,1)}), bf16[4,112,1024]{2,1,0:T(8,128)(2,1)S(1)}, u32[]{:S(2)}, u32[]{:S(2)}) %all-to-all-start.2) | async-done | bytes 917536 | tf_op jit(solution)/shard_map/all_to_all | solution.py:488
  437.1 5.0 collective-permute-done.38
  442.2 12.4 %collective-permute-start.77 = (bf16[1,256,512]{2,1,0:T(8,128)(2,1)}, bf16[1,256,512]{2,1,0:T(8,128)(2,1)}, u32[]{:S(2)}, u32[]{:S(2)}) collective-permute-start(bf16[1,256,512]{2,1,0:T(8,128)(2,1)} %get-tuple-element.120), channel_id=1, source_target_pairs={{0,24},{8,0},{16,8},{24,16},{1,25},{9,1},{17,9},{25,17},{2,26},{10... | collective-permute-start | bytes 786440 | tf_op jit(solution)/shard_map/ppermute | solution.py:474
  455.9 7.2 %collective-permute-start.61 = (bf16[256,384]{1,0:T(8,128)(2,1)}, bf16[256,384]{1,0:T(8,128)(2,1)S(1)}, u32[]{:S(2)}, u32[]{:S(2)}) collective-permute-start(bf16[256,384]{1,0:T(8,128)(2,1)} %get-tuple-element.233), channel_id=1, source_target_pairs={{0,8},{8,16},{16,24},{24,0},{1,9},{9,17},{17,25},{25,1},{2,10},{10... | collective-permute-start | bytes 589832 | tf_op jit(solution)/shard_map/ppermute | solution.py:474
  464.4 21.2 %collective-permute-done.62 = bf16[256,384]{1,0:T(8,128)(2,1)S(1)} collective-permute-done((bf16[256,384]{1,0:T(8,128)(2,1)}, bf16[256,384]{1,0:T(8,128)(2,1)S(1)}, u32[]{:S(2)}, u32[]{:S(2)}) %collective-permute-start.62) | collective-permute-done | bytes 196640 | tf_op jit(solution)/shard_map/ppermute | solution.py:474
  489.8 7.8 %all_gather.14 = bf16[384,1024]{1,0:T(8,128)(2,1)S(1)} all-gather(bf16[96,1024]{1,0:T(8,128)(2,1)S(1)} %get-tuple-element.257), channel_id=1, replica_groups=mesh['fsdp'=4,'ctx'=2,'tp'=4] {'tp'}, dimensions={0}, use_global_device_ids=true | all-gather | bytes 983040 | tf_op jit(solution)/shard_map/all_gather | solution.py:1031
  497.8 10.8 %collective-permute-done.58 = bf16[256,512]{1,0:T(8,128)(2,1)S(1)} collective-permute-done((bf16[256,512]{1,0:T(8,128)(2,1)S(1)}, bf16[256,512]{1,0:T(8,128)(2,1)S(1)}, u32[]{:S(2)}, u32[]{:S(2)}) %collective-permute-start.58) | collective-permute-done | bytes 262176 | tf_op jit(solution)/shard_map/ppermute | solution.py:474
  512.7 7.9 %all_gather.15 = bf16[384,1024]{1,0:T(8,128)(2,1)S(1)} all-gather(bf16[96,1024]{1,0:T(8,128)(2,1)S(1)} %get-tuple-element.90), channel_id=1, replica_groups=mesh['fsdp'=4,'ctx'=2,'tp'=4] {'tp'}, dimensions={0}, use_global_device_ids=true | all-gather | bytes 983040 | tf_op jit(solution)/shard_map/all_gather | solution.py:1032
  520.6 31.1 %collective-permute-done.78.refs_7_ = bf16[1,256,512]{2,1,0:T(8,128)(2,1)} collective-permute-done((bf16[1,256,512]{2,1,0:T(8,128)(2,1)}, bf16[1,256,512]{2,1,0:T(8,128)(2,1)}, u32[]{:S(2)}, u32[]{:S(2)}) %collective-permute-start.78) | collective-permute-done | bytes 262176 | tf_op jit(solution)/shard_map/ppermute | solution.py:474
  561.7 5.8 shard_map.213
  567.9 7.4 %shard_map.212 = (f32[8,256,512]{2,1,0:T(8,128)}, f32[8,256,512]{2,1,0:T(8,128)}) custom-call(s32[8]{0:T(128)} %stack.114.places_ref, bf16[2,256,512]{2,1,0:T(8,128)(2,1)} %pad_maximum_fusion.8.refs_0_, bf16[2,256,512]{2,1,0:T(8,128)(2,1)} %collective-permute-done.65.refs_1_, bf16[2,256,512]{2,1,0:T(8,128)(2,1)} %collective-permute-done.66.refs_2_, ...), custom_call_target="tpu_custom_call" | custom-call | flops 2097152 | bytes 12582912 | tf_op jit(solution)/shard_map/pallas_call | solution.py:605
  (669 shorter events, 306.0 us)
Async XLA Ops:
  102.2 35.5 %collective-permute-start.14 = (bf16[4,2,96,640]{3,2,1,0:T(8,128)(2,1)S(1)}, bf16[4,2,96,640]{3,2,1,0:T(8,128)(2,1)S(1)}, u32[]{:S(2)}, u32[]{:S(2)}) collective-permute-start(bf16[4,2,96,640]{3,2,1,0:T(8,128)(2,1)S(1)} %bitcast_dynamic-update-slice_fusion.18), channel_id=1, source_target_pairs={{0,4},{4,0},{1,5},{5,1},{2,6},{6,2},{3,7},{7,3},{8,12},{12,8},{9,1... | collective-permute-start | bytes 2949128 | tf_op jit(solution)/shard_map/ppermute | solution.py:474
  104.6 50.2 %collective-permute-start.41 = (bf16[4,2,96,640]{3,2,1,0:T(8,128)(2,1)S(1)}, bf16[4,2,96,640]{3,2,1,0:T(8,128)(2,1)S(1)}, u32[]{:S(2)}, u32[]{:S(2)}) collective-permute-start(bf16[4,2,96,640]{3,2,1,0:T(8,128)(2,1)S(1)} %bitcast_dynamic-update-slice_fusion.16), channel_id=1, source_target_pairs={{0,2},{1,3},{2,0},{3,1},{4,6},{5,7},{6,4},{7,5},{8,10},{9,11},{10,... | collective-permute-start | bytes 2949128 | tf_op jit(solution)/shard_map/ppermute | solution.py:518
  113.2 48.9 %collective-permute-start.28 = (bf16[1,256,512]{2,1,0:T(8,128)(2,1)S(1)}, bf16[1,256,512]{2,1,0:T(8,128)(2,1)S(1)}, u32[]{:S(2)}, u32[]{:S(2)}) collective-permute-start(bf16[1,256,512]{2,1,0:T(8,128)(2,1)S(1)} %copy-done.87), channel_id=1, source_target_pairs={{0,8},{8,16},{16,24},{24,0},{1,9},{9,17},{17,25},{25,1},{2,10},{10... | collective-permute-start | bytes 786440 | tf_op jit(solution)/shard_map/ppermute | solution.py:474
  152.8 42.5 %collective-permute-start.25 = (bf16[2,256,512]{2,1,0:T(8,128)(2,1)S(1)}, bf16[2,256,512]{2,1,0:T(8,128)(2,1)S(1)}, u32[]{:S(2)}, u32[]{:S(2)}) collective-permute-start(bf16[2,256,512]{2,1,0:T(8,128)(2,1)S(1)} %copy-done.72), channel_id=1, source_target_pairs={{0,8},{8,16},{16,24},{24,0},{1,9},{9,17},{17,25},{25,1},{2,10},{10... | collective-permute-start | bytes 1572872 | tf_op jit(solution)/shard_map/ppermute | solution.py:474
  162.9 32.4 %collective-permute-start.26 = (bf16[2,256,512]{2,1,0:T(8,128)(2,1)S(1)}, bf16[2,256,512]{2,1,0:T(8,128)(2,1)S(1)}, u32[]{:S(2)}, u32[]{:S(2)}) collective-permute-start(bf16[2,256,512]{2,1,0:T(8,128)(2,1)S(1)} %copy-done.73), channel_id=1, source_target_pairs={{0,16},{8,24},{16,0},{24,8},{1,17},{9,25},{17,1},{25,9},{2,18},{10... | collective-permute-start | bytes 1572872 | tf_op jit(solution)/shard_map/ppermute | solution.py:474
  167.6 32.4 %collective-permute-start.15 = (bf16[4,2,2,96,640]{4,3,2,1,0:T(8,128)(2,1)S(1)}, bf16[4,2,2,96,640]{4,3,2,1,0:T(8,128)(2,1)S(1)}, u32[]{:S(2)}, u32[]{:S(2)}) collective-permute-start(bf16[4,2,2,96,640]{4,3,2,1,0:T(8,128)(2,1)S(1)} %bitcast_dynamic-update-slice_fusion.9), channel_id=1, source_target_pairs={{0,1},{1,0},{2,3},{3,2},{4,5},{5,4},{6,7},{7,6},{8,9},{9,8},{10,11... | collective-permute-start | bytes 5898248 | tf_op jit(solution)/shard_map/ppermute | solution.py:518
  234.9 53.7 %all-to-all-start.1 = ((f32[32,1,96]{2,1,0:T(1,128)}), f32[32,1,96]{2,1,0:T(1,128)}, u32[]{:S(2)}, u32[]{:S(2)}) async-start(f32[32,1,96]{2,1,0:T(1,128)} %all_to_all.13), calls=%async_computation.1 | async-start | bytes 32768 | tf_op jit(solution)/shard_map/all_to_all | solution.py:865
  258.9 31.9 %collective-permute-start.31 = (bf16[4,2,2,96,512]{4,3,0,1,2:T(8,128)(2,1)}, bf16[4,2,2,96,512]{4,3,0,1,2:T(8,128)(2,1)}, u32[]{:S(2)}, u32[]{:S(2)}) collective-permute-start(bf16[4,2,2,96,512]{4,3,0,1,2:T(8,128)(2,1)} %bitcast.536), channel_id=1, source_target_pairs={{0,1},{1,0},{2,3},{3,2},{4,5},{5,4},{6,7},{7,6},{8,9},{9,8},{10,11... | collective-permute-start | bytes 4718600 | tf_op jit(solution)/shard_map/ppermute | solution.py:518
  259.0 43.1 %collective-permute-start.34 = (bf16[4,2,2,96,512]{4,3,0,2,1:T(8,128)(2,1)}, bf16[4,2,2,96,512]{4,3,0,2,1:T(8,128)(2,1)}, u32[]{:S(2)}, u32[]{:S(2)}) collective-permute-start(bf16[4,2,2,96,512]{4,3,0,2,1:T(8,128)(2,1)} %bitcast.535), channel_id=1, source_target_pairs={{0,1},{1,0},{2,3},{3,2},{4,5},{5,4},{6,7},{7,6},{8,9},{9,8},{10,11... | collective-permute-start | bytes 4718600 | tf_op jit(solution)/shard_map/ppermute | solution.py:518
  271.7 161.8 %collective-permute-start.66 = (bf16[2,256,512]{2,1,0:T(8,128)(2,1)}, bf16[2,256,512]{2,1,0:T(8,128)(2,1)}, u32[]{:S(2)}, u32[]{:S(2)}) collective-permute-start(bf16[2,256,512]{2,1,0:T(8,128)(2,1)} %pad_maximum_fusion.9), channel_id=1, source_target_pairs={{0,8},{8,16},{16,24},{24,0},{1,9},{9,17},{17,25},{25,1},{2,10},{10... | collective-permute-start | bytes 1572872 | tf_op jit(solution)/shard_map/ppermute | solution.py:474
  290.8 142.8 %collective-permute-start.68 = (bf16[2,256,512]{2,1,0:T(8,128)(2,1)}, bf16[2,256,512]{2,1,0:T(8,128)(2,1)}, u32[]{:S(2)}, u32[]{:S(2)}) collective-permute-start(bf16[2,256,512]{2,1,0:T(8,128)(2,1)} %pad_maximum_fusion.10), channel_id=1, source_target_pairs={{0,16},{8,24},{16,0},{24,8},{1,17},{9,25},{17,1},{25,9},{2,18},{10... | collective-permute-start | bytes 1572872 | tf_op jit(solution)/shard_map/ppermute | solution.py:474
  318.8 32.6 %collective-permute-start.33 = (bf16[4,96,512]{2,1,0:T(8,128)(2,1)S(1)}, bf16[4,96,512]{2,1,0:T(8,128)(2,1)S(1)}, u32[]{:S(2)}, u32[]{:S(2)}) collective-permute-start(bf16[4,96,512]{2,1,0:T(8,128)(2,1)S(1)} %dynamic-slice_bitcast_fusion.9), channel_id=1, source_target_pairs={{0,4},{4,0},{1,5},{5,1},{2,6},{6,2},{3,7},{7,3},{8,12},{12,8},{9,1... | collective-permute-start | bytes 1179656 | tf_op jit(solution)/shard_map/ppermute | solution.py:474
  361.1 74.0 %collective-permute-start.70 = (bf16[2,256,512]{2,1,0:T(8,128)(2,1)}, bf16[2,256,512]{2,1,0:T(8,128)(2,1)}, u32[]{:S(2)}, u32[]{:S(2)}) collective-permute-start(bf16[2,256,512]{2,1,0:T(8,128)(2,1)} %pad_maximum_fusion.11), channel_id=1, source_target_pairs={{0,24},{8,0},{16,8},{24,16},{1,25},{9,1},{17,9},{25,17},{2,26},{10... | collective-permute-start | bytes 1572872 | tf_op jit(solution)/shard_map/ppermute | solution.py:474
  366.9 63.2 %collective-permute-start.72 = (bf16[1,256,512]{2,1,0:T(8,128)(2,1)}, bf16[1,256,512]{2,1,0:T(8,128)(2,1)}, u32[]{:S(2)}, u32[]{:S(2)}) collective-permute-start(bf16[1,256,512]{2,1,0:T(8,128)(2,1)} %get-tuple-element.121.refs_0_), channel_id=1, source_target_pairs={{0,4},{4,0},{1,5},{5,1},{2,6},{6,2},{3,7},{7,3},{8,12},{12,8},{9,1... | collective-permute-start | bytes 786440 | tf_op jit(solution)/shard_map/ppermute | solution.py:474
  396.4 39.3 %collective-permute-start.37 = (bf16[96,1024]{1,0:T(8,128)(2,1)}, bf16[96,1024]{1,0:T(8,128)(2,1)}, u32[]{:S(2)}, u32[]{:S(2)}) collective-permute-start(bf16[96,1024]{1,0:T(8,128)(2,1)} %get-tuple-element.238), channel_id=1, source_target_pairs={{0,8},{8,16},{16,24},{24,0},{1,9},{9,17},{17,25},{25,1},{2,10},{10... | collective-permute-start | bytes 589832 | tf_op jit(solution)/shard_map/ppermute | solution.py:474
  435.1 52.3 %collective-permute-start.73 = (bf16[1,256,512]{2,1,0:T(8,128)(2,1)}, bf16[1,256,512]{2,1,0:T(8,128)(2,1)S(1)}, u32[]{:S(2)}, u32[]{:S(2)}) collective-permute-start(bf16[1,256,512]{2,1,0:T(8,128)(2,1)} %get-tuple-element.118), channel_id=1, source_target_pairs={{0,8},{8,16},{16,24},{24,0},{1,9},{9,17},{17,25},{25,1},{2,10},{10... | collective-permute-start | bytes 786440 | tf_op jit(solution)/shard_map/ppermute | solution.py:474
  435.7 52.1 %collective-permute-start.75 = (bf16[1,256,512]{2,1,0:T(8,128)(2,1)}, bf16[1,256,512]{2,1,0:T(8,128)(2,1)S(1)}, u32[]{:S(2)}, u32[]{:S(2)}) collective-permute-start(bf16[1,256,512]{2,1,0:T(8,128)(2,1)} %get-tuple-element.119), channel_id=1, source_target_pairs={{0,16},{8,24},{16,0},{24,8},{1,17},{9,25},{17,1},{25,9},{2,18},{10... | collective-permute-start | bytes 786440 | tf_op jit(solution)/shard_map/ppermute | solution.py:474
  442.2 45.7 %collective-permute-start.77 = (bf16[1,256,512]{2,1,0:T(8,128)(2,1)}, bf16[1,256,512]{2,1,0:T(8,128)(2,1)}, u32[]{:S(2)}, u32[]{:S(2)}) collective-permute-start(bf16[1,256,512]{2,1,0:T(8,128)(2,1)} %get-tuple-element.120), channel_id=1, source_target_pairs={{0,24},{8,0},{16,8},{24,16},{1,25},{9,1},{17,9},{25,17},{2,26},{10... | collective-permute-start | bytes 786440 | tf_op jit(solution)/shard_map/ppermute | solution.py:474
  454.6 31.0 %collective-permute-start.62 = (bf16[256,384]{1,0:T(8,128)(2,1)}, bf16[256,384]{1,0:T(8,128)(2,1)S(1)}, u32[]{:S(2)}, u32[]{:S(2)}) collective-permute-start(bf16[256,384]{1,0:T(8,128)(2,1)} %get-tuple-element.232), channel_id=1, source_target_pairs={{0,16},{8,24},{16,0},{24,8},{1,17},{9,25},{17,1},{25,9},{2,18},{10... | collective-permute-start | bytes 589832 | tf_op jit(solution)/shard_map/ppermute | solution.py:474
  497.7 58.4 %collective-permute-start.65 = (bf16[2,256,512]{2,1,0:T(8,128)(2,1)S(1)}, bf16[2,256,512]{2,1,0:T(8,128)(2,1)}, u32[]{:S(2)}, u32[]{:S(2)}) collective-permute-start(bf16[2,256,512]{2,1,0:T(8,128)(2,1)S(1)} %copy-done.35), channel_id=1, source_target_pairs={{0,4},{4,0},{1,5},{5,1},{2,6},{6,2},{3,7},{7,3},{8,12},{12,8},{9,1... | collective-permute-start | bytes 1572872 | tf_op jit(solution)/shard_map/ppermute | solution.py:474
  508.6 47.5 %collective-permute-start.67 = (bf16[2,256,512]{2,1,0:T(8,128)(2,1)}, bf16[2,256,512]{2,1,0:T(8,128)(2,1)}, u32[]{:S(2)}, u32[]{:S(2)}) collective-permute-start(bf16[2,256,512]{2,1,0:T(8,128)(2,1)} %collective-permute-done.66.refs_2_), channel_id=1, source_target_pairs={{0,4},{4,0},{1,5},{5,1},{2,6},{6,2},{3,7},{7,3},{8,12},{12,8},{9,1... | collective-permute-start | bytes 1572872 | tf_op jit(solution)/shard_map/ppermute | solution.py:474
  508.6 49.1 %collective-permute-start.69 = (bf16[2,256,512]{2,1,0:T(8,128)(2,1)}, bf16[2,256,512]{2,1,0:T(8,128)(2,1)}, u32[]{:S(2)}, u32[]{:S(2)}) collective-permute-start(bf16[2,256,512]{2,1,0:T(8,128)(2,1)} %collective-permute-done.68.refs_4_), channel_id=1, source_target_pairs={{0,4},{4,0},{1,5},{5,1},{2,6},{6,2},{3,7},{7,3},{8,12},{12,8},{9,1... | collective-permute-start | bytes 1572872 | tf_op jit(solution)/shard_map/ppermute | solution.py:474
  510.6 47.1 %collective-permute-start.71 = (bf16[2,256,512]{2,1,0:T(8,128)(2,1)}, bf16[2,256,512]{2,1,0:T(8,128)(2,1)}, u32[]{:S(2)}, u32[]{:S(2)}) collective-permute-start(bf16[2,256,512]{2,1,0:T(8,128)(2,1)} %collective-permute-done.70.refs_6_), channel_id=1, source_target_pairs={{0,4},{4,0},{1,5},{5,1},{2,6},{6,2},{3,7},{7,3},{8,12},{12,8},{9,1... | collective-permute-start | bytes 1572872 | tf_op jit(solution)/shard_map/ppermute | solution.py:474
  510.7 41.0 %collective-permute-start.78 = (bf16[1,256,512]{2,1,0:T(8,128)(2,1)}, bf16[1,256,512]{2,1,0:T(8,128)(2,1)}, u32[]{:S(2)}, u32[]{:S(2)}) collective-permute-start(bf16[1,256,512]{2,1,0:T(8,128)(2,1)} %collective-permute-done.77.refs_6_), channel_id=1, source_target_pairs={{0,4},{4,0},{1,5},{5,1},{2,6},{6,2},{3,7},{7,3},{8,12},{12,8},{9,1... | collective-permute-start | bytes 786440 | tf_op jit(solution)/shard_map/ppermute | solution.py:474
  (183 other events, 2663.2 us)
